TPU v7x, 32 devices: a whole 2x2x4 slice. The times are simulated.
32 devices in a mesh: dp: 8 (over y, x, core), tensor: 4 (over z).
Axes of the slice: x: 2, y: 2, z: 4, core: 2. Of those that a mesh axis runs over, the one named last changes fastest.
Arguments:
- tokens: bfloat16 [20480, 768], P(('dp', 'tensor')), may hold values from -6 to 6
- visible_counts: int32 [256], P('dp'), may hold values from 20 to 78, as said below
- norm_one_gain: float32 [768], replicated, may hold values from 0.1 to 1.9
- norm_one_shift: float32 [768], replicated, may hold values from -1.8 to 1.8
- input_weight: bfloat16 [768, 3, 768], P(None, None, 'tensor'), may hold values from -0.21875 to 0.21875
- input_bias: bfloat16 [2, 768], P(None, 'tensor'), may hold values from -1.796875 to 1.796875
- mixer_weight: bfloat16 [768, 768], P('tensor'), may hold values from -1.25 to 1.25
- mixer_bias: float32 [768], replicated, may hold values from -1.8 to 1.8
- norm_two_gain: float32 [768], replicated, may hold values from 0.1 to 1.9
- norm_two_shift: float32 [768], replicated, may hold values from -1.8 to 1.8
- up_weight: bfloat16 [768, 3072], P(None, 'tensor'), may hold values from -0.21875 to 0.21875
- up_bias: bfloat16 [3072], P('tensor'), may hold values from -1.796875 to 1.796875
- down_weight: bfloat16 [3072, 768], P('tensor'), may hold values from -0.109375 to 0.109375
- down_bias: float32 [768], replicated, may hold values from -1.8 to 1.8
- output_grad: bfloat16 [20480, 768], P(('dp', 'tensor')), may hold values from -6 to 6
Outputs:
- block_output: bfloat16 [20480, 768], P(('dp', 'tensor'))
- grad_tokens: float32 [20480, 768], P(('dp', 'tensor'))
- grad_norm_one_gain: float32 [768], replicated
- grad_norm_one_shift: float32 [768], replicated
- grad_input_weight: float32 [768, 3, 768], P(None, None, 'tensor')
- grad_input_bias: float32 [2, 768], P(None, 'tensor')
- grad_mixer_weight: float32 [768, 768], P('tensor')
- grad_mixer_bias: float32 [768], replicated
- grad_norm_two_gain: float32 [768], replicated
- grad_norm_two_shift: float32 [768], replicated
- grad_up_weight: float32 [768, 3072], P(None, 'tensor')
- grad_up_bias: float32 [3072], P('tensor')
- grad_down_weight: float32 [3072, 768], P('tensor')
- grad_down_bias: float32 [768], replicated
Inputs may be any that keep to these rules, and one draw needn't show every extreme that they name: `visible_counts`: each image has 20 to 78 visible patches; some image has exactly 78 and some exactly 20.
All inputs are finite; a program needn't handle non-finite values.
Results may differ from a plain program's by a relative error of at most 0.014.
Values may be sent and summed in bfloat16 or wider, within the bound.
No kernel may reach another device: no remote copies, remote signals or barrier semaphores. Data moves between devices by JAX's collectives and lax.ppermute only.
A program may use at most 128 MiB of HBM per device.

v0:
```python
import jax
import jax.numpy as jnp
from jax import lax
from jax.sharding import PartitionSpec as P

HD = 64
SLOTS = 80


masked_score = -1000000000.0


def layer_norm(inputs, norm_gain, norm_shift):
    center = inputs - jnp.mean(inputs, axis=-1, keepdims=True)
    spread = jnp.mean(center * center, axis=-1, keepdims=True)
    return center * lax.rsqrt(spread + 1e-06) * norm_gain + norm_shift


def norm_back(inputs, norm_gain, norm_shift, grad_normed):
    unused, pullback = jax.vjp(layer_norm, inputs, norm_gain, norm_shift)
    return pullback(grad_normed)


def gelu_exact(inputs):
    return jax.nn.gelu(inputs, approximate=False)


def split_heads(flat, slot_count, head_dim):
    return flat.reshape(
        flat.shape[0] // slot_count, slot_count, flat.shape[1] // head_dim, head_dim
    )


def visible_keys(counts, slot_count):
    return (lax.broadcasted_iota(jnp.int32, (counts.shape[0], slot_count), 1) < counts[:, None])[
        :, None, None, :
    ]


def project_inputs(normed_rows, weight_in, bias_in, slot_count, head_dim):
    columns = weight_in.shape[2]
    product = jnp.dot(
        normed_rows,
        weight_in.reshape(weight_in.shape[0], 3 * columns),
        preferred_element_type=jnp.float32,
    ).reshape(-1, 3, columns)
    queries = (product[:, 0] + bias_in[0]).astype(jnp.bfloat16)
    key_rows = product[:, 1].astype(jnp.bfloat16)
    values = (product[:, 2] + bias_in[1]).astype(jnp.bfloat16)
    return (
        split_heads(queries, slot_count, head_dim),
        split_heads(key_rows, slot_count, head_dim),
        split_heads(values, slot_count, head_dim),
    )


def attend(queries, key_rows, values, counts):
    factor = queries.shape[-1] ** (-0.5)
    scores = (
        jnp.einsum("bqhd,bkhd->bhqk", queries, key_rows, preferred_element_type=jnp.float32)
        * factor
    )
    scores = jnp.where(visible_keys(counts, key_rows.shape[1]), scores, masked_score)
    maxima = jnp.max(scores, axis=-1, keepdims=True)
    exponent = jnp.exp(scores - maxima)
    totals = jnp.sum(exponent, axis=-1, keepdims=True)
    soft_low = (exponent / totals).astype(jnp.bfloat16)
    blended = jnp.einsum("bhqk,bkhd->bqhd", soft_low, values, preferred_element_type=jnp.float32)
    return (blended, maxima + jnp.log(totals))


def attend_back(queries, key_rows, values, counts, log_totals, grad_blend):
    factor = queries.shape[-1] ** (-0.5)
    scores = (
        jnp.einsum("bqhd,bkhd->bhqk", queries, key_rows, preferred_element_type=jnp.float32)
        * factor
    )
    scores = jnp.where(visible_keys(counts, key_rows.shape[1]), scores, masked_score)
    soft = jnp.exp(scores - log_totals)
    soft_low = soft.astype(jnp.bfloat16)
    grad_values = jnp.einsum(
        "bhqk,bqhd->bkhd", soft_low, grad_blend, preferred_element_type=jnp.float32
    )
    grad_soft = jnp.einsum(
        "bqhd,bkhd->bhqk", grad_blend, values, preferred_element_type=jnp.float32
    )
    grad_scores = soft * (grad_soft - jnp.sum(grad_soft * soft, axis=-1, keepdims=True))
    grad_low = grad_scores.astype(jnp.bfloat16)
    grad_queries = (
        jnp.einsum("bhqk,bkhd->bqhd", grad_low, key_rows, preferred_element_type=jnp.float32)
        * factor
    )
    grad_keys = (
        jnp.einsum("bhqk,bqhd->bkhd", grad_low, queries, preferred_element_type=jnp.float32)
        * factor
    )
    return (grad_queries, grad_keys, grad_values)


def mlp_back(normed_rows, hidden_pre, active, grad_rows, weight_down):
    grad_down = jnp.einsum("rf,rd->fd", active, grad_rows, preferred_element_type=jnp.float32)
    grad_active = jnp.einsum(
        "rd,fd->rf", grad_rows, weight_down, preferred_element_type=jnp.float32
    )
    unused, pullback = jax.vjp(gelu_exact, hidden_pre)
    grad_pre = pullback(grad_active)[0]
    grad_up_b = jnp.sum(grad_pre, axis=0)
    grad_pre_low = grad_pre.astype(jnp.bfloat16)
    grad_up = jnp.einsum("rd,rf->df", normed_rows, grad_pre_low, preferred_element_type=jnp.float32)
    return (grad_down, grad_up, grad_up_b, grad_pre_low)


def mixer_back(
    normed_rows,
    queries,
    key_rows,
    values,
    counts,
    log_totals,
    grad_rows,
    blend_low,
    weight_mix,
    slot_count,
    head_dim,
):
    row_total = blend_low.shape[0]
    grad_mix = jnp.einsum("rc,rd->cd", blend_low, grad_rows, preferred_element_type=jnp.float32)
    grad_blend = jnp.einsum(
        "rd,cd->rc", grad_rows, weight_mix, preferred_element_type=jnp.float32
    ).astype(jnp.bfloat16)
    grad_queries, grad_keys, grad_values = attend_back(
        queries, key_rows, values, counts, log_totals, split_heads(grad_blend, slot_count, head_dim)
    )
    grad_queries = grad_queries.reshape(row_total, -1)
    grad_keys = grad_keys.reshape(row_total, -1)
    grad_values = grad_values.reshape(row_total, -1)
    grad_bias_in = jnp.stack([jnp.sum(grad_queries, axis=0), jnp.sum(grad_values, axis=0)])
    grad_projected = jnp.stack([grad_queries, grad_keys, grad_values], axis=1).astype(jnp.bfloat16)
    grad_weight_in = jnp.einsum(
        "rd,rjc->djc", normed_rows, grad_projected, preferred_element_type=jnp.float32
    )
    return (grad_mix, grad_bias_in, grad_weight_in, grad_projected)


def local(
    tokens,
    visible_counts,
    norm_one_gain,
    norm_one_shift,
    input_weight,
    input_bias,
    mixer_weight,
    mixer_bias,
    norm_two_gain,
    norm_two_shift,
    up_weight,
    up_bias,
    down_weight,
    down_bias,
    output_grad,
):
    slot_count = SLOTS
    head_dim = HD
    inputs = tokens.astype(jnp.float32)
    grad_output = output_grad.astype(jnp.float32)
    low_one = layer_norm(inputs, norm_one_gain, norm_one_shift).astype(jnp.bfloat16)
    whole_one = lax.all_gather(low_one, "tensor", axis=0, tiled=True)
    queries, key_rows, values = project_inputs(
        whole_one, input_weight, input_bias, slot_count, head_dim
    )
    blended, log_totals = attend(queries, key_rows, values, visible_counts)
    blend_low = blended.reshape(whole_one.shape[0], -1).astype(jnp.bfloat16)
    first_sum = (
        inputs
        + lax.psum_scatter(
            jnp.dot(blend_low, mixer_weight, preferred_element_type=jnp.float32),
            "tensor",
            scatter_dimension=0,
            tiled=True,
        )
        + mixer_bias
    )
    low_two = layer_norm(first_sum, norm_two_gain, norm_two_shift).astype(jnp.bfloat16)
    whole_two = lax.all_gather(low_two, "tensor", axis=0, tiled=True)
    hidden_pre = jnp.dot(whole_two, up_weight, preferred_element_type=jnp.float32) + up_bias
    active = gelu_exact(hidden_pre).astype(jnp.bfloat16)
    result = (
        first_sum
        + lax.psum_scatter(
            jnp.dot(active, down_weight, preferred_element_type=jnp.float32).astype(jnp.bfloat16),
            "tensor",
            scatter_dimension=0,
            tiled=True,
        ).astype(jnp.float32)
        + down_bias
    )
    whole_grad = lax.all_gather(output_grad, "tensor", axis=0, tiled=True)
    grad_down, grad_up, grad_up_b, grad_pre_low = mlp_back(
        whole_two, hidden_pre, active, whole_grad, down_weight
    )
    grad_normed_two = lax.psum_scatter(
        jnp.einsum("rf,df->rd", grad_pre_low, up_weight, preferred_element_type=jnp.float32),
        "tensor",
        scatter_dimension=0,
        tiled=True,
    )
    grad_first, grad_gain_two, grad_shift_two = norm_back(
        first_sum, norm_two_gain, norm_two_shift, grad_normed_two
    )
    grad_first = grad_output + grad_first
    whole_first = lax.all_gather(grad_first.astype(jnp.bfloat16), "tensor", axis=0, tiled=True)
    grad_mix, grad_bias_in, grad_weight_in, grad_projected = mixer_back(
        whole_one,
        queries,
        key_rows,
        values,
        visible_counts,
        log_totals,
        whole_first,
        blend_low,
        mixer_weight,
        slot_count,
        head_dim,
    )
    grad_normed_one = lax.psum_scatter(
        jnp.einsum(
            "rjc,djc->rd", grad_projected, input_weight, preferred_element_type=jnp.float32
        ).astype(jnp.bfloat16),
        "tensor",
        scatter_dimension=0,
        tiled=True,
    ).astype(jnp.float32)
    weight_terms = (grad_weight_in, grad_bias_in, grad_mix, grad_up, grad_up_b, grad_down)
    grad_inputs, grad_gain_one, grad_shift_one = norm_back(
        inputs, norm_one_gain, norm_one_shift, grad_normed_one
    )
    grad_tokens = grad_first + grad_inputs
    sum_gain_one, sum_shift_one, sum_mix_bias, sum_gain_two, sum_shift_two, sum_down_bias = (
        lax.psum(
            (
                grad_gain_one,
                grad_shift_one,
                jnp.sum(grad_first, axis=0),
                grad_gain_two,
                grad_shift_two,
                jnp.sum(grad_output, axis=0),
            ),
            ("dp", "tensor"),
        )
    )
    sum_weight_in, sum_bias_in, sum_mix, sum_up, sum_up_b, sum_down = lax.psum(
        (
            weight_terms[0],
            weight_terms[1],
            weight_terms[2],
            weight_terms[3],
            weight_terms[4],
            weight_terms[5],
        ),
        "dp",
    )
    return (
        result.astype(jnp.bfloat16),
        grad_tokens,
        sum_gain_one,
        sum_shift_one,
        sum_weight_in,
        sum_bias_in,
        sum_mix,
        sum_mix_bias,
        sum_gain_two,
        sum_shift_two,
        sum_up,
        sum_up_b,
        sum_down,
        sum_down_bias,
    )


def solution(mesh):
    in_specs = (
        P(("dp", "tensor"), None),
        P("dp"),
        P(),
        P(),
        P(None, None, "tensor"),
        P(None, "tensor"),
        P("tensor", None),
        P(),
        P(),
        P(),
        P(None, "tensor"),
        P("tensor"),
        P("tensor", None),
        P(),
        P(("dp", "tensor"), None),
    )
    out_specs = (
        P(("dp", "tensor"), None),
        P(("dp", "tensor"), None),
        P(),
        P(),
        P(None, None, "tensor"),
        P(None, "tensor"),
        P("tensor", None),
        P(),
        P(),
        P(),
        P(None, "tensor"),
        P("tensor"),
        P("tensor", None),
        P(),
    )
    return jax.shard_map(local, mesh=mesh, in_specs=in_specs, out_specs=out_specs, check_vma=False)
```

profile of v0, /device:TPU:0, one launch (start us, length us, event | category | flops | bytes accessed | tf_op | source)
XLA Modules:
  0.0 1010.1 jit_solution(16693348201039939642)
XLA Ops:
  7.3 1.5 convert_reduce_fusion.1
  8.8 1.6 fusion.20
  11.7 2.6 fusion.19
  14.6 79.0 %all-gather.5.cloned.1.call-done = bf16[2560,768]{1,0:T(8,128)(2,1)} async-done(((bf16[640,768]{1,0:T(8,128)(2,1)}), bf16[2560,768]{1,0:T(8,128)(2,1)}) %all-gather.5.cloned.1.call-update) | async-done | bytes 3932176 | tf_op jit(solution)/shard_map/all_gather | solution.py:167
  93.6 4.6 fusion.6
  99.2 2.2 fusion.56
  101.4 3.3 convert_element_type.82
  104.7 4.7 squeeze.4
  109.4 4.1 squeeze.10
  113.5 5.2 fusion.57
  119.9 2.2 copy-done.9
  122.1 3.0 fusion.34
  125.1 2.2 copy.43
  127.2 3.6 convert_element_type.86
  130.9 4.3 fusion.58
  135.3 134.9 %reduce-scatter.5.cloned.1.call-done = f32[640,768]{1,0:T(8,128)} async-done(((f32[2560,768]{1,0:T(8,128)}), f32[640,768]{1,0:T(8,128)}) %reduce-scatter.5.cloned.1.call-update) | async-done | bytes 1966096 | tf_op jit(solution)/shard_map/reduce_scatter | solution.py:175
  270.2 2.1 fusion.54
  272.7 1.3 add_convert_fusion.1
  274.7 76.5 %all-gather.7.cloned.1.call-done = bf16[2560,768]{1,0:T(8,128)(2,1)} async-done(((bf16[640,768]{1,0:T(8,128)(2,1)}), bf16[2560,768]{1,0:T(8,128)(2,1)}) %all-gather.7.cloned.1.call-update) | async-done | bytes 3932176 | tf_op jit(solution)/shard_map/all_gather | solution.py:184
  351.2 9.0 fusion.59
  360.2 67.5 %all-gather.9.cloned.1.call-done = bf16[2560,768]{1,0:T(8,128)(2,1)} async-done(((bf16[640,768]{1,0:T(8,128)(2,1)}), bf16[2560,768]{1,0:T(8,128)(2,1)}) %all-gather.9.cloned.1.call-update) | async-done | bytes 3932176 | tf_op jit(solution)/shard_map/all_gather | solution.py:197
  427.6 23.8 %fusion.51 = (f32[768]{0:T(1024)S(1)}, bf16[2560,768]{1,0:T(8,128)(2,1)S(1)}, f32[2560,768]{1,0:T(8,128)}) fusion(f32[2560,768]{1,0:T(8,128)} %fusion.59, f32[768]{0:T(1024)S(1)} %convert_element_type.88, bf16[2560,768]{1,0:T(8,128)(2,1)} %all-gather.9.cloned.1.call-done, bf16[768,768]{1,0:T(8,128)(2,1)S(1)} %copy-done), kind=kOutput, calls=%fused_computation.106 | convolution fusion | flops 3165388032 | bytes 24778752 | tf_op jit(solution)/shard_map/rd,fd->rf/dot_general | solution.py:102
  451.4 1.9 copy-done.46
  453.3 5.4 fusion.29
  459.2 8.0 multiply_convert_fusion
  467.2 2.0 copy-done.15
  469.2 4.7 convolution_convert_fusion
  473.9 119.7 %reduce-scatter.9.cloned.1.call-done = f32[640,768]{1,0:T(8,128)} async-done(((f32[2560,768]{1,0:T(8,128)}), f32[640,768]{1,0:T(8,128)}) %reduce-scatter.9.cloned.1.call-update) | async-done | bytes 1966096 | tf_op jit(solution)/shard_map/reduce_scatter | solution.py:201
  593.7 2.3 multiply_reduce_fusion.1
  596.0 73.1 %reduce-scatter.7.cloned.1.call-done = bf16[640,768]{1,0:T(8,128)(2,1)} async-done(((bf16[2560,768]{1,0:T(8,128)(2,1)}), bf16[640,768]{1,0:T(8,128)(2,1)}) %reduce-scatter.7.cloned.1.call-update) | async-done | bytes 983056 | tf_op jit(solution)/shard_map/reduce_scatter | solution.py:189
  669.0 3.7 fusion.53
  672.7 1.3 copy-done.5
  675.4 76.9 %all-gather.11.cloned.1.call-done = bf16[2560,768]{1,0:T(8,128)(2,1)} async-done(((bf16[640,768]{1,0:T(8,128)(2,1)}), bf16[2560,768]{1,0:T(8,128)(2,1)}) %all-gather.11.cloned.1.call-update) | async-done | bytes 3932176 | tf_op jit(solution)/shard_map/all_gather | solution.py:211
  752.2 4.5 convolution_convert_fusion.1
  756.7 3.3 reshape.157
  760.0 7.1 multiply_reduce_fusion
  767.1 3.0 bitcast_convert_fusion.1
  772.0 4.0 fusion.33
  776.1 3.4 bitcast_convert_fusion.2
  780.6 3.9 stack_reshape.14
  784.4 2.4 copy.49
  786.9 3.7 stack_reshape.13
  790.5 2.4 copy.47
  793.0 3.7 stack_reshape.12
  796.6 1.4 constant_dynamic-update-slice_fusion.2
  798.0 1.3 constant_dynamic-update-slice_fusion.1
  799.4 1.6 copy-done.22
  800.9 4.7 bitcast_convert_fusion
  806.0 8.1 fusion.27
  814.2 4.8 fusion.61
  819.1 1.7 fusion.60
  820.9 3.7 fusion.62
  824.6 2.3 bitcast_reduce_fusion
  827.0 2.4 bitcast_reduce_fusion.1
  829.5 14.4 %all-reduce.1 = (f32[2,192]{1,0:T(2,128)}, f32[768]{0:T(1024)}) all-reduce(f32[2,192]{1,0:T(2,128)S(1)} %pad_maximum_fusion, f32[768]{0:T(1024)S(1)} %get-tuple-element.37), channel_id=1, replica_groups=mesh['dp'=8,'tensor'=4] {'dp'}, use_global_device_ids=true, to_apply=%region_22.23 | all-reduce | flops 1152 | bytes 9216 | tf_op jit(solution)/shard_map/psum | solution.py:251
  843.9 33.2 %reduce-scatter.11.cloned.1.call-done = bf16[640,768]{1,0:T(8,128)(2,1)} async-done(((bf16[2560,768]{1,0:T(8,128)(2,1)}), bf16[640,768]{1,0:T(8,128)(2,1)}) %reduce-scatter.11.cloned.1.call-update) | async-done | bytes 983056 | tf_op jit(solution)/shard_map/reduce_scatter | solution.py:225
  877.1 2.0 convert_reduce_fusion
  879.2 2.3 fusion.23
  881.6 2.2 convert_reduce_fusion.2
  883.8 41.7 %all-reduce = (f32[768]{0:T(1024)}, f32[768]{0:T(1024)}, f32[768]{0:T(1024)}, f32[768]{0:T(1024)}, f32[768]{0:T(1024)}, /*index=5*/f32[768]{0:T(1024)}) all-reduce(f32[768]{0:T(1024)S(1)} %get-tuple-element.16, f32[768]{0:T(1024)S(1)} %get-tuple-element.21, ...), channel_id=1, replica_groups=mesh['dp'=8,'tensor'=4] {'dp','tensor'}, use_global_device_ids=true, to_apply=%region_16.17 | all-reduce | flops 4608 | bytes 36864 | tf_op jit(solution)/shard_map/psum | solution.py:239
  925.4 71.1 %all-reduce.5.cloned.1.call-done = (f32[768,3,192]{0,2,1:T(8,128)}, f32[192,768]{1,0:T(8,128)}, f32[768,768]{1,0:T(8,128)}, f32[768,768]{1,0:T(8,128)}) async-done(((f32[768,3,192]{0,2,1:T(8,128)}, f32[192,768]{1,0:T(8,128)}, f32[768,768]{1,0:T(8,128)}, f32[768,768]{1,0:T(8,128)}), (f32[768,3,192]{0,2,1:T(8,128)}, f32[192,768]{1,0:T(8,128)}, f32[768,768]{1,0:T(8,128)}, ...) | async-done | bytes 7077904 | tf_op jit(solution)/shard_map/psum | solution.py:251
  996.5 2.9 copy.93
  1000.3 1.4 copy.95
  1001.7 1.4 copy.96
  (132 shorter events, 11.3 us)
Async XLA Ops:
  7.2 420.5 %copy-start = (bf16[768,768]{1,0:T(8,128)(2,1)S(1)}, bf16[768,768]{1,0:T(8,128)(2,1)}, u32[]{:S(2)}) copy-start(bf16[768,768]{1,0:T(8,128)(2,1)} %param.27) | copy-start | bytes 3538948
  7.2 7.1 copy-start.38
  7.2 7.3 copy-start.40
  7.2 86.3 %copy-start.44 = (bf16[768,3,192]{0,2,1:T(8,128)(2,1)S(1)}, bf16[768,3,192]{0,2,1:T(8,128)(2,1)}, u32[]{:S(2)}) copy-start(bf16[768,3,192]{0,2,1:T(8,128)(2,1)} %param.19) | copy-start | bytes 2654212
  7.2 86.3 %all-gather.5.cloned.1.call-start = ((), (), s32[]{:S(2)}) async-start(), calls=%async_computation.4 | async-start | bytes 4915200 | tf_op jit(solution)/shard_map/all_gather | solution.py:167
  8.8 2.2 copy-start.27
  10.4 0.6 copy-start.32
  11.1 0.6 copy-start.30
  14.3 255.9 %reduce-scatter.5.cloned.1.call-start = ((), (), s32[]{:S(2)}) async-start(), calls=%async_computation.5 | async-start | bytes 9830400 | tf_op jit(solution)/shard_map/reduce_scatter | solution.py:175
  104.7 8.9 copy-start.7
  118.7 6.3 copy-start.1
  118.8 3.3 copy-start.9
  122.1 3.0 copy-start.25
  125.1 5.8 copy-start.24
  130.9 4.3 copy-start.10
  135.2 135.0 %copy-start.35 = (f32[768]{0:T(1024)S(1)}, f32[768]{0:T(1024)}, u32[]{:S(2)}) copy-start(f32[768]{0:T(1024)} %param.22) | copy-start | bytes 9220
  135.2 137.5 %copy-start.34 = (f32[768]{0:T(1024)S(1)}, f32[768]{0:T(1024)}, u32[]{:S(2)}) copy-start(f32[768]{0:T(1024)} %param.23) | copy-start | bytes 9220
  135.2 137.5 %copy-start.36 = (f32[768]{0:T(1024)S(1)}, f32[768]{0:T(1024)}, u32[]{:S(2)}) copy-start(f32[768]{0:T(1024)} %param.24) | copy-start | bytes 9220
  135.3 215.9 %all-gather.7.cloned.1.call-start = ((), (), s32[]{:S(2)}) async-start(), calls=%async_computation.6 | async-start | bytes 4915200 | tf_op jit(solution)/shard_map/all_gather | solution.py:184
  272.3 2.4 copy-start.39
  274.1 153.6 %all-gather.9.cloned.1.call-start = ((), (), s32[]{:S(2)}) async-start(), calls=%async_computation.8 | async-start | bytes 4915200 | tf_op jit(solution)/shard_map/all_gather | solution.py:197
  274.6 319.0 %reduce-scatter.9.cloned.1.call-start = ((), (), s32[]{:S(2)}) async-start(), calls=%async_computation.9 | async-start | bytes 9830400 | tf_op jit(solution)/shard_map/reduce_scatter | solution.py:201
  427.6 25.7 %copy-start.43 = (bf16[768,768]{1,0:T(8,128)(2,1)S(1)}, bf16[768,768]{1,0:T(8,128)(2,1)}, u32[]{:S(2)}) copy-start(bf16[768,768]{1,0:T(8,128)(2,1)} %param.25) | copy-start | bytes 3538948
  451.4 1.9 copy-start.46
  458.7 210.3 %reduce-scatter.7.cloned.1.call-start = ((), (), s32[]{:S(2)}) async-start(), calls=%async_computation.7 | async-start | bytes 4915200 | tf_op jit(solution)/shard_map/reduce_scatter | solution.py:189
  467.2 2.0 copy-start.15
  473.8 195.2 %copy-start.37 = (f32[768]{0:T(1024)S(1)}, f32[768]{0:T(1024)}, u32[]{:S(2)}) copy-start(f32[768]{0:T(1024)} %param.28) | copy-start | bytes 9220
  473.9 278.3 %all-gather.11.cloned.1.call-start = ((), (), s32[]{:S(2)}) async-start(), calls=%async_computation.10 | async-start | bytes 4915200 | tf_op jit(solution)/shard_map/all_gather | solution.py:211
  669.0 5.0 copy-start.12
  672.7 1.3 copy-start.5
  672.7 2.6 copy-start.26
  675.3 201.8 %reduce-scatter.11.cloned.1.call-start = ((), (), s32[]{:S(2)}) async-start(), calls=%async_computation.11 | async-start | bytes 4915200 | tf_op jit(solution)/shard_map/reduce_scatter | solution.py:225
  759.9 7.2 copy-start.2
  770.2 1.9 copy-start.4
  772.0 4.0 copy-start.8
  796.6 2.7 copy-start.18
  796.6 4.3 copy-start.45
  799.4 1.6 copy-start.22
  805.7 190.8 %all-reduce.5.cloned.1.call-start = ((), (), s32[]{:S(2)}) async-start(), calls=%async_computation.12 | async-start | bytes 14155776 | tf_op jit(solution)/shard_map/psum | solution.py:251
  806.0 8.2 copy-start.16
  806.0 8.2 copy-start.42
  814.2 4.9 copy-start.11
  814.2 4.9 copy-start.17
  814.2 6.6 copy-start.41
  819.1 1.9 copy-start.23
  824.6 52.5 %copy-start.3 = (bf16[640,768]{1,0:T(8,128)(2,1)S(1)}, bf16[640,768]{1,0:T(8,128)(2,1)}, u32[]{:S(2)}) copy-start(bf16[640,768]{1,0:T(8,128)(2,1)} %param.15) | copy-start | bytes 2949124
  824.6 52.5 %copy-start.28 = (f32[640]{0:T(1024)S(1)}, f32[640]{0:T(1024)}, u32[]{:S(2)}) copy-start(f32[640]{0:T(1024)} %copy-done.27) | copy-start | bytes 7684
  824.6 52.5 %copy-start.29 = (f32[768]{0:T(1024)S(1)}, f32[768]{0:T(1024)}, u32[]{:S(2)}) copy-start(f32[768]{0:T(1024)} %param.17) | copy-start | bytes 9220
  826.9 52.3 %copy-start.33 = (f32[640]{0:T(1024)S(1)}, f32[640]{0:T(1024)}, u32[]{:S(2)}) copy-start(f32[640]{0:T(1024)} %copy-done.32) | copy-start | bytes 7684
  826.9 52.3 %copy-start.31 = (f32[640]{0:T(1024)S(1)}, f32[640]{0:T(1024)}, u32[]{:S(2)}) copy-start(f32[640]{0:T(1024)} %copy-done.30) | copy-start | bytes 7684
  827.0 54.6 %copy-start.13 = (bf16[640,768]{1,0:T(8,128)(2,1)S(1)}, bf16[640,768]{1,0:T(8,128)(2,1)}, u32[]{:S(2)}) copy-start(bf16[640,768]{1,0:T(8,128)(2,1)} %param.29) | copy-start | bytes 2949124
  877.1 4.5 copy-start.6
  877.1 4.5 copy-start.14
  996.5 3.0 copy-start.21
  996.5 3.8 copy-start.20
  999.5 2.2 copy-start.19
Sparse Core Ops, SparseCore 0:
  14.4 79.1 all-gather.4
  135.4 134.8 reduce-scatter.4
  274.2 76.9 all-gather.6
  352.6 74.9 all-gather.8
  458.8 134.8 reduce-scatter.8
  595.8 73.1 reduce-scatter.6
  675.4 76.7 all-gather.10
  805.8 71.2 reduce-scatter.10
  881.9 114.5 all-reduce.4
where the time goes:
time: 1010 us
  waiting for transfers between devices  732 us (72%)
  matrix products  105 us (10%)
  local copies, waits for them, and re-layouts  62.3 us (6%)
  blocking collectives  56.1 us (6%)
  other arithmetic  38.2 us (4%)
  between operations  14.8 us (1%)
    reduce_scatter x1, waiting for transfers between devices, local(): lax.psum_scatter(jnp.dot(blend_low, mixer_weight, preferred_element_type=...  135 us
    reduce_scatter x1, waiting for transfers between devices, local(): lax.psum_scatter(jnp.einsum('rf,df->rd', grad_pre_low, up_weight, preferr...  120 us
    all_gather x1, waiting for transfers between devices, local(): whole_one = lax.all_gather(low_one, 'tensor', axis=0, tiled=True)  79 us
    all_gather x1, waiting for transfers between devices, local(): lax.all_gather(grad_first.astype(jnp.bfloat16), 'tensor', axis=0, tiled=T...  76.9 us
    all_gather x1, waiting for transfers between devices, local(): whole_two = lax.all_gather(low_two, 'tensor', axis=0, tiled=True)  76.5 us
    reduce_scatter x1, waiting for transfers between devices, local(): lax.psum_scatter(jnp.dot(active, down_weight, preferred_element_type=jnp....  73.1 us
    psum x1, waiting for transfers between devices, local(): lax.psum((weight_terms[0], weight_terms[1], weight_terms[2], weight_terms...  71.1 us
    all_gather x1, waiting for transfers between devices, local(): whole_grad = lax.all_gather(output_grad, 'tensor', axis=0, tiled=True)  67.5 us
  transfers between devices with their start and end apart: 9, of which 9 were waited for; matrix products, arithmetic and copies ran while one was open for 5% of the time, Pallas kernels for 0%

commit v1 on v0

v1 whole, which is shorter than its diff:
```python
import functools

import jax
import jax.numpy as jnp
import numpy as np
from jax import lax
from jax.experimental import pallas as pl
from jax.experimental.pallas import tpu as pltpu
from jax.sharding import PartitionSpec as P

HD = 64
SLOTS = 80
LANES = 128
TILE_IMAGES = 4
MASKED = -1000000000.0
EPS = 1e-06
F32 = jnp.float32
BF16 = jnp.bfloat16

ANY = pl.BlockSpec(memory_space=pl.ANY)
SMEM = pl.BlockSpec(memory_space=pltpu.SMEM)
VMEM = pl.BlockSpec(memory_space=pltpu.VMEM)


def shape(dims, kind):
    return jax.ShapeDtypeStruct(tuple(dims), kind)


def params(megabytes, grid_dims=0):
    semantics = ("arbitrary",) * grid_dims if grid_dims else None
    return pltpu.CompilerParams(
        vmem_limit_bytes=megabytes * 1024 * 1024, dimension_semantics=semantics
    )


def cost(flops, moved):
    return pl.CostEstimate(flops=int(flops), bytes_accessed=int(moved), transcendentals=0)


def dot(left, right):
    return lax.dot_general(left, right, (((1,), (0,)), ((), ())), preferred_element_type=F32)


def dot_rows(left, right):
    return lax.dot_general(left, right, (((1,), (1,)), ((), ())), preferred_element_type=F32)


def dot_columns(left, right):
    return lax.dot_general(left, right, (((0,), (0,)), ((), ())), preferred_element_type=F32)


def centred(rows):
    center = rows - jnp.mean(rows, axis=-1, keepdims=True)
    spread = jnp.mean(center * center, axis=-1, keepdims=True)
    return center, lax.rsqrt(spread + EPS)


def norm_back(rows, gain, grad):
    center, rstd = centred(rows)
    xhat = center * rstd
    e = grad * gain
    back = rstd * (
        e - jnp.mean(e, axis=-1, keepdims=True) - xhat * jnp.mean(e * xhat, axis=-1, keepdims=True)
    )
    return (
        back,
        jnp.sum(grad * xhat, axis=0, keepdims=True),
        jnp.sum(grad, axis=0, keepdims=True),
    )


def norm_one_kernel(images, chunk, place, counts, tokens, gain, shift, out):
    rows = tokens.shape[0]

    @pl.loop(0, rows // chunk)
    def _(step):
        at = pl.ds(pl.multiple_of(step * chunk, chunk), chunk)
        center, rstd = centred(tokens[at, :].astype(F32))
        out[at, :] = (center * rstd * gain[...] + shift[...]).astype(BF16)

    extra = out.shape[0] - rows
    row = lax.broadcasted_iota(jnp.int32, (extra, out.shape[1]), 0)
    table = jnp.zeros((extra, out.shape[1]), F32)
    first = place[2] * images
    for image in range(images):
        table = jnp.where(row == image, counts[first + image].astype(F32), table)
    out[rows:, :] = table.astype(BF16)


def norm_one(place, counts, tokens, gain, shift):
    rows, width = tokens.shape
    images = rows // SLOTS
    return pl.pallas_call(
        functools.partial(norm_one_kernel, images, SLOTS),
        out_shape=shape((rows + 16, width), BF16),
        in_specs=[SMEM, SMEM, VMEM, VMEM, VMEM],
        out_specs=VMEM,
        compiler_params=params(16),
        cost_estimate=cost(rows * width * 10, rows * width * 4),
    )(place, counts, tokens, gain, shift)


def norm_two_kernel(tokens, mine, received, bias, gain, shift, first_sum, normed):
    total = tokens[...].astype(F32) + (mine[...] + received[...].astype(F32)) + bias[...]
    first_sum[...] = total
    center, rstd = centred(total)
    normed[...] = (center * rstd * gain[...] + shift[...]).astype(BF16)


def rows_spec(tile, width):
    return pl.BlockSpec((tile, width), lambda i: (i, 0))


def fixed_spec(*dims):
    return pl.BlockSpec(dims, lambda i: (0,) * len(dims))


def norm_two(tokens, mine, received, bias, gain, shift):
    rows, width = tokens.shape
    tile = 2 * SLOTS
    row = rows_spec(tile, width)
    vector = fixed_spec(1, width)
    return pl.pallas_call(
        norm_two_kernel,
        grid=(rows // tile,),
        out_shape=(shape((rows, width), F32), shape((rows, width), BF16)),
        in_specs=[row, row, row, vector, vector, vector],
        out_specs=(row, row),
        compiler_params=params(16, 1),
        cost_estimate=cost(rows * width * 12, rows * width * 14),
    )(tokens, mine, received, bias, gain, shift)


def norm_two_back_kernel(mine, received, first_sum, gain, output_grad, grad_first, low, sums):
    grad = mine[...] + received[...].astype(F32)
    back, grad_gain, grad_shift = norm_back(first_sum[...], gain[...], grad)
    out_grad = output_grad[...].astype(F32)
    total = out_grad + back
    grad_first[...] = total
    low[...] = total.astype(BF16)

    @pl.when(pl.program_id(0) == 0)
    def _():
        sums[...] = jnp.zeros_like(sums)

    sums[0:1, :] += grad_gain
    sums[1:2, :] += grad_shift
    sums[2:3, :] += jnp.sum(total, axis=0, keepdims=True)
    sums[3:4, :] += jnp.sum(out_grad, axis=0, keepdims=True)


def norm_two_back(mine, received, first_sum, gain, output_grad):
    rows, width = mine.shape
    tile = 2 * SLOTS
    row = rows_spec(tile, width)
    return pl.pallas_call(
        norm_two_back_kernel,
        grid=(rows // tile,),
        out_shape=(shape((rows, width), F32), shape((rows, width), BF16), shape((8, width), F32)),
        in_specs=[row, row, row, fixed_spec(1, width), row],
        out_specs=(row, row, fixed_spec(8, width)),
        compiler_params=params(16, 1),
        cost_estimate=cost(rows * width * 25, rows * width * 18),
    )(mine, received, first_sum, gain, output_grad)


def norm_one_back_kernel(mine, received, tokens, gain, grad_first, grad_tokens, sums):
    grad = mine[...] + received[...].astype(F32)
    back, grad_gain, grad_shift = norm_back(tokens[...].astype(F32), gain[...], grad)
    grad_tokens[...] = grad_first[...] + back

    @pl.when(pl.program_id(0) == 0)
    def _():
        sums[...] = jnp.zeros_like(sums)

    sums[0:1, :] += grad_gain
    sums[1:2, :] += grad_shift


def norm_one_back(mine, received, tokens, gain, grad_first):
    rows, width = mine.shape
    tile = 2 * SLOTS
    row = rows_spec(tile, width)
    return pl.pallas_call(
        norm_one_back_kernel,
        grid=(rows // tile,),
        out_shape=(shape((rows, width), F32), shape((8, width), F32)),
        in_specs=[row, row, row, fixed_spec(1, width), row],
        out_specs=(row, fixed_spec(8, width)),
        compiler_params=params(16, 1),
        cost_estimate=cost(rows * width * 25, rows * width * 16),
    )(mine, received, tokens, gain, grad_first)


def pack_attention_kernel(place, projection, mixer, bias, out, sem):
    quarter = place[0]
    size = out.shape[0] - 16
    feature_rows = projection.shape[0]
    first = pl.multiple_of(quarter * size, 16)
    from_projection = quarter * size < feature_rows

    @pl.when(from_projection)
    def _():
        copy = pltpu.make_async_copy(
            projection.at[pl.ds(first, size)], out.at[pl.ds(0, size)], sem
        )
        copy.start()
        copy.wait()

    @pl.when(jnp.logical_not(from_projection))
    def _():
        copy = pltpu.make_async_copy(mixer, out.at[pl.ds(0, size)], sem)
        copy.start()
        copy.wait()

    columns = bias.shape[1]
    row = lax.broadcasted_iota(jnp.int32, (16, columns), 0)
    both = bias[...].astype(F32)
    rows = jnp.where(row == 0, both[0:1, :], jnp.where(row == 1, both[1:2, :], 0.0))
    out[size:, :] = jnp.zeros((16, out.shape[1]), BF16)
    out[size:, 0:columns] = rows.astype(BF16)


def pack_attention(place, projection, mixer, bias):
    size, width = mixer.shape
    return pl.pallas_call(
        pack_attention_kernel,
        out_shape=shape((size + 16, width), BF16),
        in_specs=[SMEM, ANY, ANY, VMEM],
        out_specs=VMEM,
        scratch_shapes=[pltpu.SemaphoreType.DMA(())],
        compiler_params=params(8),
        cost_estimate=cost(0, 2 * size * width),
    )(place, projection, mixer, bias)


def pack_hidden_kernel(place, up, down, bias, out, sems):
    size = (out.shape[0] - 16) // 2
    first = pl.multiple_of(place[0] * size, 16)
    copies = [
        pltpu.make_async_copy(
            source.at[pl.ds(first, size)], out.at[pl.ds(index * size, size)], sems.at[index]
        )
        for index, source in enumerate((up, down))
    ]
    for copy in copies:
        copy.start()
    row = lax.broadcasted_iota(jnp.int32, (16, out.shape[1]), 0)
    out[2 * size :, :] = jnp.where(row == 0, bias[...].astype(F32), 0.0).astype(BF16)
    for copy in copies:
        copy.wait()


def pack_hidden(place, up, down, bias):
    size, width = up.shape[0] // 4, up.shape[1]
    return pl.pallas_call(
        pack_hidden_kernel,
        out_shape=shape((2 * size + 16, width), BF16),
        in_specs=[SMEM, ANY, ANY, VMEM],
        out_specs=VMEM,
        scratch_shapes=[pltpu.SemaphoreType.DMA((2,))],
        compiler_params=params(8),
        cost_estimate=cost(0, 4 * size * width),
    )(place, up, down, bias)


def piece_copies(place, pieces, target, matrices, sems):
    size = (pieces[0].shape[0] - 16) // matrices
    copies = []
    for flip, piece in enumerate(pieces):
        quarter = lax.bitwise_xor(place[0], flip)
        for matrix in range(matrices):
            to = pl.multiple_of(matrix * 4 * size + quarter * size, 16)
            copies.append((piece.at[pl.ds(matrix * size, size)], target.at[pl.ds(to, size)]))
    copies.append(
        (pieces[0].at[pl.ds(matrices * size, 16)], target.at[pl.ds(matrices * 4 * size, 16)])
    )
    return [
        pltpu.make_async_copy(source, to, sems.at[index])
        for index, (source, to) in enumerate(copies)
    ]


def shard_copies(shards, piece, target, sems):
    copies = []
    at = 0
    for shard in shards:
        copies.append((shard, target.at[pl.ds(at, shard.shape[0])]))
        at += shard.shape[0]
    copies.append((piece.at[pl.ds(piece.shape[0] - 16, 16)], target.at[pl.ds(at, 16)]))
    return [
        pltpu.make_async_copy(source, to, sems.at[index])
        for index, (source, to) in enumerate(copies)
    ]


def run_copies(copies):
    for copy in copies:
        copy.start()
    for copy in copies:
        copy.wait()


def head_lanes(rows, width):
    return lax.broadcasted_iota(jnp.int32, (rows, width), 1) // HD


def spread_heads(block, lanes, heads):
    gap = jnp.zeros((LANES - SLOTS, block.shape[1]), block.dtype)
    parts = []
    for head in range(heads):
        parts.append(jnp.where(lanes == head, block, jnp.zeros_like(block)))
        parts.append(gap)
    return jnp.concatenate(parts, axis=0)


def gather_heads(product, lanes, heads):
    total = product[0:SLOTS]
    for head in range(1, heads):
        total = jnp.where(lanes == head, product[head * LANES : head * LANES + SLOTS], total)
    return total


def load_attention(place, projection, mixer, piece, near, far, weights, sems):
    @pl.when(pl.program_id(0) == 0)
    def _():
        copies = piece_copies(place, near, weights.at[1], 1, sems)
        for copy in copies:
            copy.start()

        @pl.when(place[1] == 0)
        def _():
            run_copies(
                shard_copies((projection, mixer), piece, weights.at[0], sems.at[pl.ds(8, 8)])
            )

        @pl.when(place[1] != 0)
        def _():
            run_copies(piece_copies(place, far, weights.at[0], 1, sems.at[pl.ds(8, 8)]))

        for copy in copies:
            copy.wait()


def attention_kernel(
    heads,
    place,
    projection,
    mixer,
    piece,
    near0,
    near1,
    near2,
    near3,
    far0,
    far1,
    far2,
    far3,
    normed,
    counts,
    *rest,
):
    saved, soft, part, weights, table, sems = rest[-6:]
    load_attention(
        place,
        projection,
        mixer,
        piece,
        (near0, near1, near2, near3),
        (far0, far1, far2, far3),
        weights,
        sems,
    )
    cols = heads * HD
    visible_rows = counts[:, 0:LANES].astype(F32)
    for image in range(visible_rows.shape[0]):
        table[image, :, :] = visible_rows[image : image + 1, :]
    rows = normed[...]
    for slot in range(2):
        for index in range(3):
            value = dot_rows(rows, weights[slot, index * cols : (index + 1) * cols, :])
            if index != 1:
                bias_row = 0 if index == 0 else 1
                bias = weights[slot, 4 * cols : 4 * cols + 16, 0:cols].astype(F32)
                value = value + bias[bias_row : bias_row + 1, :]
            saved[4 * slot + index, :, :] = value.astype(BF16)

    lanes = head_lanes(SLOTS, cols)
    key_index = lax.broadcasted_iota(jnp.int32, (SLOTS, LANES), 1).astype(F32)
    first = pl.program_id(0) * TILE_IMAGES

    def one_image(image, carry):
        at = pl.ds(pl.multiple_of(image * SLOTS, 16), SLOTS)
        visible = key_index < table[first + image]
        for slot in range(2):
            queries = saved[4 * slot, at, :]
            keys = spread_heads(saved[4 * slot + 1, at, :], lanes, heads)
            values = spread_heads(saved[4 * slot + 2, at, :], lanes, heads)
            scores = dot_rows(queries, keys) * (HD**-0.5)
            lows = []
            for head in range(heads):
                one = jnp.where(visible, scores[:, head * LANES : (head + 1) * LANES], MASKED)
                exponent = jnp.exp(one - jnp.max(one, axis=-1, keepdims=True))
                total = jnp.sum(exponent, axis=-1, keepdims=True)
                lows.append((exponent / total).astype(BF16))
            low = jnp.concatenate(lows, axis=1)
            soft[at, slot * heads * LANES : (slot + 1) * heads * LANES] = low
            saved[4 * slot + 3, at, :] = dot(low, values).astype(BF16)
        return carry

    lax.fori_loop(0, TILE_IMAGES, one_image, 0, unroll=2)
    total = dot(saved[3, :, :], weights[0, 3 * cols : 4 * cols, :])
    total = total + dot(saved[7, :, :], weights[1, 3 * cols : 4 * cols, :])
    part[...] = total.astype(part.dtype)


def attention(place, own, near, far, normed, before, kind):
    projection, mixer, piece = own
    cols, width = mixer.shape
    heads = cols // HD
    rows = normed.shape[0] - 16
    tile = TILE_IMAGES * SLOTS
    tiles = rows // tile
    base = tiles if before is None else 0
    extra = () if before is None else tuple(before)
    args = (place, projection, mixer, piece, *near, *far, normed, normed, *extra)
    return pl.pallas_call(
        functools.partial(attention_kernel, heads),
        grid=(tiles,),
        out_shape=(
            shape((8, 2 * rows, cols), BF16),
            shape((2 * rows, 2 * heads * LANES), BF16),
            shape((rows, width), kind),
        ),
        in_specs=[SMEM]
        + [ANY] * 11
        + [
            pl.BlockSpec((tile, width), lambda i: (i, 0)),
            pl.BlockSpec((16, width), lambda i: (rows // 16, 0)),
        ]
        + [ANY] * len(extra),
        out_specs=(
            pl.BlockSpec((8, tile, cols), lambda i: (0, base + i, 0)),
            pl.BlockSpec((tile, 2 * heads * LANES), lambda i: (base + i, 0)),
            pl.BlockSpec((tile, width), lambda i: (i, 0)),
        ),
        scratch_shapes=[
            pltpu.VMEM((2, 4 * cols + 16, width), BF16),
            pltpu.VMEM((16, 1, LANES), F32),
            pltpu.SemaphoreType.DMA((16,)),
        ],
        input_output_aliases={14: 0, 15: 1} if extra else {},
        compiler_params=params(32, 1),
        cost_estimate=cost(rows * width * cols * 16 + rows * 400000, rows * width * 10 + 5e6),
    )(*args)


def split_gradient(place, source, matrices, send_x, send_y, keep_x, keep_y):
    half = send_x.shape[2]
    for flip in range(4):
        quarter = lax.bitwise_xor(place[0], flip)
        for part in range(2):
            at = pl.ds(pl.multiple_of((2 * quarter + part) * half, 16), half)
            if part == 0:
                ref, index = (keep_x, flip // 2) if flip % 2 == 0 else (send_x, flip // 2)
            else:
                ref, index = (keep_y, flip % 2) if flip < 2 else (send_y, flip % 2)
            for matrix in range(matrices):
                ref[matrix, index, :, :] = source(matrix, at).astype(BF16)


def gradient_outputs(matrices, size, width):
    spec = pl.BlockSpec((matrices, 2, size // 8, width), lambda i: (0, 0, 0, 0))
    return (shape((matrices, 2, size // 8, width), BF16),) * 4, (spec,) * 4


def attention_back_kernel(
    heads,
    place,
    projection,
    mixer,
    piece,
    near0,
    near1,
    near2,
    near3,
    far0,
    far1,
    far2,
    far3,
    normed_mine,
    normed_other,
    grad_mine,
    grad_other,
    saved,
    soft,
    send_x,
    send_y,
    keep_x,
    keep_y,
    back_mine,
    back_other,
    bias_sums,
    weights,
    sums,
    grads,
    sems,
):
    step = pl.program_id(0)
    steps = pl.num_programs(0)
    load_attention(
        place,
        projection,
        mixer,
        piece,
        (near0, near1, near2, near3),
        (far0, far1, far2, far3),
        weights,
        sems,
    )
    cols = heads * HD
    mine = step < steps // 2
    normed = jnp.where(mine, normed_mine[...], normed_other[...])
    grad = jnp.where(mine, grad_mine[...], grad_other[...])

    @pl.when(step == 0)
    def _():
        sums[...] = jnp.zeros_like(sums)
        bias_sums[...] = jnp.zeros_like(bias_sums)

    for slot in range(2):
        grads[4 * slot + 3, :, :] = dot_rows(
            grad, weights[slot, 3 * cols : 4 * cols, :]
        ).astype(BF16)

    lanes = head_lanes(SLOTS, cols)

    def one_image(image, carry):
        at = pl.ds(pl.multiple_of(image * SLOTS, 16), SLOTS)
        for slot in range(2):
            queries = saved[4 * slot, at, :]
            keys = spread_heads(saved[4 * slot + 1, at, :], lanes, heads)
            values = spread_heads(saved[4 * slot + 2, at, :], lanes, heads)
            grad_mixed = grads[4 * slot + 3, at, :]
            low = soft[at, slot * heads * LANES : (slot + 1) * heads * LANES]
            grad_soft = dot_rows(grad_mixed, values)
            lows = []
            for head in range(heads):
                one = low[:, head * LANES : (head + 1) * LANES].astype(F32)
                grad_one = grad_soft[:, head * LANES : (head + 1) * LANES]
                inner = jnp.sum(grad_one * one, axis=-1, keepdims=True)
                lows.append((one * (grad_one - inner) * (HD**-0.5)).astype(BF16))
            grad_scores = jnp.concatenate(lows, axis=1)
            grad_queries = dot(grad_scores, keys)
            grad_values = gather_heads(dot_columns(low, grad_mixed), lanes, heads)
            grad_keys = gather_heads(dot_columns(grad_scores, queries), lanes, heads)
            bias_sums[2 * slot : 2 * slot + 1, :] += jnp.sum(grad_queries, axis=0, keepdims=True)
            bias_sums[2 * slot + 1 : 2 * slot + 2, :] += jnp.sum(
                grad_values, axis=0, keepdims=True
            )
            grads[4 * slot, at, :] = grad_queries.astype(BF16)
            grads[4 * slot + 1, at, :] = grad_keys.astype(BF16)
            grads[4 * slot + 2, at, :] = grad_values.astype(BF16)
        return carry

    lax.fori_loop(0, TILE_IMAGES, one_image, 0, unroll=2)
    back = None
    for slot in range(2):
        for index in range(3):
            at = slice(index * cols, (index + 1) * cols)
            value = grads[4 * slot + index, :, :]
            term = dot(value, weights[slot, at, :])
            back = term if back is None else back + term
            sums[slot, at, :] += dot_columns(value, normed)
        sums[slot, 3 * cols : 4 * cols, :] += dot_columns(saved[4 * slot + 3, :, :], grad)

    @pl.when(mine)
    def _():
        back_mine[...] = back

    @pl.when(jnp.logical_not(mine))
    def _():
        back_other[...] = back.astype(BF16)

    @pl.when(step == steps - 1)
    def _():
        split_gradient(
            place, lambda m, at: sums[m, at, :], 2, send_x, send_y, keep_x, keep_y
        )


def half_spec(tile, width, tiles, second):
    if second:
        return pl.BlockSpec((tile, width), lambda i: (jnp.maximum(i - tiles, 0), 0))
    return pl.BlockSpec((tile, width), lambda i: (jnp.minimum(i, tiles - 1), 0))


def attention_back(place, own, near, far, normed, grads, saved, soft):
    projection, mixer, piece = own
    cols, width = mixer.shape
    heads = cols // HD
    rows = grads[0].shape[0]
    tile = TILE_IMAGES * SLOTS
    tiles = rows // tile
    mine, other = half_spec(tile, width, tiles, False), half_spec(tile, width, tiles, True)
    grad_shapes, grad_specs = gradient_outputs(2, 4 * cols, width)
    return pl.pallas_call(
        functools.partial(attention_back_kernel, heads),
        grid=(2 * tiles,),
        out_shape=(
            *grad_shapes,
            shape((rows, width), F32),
            shape((rows, width), BF16),
            shape((8, cols), F32),
        ),
        in_specs=[SMEM]
        + [ANY] * 11
        + [
            mine,
            other,
            mine,
            other,
            pl.BlockSpec((8, tile, cols), lambda i: (0, i, 0)),
            pl.BlockSpec((tile, 2 * heads * LANES), lambda i: (i, 0)),
        ],
        out_specs=(*grad_specs, mine, other, fixed_spec(8, cols)),
        scratch_shapes=[
            pltpu.VMEM((2, 4 * cols + 16, width), BF16),
            pltpu.VMEM((2, 4 * cols, width), F32),
            pltpu.VMEM((8, tile, cols), BF16),
            pltpu.SemaphoreType.DMA((16,)),
        ],
        compiler_params=params(48, 1),
        cost_estimate=cost(rows * width * cols * 60 + rows * 1.2e6, rows * width * 20 + 8e6),
    )(place, projection, mixer, piece, *near, *far, *normed, *grads, saved, soft)


def hidden_kernel(
    whole,
    last,
    place,
    up,
    down,
    piece,
    piece0,
    piece1,
    piece2,
    piece3,
    normed_mine,
    normed_other,
    grad_mine,
    grad_other,
    *rest,
):
    if last:
        out_in, back_in = rest[:2]
        rest = rest[2:]
        send_x, send_y, keep_x, keep_y, bias_sums = rest[:5]
        out_mine, out_other, back_mine, back_other = rest[5:9]
        rest = rest[9:]
    else:
        send_x, send_y, keep_x, keep_y, bias_sums = rest[:5]
        out_sum, back_sum = rest[5:7]
        rest = rest[7:]
    weights, sums_up, sums_down, out_part, back_part, sems = rest
    step = pl.program_id(0)
    steps = pl.num_programs(0)
    width = normed_mine.shape[1]

    @pl.when(step == 0)
    def _():
        pieces = (piece0, piece1, piece2, piece3)
        if whole:

            @pl.when(place[1] == 0)
            def _():
                run_copies(shard_copies((up, down), piece, weights, sems))

            @pl.when(place[1] != 0)
            def _():
                run_copies(piece_copies(place, pieces, weights, 2, sems))

        else:
            run_copies(piece_copies(place, pieces, weights, 2, sems))
        sums_up[...] = jnp.zeros_like(sums_up)
        sums_down[...] = jnp.zeros_like(sums_down)
        bias_sums[...] = jnp.zeros_like(bias_sums)

    mine = step < steps // 2
    normed = jnp.where(mine, normed_mine[...], normed_other[...])
    grad = jnp.where(mine, grad_mine[...], grad_other[...])
    bias_rows = weights[2 * width : 2 * width + 16, :].astype(F32)
    chunk = 256
    for first in range(0, width, chunk):
        columns = slice(first, first + chunk)
        up_part = weights[0:width, columns]
        down_part = weights[width + first : width + first + chunk, :]
        hidden = dot(normed, up_part) + bias_rows[0:1, columns]
        phi = 0.5 + 0.5 * lax.erf(hidden * (0.5**0.5))
        slope = phi + hidden * (jnp.exp(-0.5 * hidden * hidden) * ((2.0 * np.pi) ** -0.5))
        active = (hidden * phi).astype(BF16)
        grad_pre = dot_rows(grad, down_part) * slope
        bias_sums[0:1, columns] += jnp.sum(grad_pre, axis=0, keepdims=True)
        grad_low = grad_pre.astype(BF16)
        out_term = dot(active, down_part)
        back_term = dot_rows(grad_low, up_part)
        if first == 0:
            if last:
                out_part[...] = out_in[...] + out_term
                back_part[...] = back_in[...] + back_term
            else:
                out_part[...] = out_term
                back_part[...] = back_term
        else:
            out_part[...] += out_term
            back_part[...] += back_term
        sums_up[:, columns] += dot_columns(normed, grad_low)
        sums_down[columns, :] += dot_columns(active, grad)

    if last:

        @pl.when(mine)
        def _():
            out_mine[...] = out_part[...]
            back_mine[...] = back_part[...]

        @pl.when(jnp.logical_not(mine))
        def _():
            out_other[...] = out_part[...].astype(BF16)
            back_other[...] = back_part[...].astype(BF16)

    else:
        out_sum[...] = out_part[...]
        back_sum[...] = back_part[...]

    @pl.when(step == steps - 1)
    def _():
        split_gradient(
            place,
            lambda m, at: (sums_up if m == 0 else sums_down)[at, :],
            2,
            send_x,
            send_y,
            keep_x,
            keep_y,
        )


def hidden_block(place, own, pieces, normed, grads, sums_before, whole):
    up, down, piece = own
    width = up.shape[0]
    rows = normed[0].shape[0]
    tile = TILE_IMAGES * SLOTS
    tiles = rows // tile
    last = sums_before is not None
    mine, other = half_spec(tile, width, tiles, False), half_spec(tile, width, tiles, True)
    both = rows_spec(tile, width)
    grad_shapes, grad_specs = gradient_outputs(2, width, width)
    if last:
        more_shapes = (
            shape((rows, width), F32),
            shape((rows, width), BF16),
            shape((rows, width), F32),
            shape((rows, width), BF16),
        )
        more_specs = (mine, other, mine, other)
    else:
        more_shapes = (shape((2 * rows, width), F32),) * 2
        more_specs = (both, both)
    return pl.pallas_call(
        functools.partial(hidden_kernel, whole, last),
        grid=(2 * tiles,),
        out_shape=(*grad_shapes, shape((8, width), F32), *more_shapes),
        in_specs=[SMEM]
        + [ANY] * 7
        + [mine, other, mine, other]
        + ([both, both] if last else []),
        out_specs=(*grad_specs, fixed_spec(8, width), *more_specs),
        scratch_shapes=[
            pltpu.VMEM((2 * width + 16, width), BF16),
            pltpu.VMEM((width, width), F32),
            pltpu.VMEM((width, width), F32),
            pltpu.VMEM((tile, width), F32),
            pltpu.VMEM((tile, width), F32),
            pltpu.SemaphoreType.DMA((16,)),
        ],
        compiler_params=params(52, 1),
        cost_estimate=cost(rows * width * width * 24, rows * width * 24 + 8e6),
    )(place, up, down, piece, *pieces, *normed, *grads, *(sums_before or ()))


def finish_kernel(place, mine, other, *outs):
    half = mine.shape[2]
    for flip in range(4):
        quarter = lax.bitwise_xor(place[0], flip)
        for side, ref in enumerate((mine, other)):
            part = place[1] if side == 0 else 1 - place[1]
            for matrix, out in enumerate(outs):
                at = pl.ds(pl.multiple_of((2 * quarter + part) * half, 8), half)
                out[at, :] = ref[flip, matrix, :, :].astype(F32)


def finish(place, mine, other):
    matrices, half, width = mine.shape[1:]
    return pl.pallas_call(
        finish_kernel,
        out_shape=(shape((8 * half, width), F32),) * matrices,
        in_specs=[SMEM, VMEM, VMEM],
        out_specs=(VMEM,) * matrices,
        compiler_params=params(32),
        cost_estimate=cost(0, matrices * half * width * 48),
    )(place, mine, other)


def local(
    tokens,
    visible_counts,
    norm_one_gain,
    norm_one_shift,
    input_weight,
    input_bias,
    mixer_weight,
    mixer_bias,
    norm_two_gain,
    norm_two_shift,
    up_weight,
    up_bias,
    down_weight,
    down_bias,
    output_grad,
    groups,
    outer,
):
    width = tokens.shape[1]
    rows = tokens.shape[0]
    cols = mixer_weight.shape[0]
    t = lax.axis_index("t")
    core = lax.axis_index("c")
    place = jnp.stack([2 * lax.axis_index("a") + lax.axis_index("b"), core, t]).astype(jnp.int32)
    one_row = lambda v: v.reshape(1, -1)

    swap = [(0, 1), (1, 0)]
    cross = [(0, 3), (1, 2), (2, 1), (3, 0)]
    to_near = [(z, (z + 1) % groups) for z in range(groups)] + [
        (groups + z, groups + (z + 2) % groups) for z in range(groups)
    ]
    to_far = [(groups + z, groups + (z + 3) % groups) for z in range(groups)]
    back_near = [(j, i) for i, j in to_near]
    back_far = [(j, i) for i, j in to_far]
    flip_x = [(2 * i + 1, 2 * (i ^ 1) + 1) for i in range(4)]
    flip_y = [(2 * i + 1, 2 * (i ^ 2) + 1) for i in range(4)]
    flip_xy = [(2 * i + 1, 2 * (i ^ 3) + 1) for i in range(4)]

    def spread(piece):
        return (
            piece,
            lax.ppermute(piece, "b", swap),
            lax.ppermute(piece, "a", swap),
            lax.ppermute(piece, ("a", "b"), cross),
        )

    def spread_second(piece):
        return (
            piece,
            lax.ppermute(piece, ("a", "b", "c"), flip_x),
            lax.ppermute(piece, ("a", "b", "c"), flip_y),
            lax.ppermute(piece, ("a", "b", "c"), flip_xy),
        )

    projection = input_weight.transpose(1, 2, 0).reshape(3 * cols, width)
    piece_one = pack_attention(place, projection, mixer_weight, input_bias)
    near_one = spread(lax.ppermute(piece_one, ("c", "t"), to_near))
    far_one = spread_second(lax.ppermute(piece_one, ("c", "t"), to_far))
    normed_one = norm_one(
        place, visible_counts, tokens, one_row(norm_one_gain), one_row(norm_one_shift)
    )
    normed_other = lax.ppermute(normed_one, "c", swap)
    piece_two = pack_hidden(place, up_weight, down_weight, one_row(up_bias))
    near_two = spread(lax.ppermute(piece_two, ("c", "t"), to_near))
    far_two = spread_second(lax.ppermute(piece_two, ("c", "t"), to_far))
    grad_other = lax.ppermute(output_grad, "c", swap)

    own_one = (projection, mixer_weight, piece_one)
    saved, soft, part = attention(place, own_one, near_one, far_one, normed_other, None, BF16)
    part_received = lax.ppermute(part, "c", swap)
    saved, soft, part = attention(
        place, own_one, near_one, far_one, normed_one, (saved, soft), F32
    )
    first_sum, normed_two = norm_two(
        tokens,
        part,
        part_received,
        one_row(mixer_bias),
        one_row(norm_two_gain),
        one_row(norm_two_shift),
    )
    normed_two_both = (normed_two, lax.ppermute(normed_two, "c", swap))

    own_two = (up_weight, down_weight, piece_two)
    grad_both = (output_grad, grad_other)
    *grads_near, bias_near, out_sum, back_sum = hidden_block(
        place, own_two, near_two, normed_two_both, grad_both, None, False
    )
    *grads_far, bias_far, out_mine, out_send, back_mine, back_send = hidden_block(
        place, own_two, far_two, normed_two_both, grad_both, (out_sum, back_sum), True
    )
    back_received = lax.ppermute(back_send, "c", swap)
    grad_first, grad_first_low, sums_two = norm_two_back(
        back_mine, back_received, first_sum, one_row(norm_two_gain), output_grad
    )
    out_received = lax.ppermute(out_send, "c", swap)
    result = (first_sum + (out_mine + out_received.astype(F32)) + down_bias).astype(BF16)

    first_both = (grad_first_low, lax.ppermute(grad_first_low, "c", swap))
    *grads_one, back_mine, back_send, bias_one = attention_back(
        place, own_one, near_one, far_one, (normed_one, normed_other), first_both, saved, soft
    )
    back_received = lax.ppermute(back_send, "c", swap)
    grad_tokens, sums_one = norm_one_back(
        back_mine, back_received, tokens, one_row(norm_one_gain), grad_first
    )

    def plane_sum(send_x, send_y, keep_x, keep_y):
        got_x = lax.ppermute(send_x, "b", swap)
        got_y = lax.ppermute(send_y, "a", swap)
        add = lambda u, v: u.astype(F32) + v.astype(F32)
        next_y = lax.ppermute(add(keep_x[:, 1], got_x[:, 1]).astype(BF16), "a", swap)
        next_x = lax.ppermute(add(keep_y[:, 1], got_y[:, 1]).astype(BF16), "b", swap)
        first = (add(keep_x[:, 0], got_x[:, 0]) + next_y.astype(F32)).astype(BF16)
        second = (add(keep_y[:, 0], got_y[:, 0]) + next_x.astype(F32)).astype(BF16)
        return jnp.stack([first, second])

    is_first = core == 0

    def depth_sum(local_far, far, near):
        total = jnp.where(is_first, local_far, far).astype(F32) + near.astype(F32)
        keep = jnp.where(is_first, total[0], total[1])
        send = jnp.where(is_first, total[1], total[0]).astype(BF16)
        total = keep + lax.ppermute(send, "c", swap).astype(F32)
        if outer > 1:
            total = lax.psum(total, "o")
        return total.astype(BF16)

    def collect(part):
        mine = jnp.stack(spread(part))
        return finish(place, mine, lax.ppermute(mine, "c", swap))

    plane_near = plane_sum(*grads_near)
    plane_far = plane_sum(*grads_far)
    depth_near = lax.ppermute(plane_near, ("c", "t"), back_near)
    depth_far = lax.ppermute(plane_far, ("c", "t"), back_far)
    grad_up, grad_down = collect(depth_sum(plane_far, depth_far, depth_near))

    plane_one = plane_sum(*grads_one)
    far_part, near_part = plane_one[:, 0:1], plane_one[:, 1:2]
    depth_near = lax.ppermute(near_part, ("c", "t"), back_near)
    depth_far = lax.ppermute(far_part, ("c", "t"), back_far)
    (grad_block,) = collect(depth_sum(far_part, depth_far, depth_near))
    grad_input = grad_block[: 3 * cols].reshape(3, cols, width).transpose(2, 0, 1)
    grad_mixer = grad_block[3 * cols :]

    near_owner = jnp.where(is_first, t - 1, t - 2) % groups
    far_owner = jnp.where(is_first, t, t - 3) % groups
    owners = jnp.arange(groups)[:, None]
    by_owner = lambda near, far: jnp.where(owners == near_owner, near, 0.0) + jnp.where(
        owners == far_owner, far, 0.0
    )
    wide = lambda v: jnp.pad(v.reshape(1, -1), ((0, 0), (0, width - v.size)))
    bias_rows = by_owner(bias_near[0:1], bias_far[0:1])
    input_rows = by_owner(wide(bias_one[2:4]), wide(bias_one[0:2]))
    vectors = jnp.concatenate([sums_one[0:2], sums_two[0:4], bias_rows, input_rows])
    for axis in ("c", "b", "a"):
        vectors = vectors + lax.ppermute(vectors, axis, swap)
    turns = [
        lax.ppermute(vectors, "t", [(z, (z + k) % groups) for z in range(groups)])
        for k in range(1, groups)
    ]
    for turn in turns:
        vectors = vectors + turn
    if outer > 1:
        vectors = lax.psum(vectors, "o")
    grad_up_bias = lax.dynamic_slice_in_dim(vectors, 6 + t, 1)[0]
    grad_input_bias = lax.dynamic_slice_in_dim(vectors, 6 + groups + t, 1)[0, : 2 * cols].reshape(
        2, cols
    )
    return (
        result,
        grad_tokens,
        vectors[0],
        vectors[1],
        grad_input,
        grad_input_bias,
        grad_mixer,
        vectors[4],
        vectors[2],
        vectors[3],
        grad_up,
        grad_up_bias,
        grad_down,
        vectors[5],
    )


def solution(mesh):
    dp, groups = mesh.shape["dp"], mesh.shape["tensor"]
    outer = dp // 8
    split = jax.sharding.Mesh(
        mesh.devices.reshape(outer, 2, 2, 2, groups), ("o", "a", "b", "c", "t")
    )
    dp_axes = ("o", "a", "b", "c")
    all_axes = dp_axes + ("t",)
    in_specs = (
        P(all_axes, None),
        P(dp_axes),
        P(),
        P(),
        P(None, None, "t"),
        P(None, "t"),
        P("t", None),
        P(),
        P(),
        P(),
        P(None, "t"),
        P("t"),
        P("t", None),
        P(),
        P(all_axes, None),
    )
    out_specs = (
        P(all_axes, None),
        P(all_axes, None),
        P(),
        P(),
        P(None, None, "t"),
        P(None, "t"),
        P("t", None),
        P(),
        P(),
        P(),
        P(None, "t"),
        P("t"),
        P("t", None),
        P(),
    )
    return jax.shard_map(
        functools.partial(local, groups=groups, outer=outer),
        mesh=split,
        in_specs=in_specs,
        out_specs=out_specs,
        check_vma=False,
    )
```

time: 1010 us -> 336 us (0.33)
  waiting for transfers between devices: 732 us -> 103 us
  matrix products: 105 us -> 0 us
  Pallas kernels: 0 us -> 105 us
  starting transfers between devices: 1.09 us -> 88.2 us
  blocking collectives: 56.1 us -> 0 us
  local copies, waits for them, and re-layouts: 62.3 us -> 22.6 us
  other arithmetic: 38.2 us -> 14.1 us
  between operations: 14.8 us -> 1.5 us
    reduce_scatter x4 -> x0, waiting for transfers between devices: 361 us -> none  [the longest x1 135 us: local(): lax.psum_scatter(jnp.dot(blend_low, mixer_weight, preferred_element_type=...]
    all_gather x4 -> x0, waiting for transfers between devices: 300 us -> none  [the longest x1 79 us: local(): whole_one = lax.all_gather(low_one, 'tensor', axis=0, tiled=True)]
    pallas_call x0 -> x13, Pallas kernels: none -> 105 us  [the longest x2 39.4 us: hidden_block(): pl.pallas_call(functools.partial(hidden_kernel, whole, last), grid=(2 * t...]
    ppermute x0 -> x56, waiting for transfers between devices: none -> 103 us  [the longest x3 20 us: plane_sum(): got_y = lax.ppermute(send_y, 'a', swap)]
    dot_general x17 -> x0, matrix products: 102 us -> none  [the longest x1 23.8 us: mlp_back(): jnp.einsum('rd,fd->rf', grad_rows, weight_down, preferred_element_type=jn...]
    ppermute x0 -> x56, starting transfers between devices: none -> 88.2 us  [the longest x2 13.1 us: depth_sum(): total = keep + lax.ppermute(send, 'c', swap).astype(F32)]
    psum x1 -> x0, waiting for transfers between devices: 71.1 us -> none  [local(): lax.psum((weight_terms[0], weight_terms[1], weight_terms[2], weight_terms...]
    psum x2 -> x0, blocking collectives: 56.1 us -> none  [the longest x1 41.7 us: local(): lax.psum((grad_gain_one, grad_shift_one, jnp.sum(grad_first, axis=0), gra...]
  transfers between devices with their start and end apart: 9 -> 56, of which waited for: 9 -> 19; matrix products, arithmetic and copies ran while one was open for 5% -> 5% of each run, Pallas kernels for 0% -> 27%
where the time goes in v1:
time: 336 us; the launch traced here: 335 us
  Pallas kernels  105 us (31%)
  waiting for transfers between devices  103 us (31%)
  starting transfers between devices  88.2 us (26%)
  local copies, waits for them, and re-layouts  22.6 us (7%)
  other arithmetic  14.1 us (4%)
    pallas_call x2, Pallas kernels, hidden_block(): pl.pallas_call(functools.partial(hidden_kernel, whole, last), grid=(2 * t...  39.4 us
    pallas_call x1, Pallas kernels, attention_back(): pl.pallas_call(functools.partial(attention_back_kernel, heads), grid=(2 *...  29 us
    pallas_call x2, Pallas kernels, attention(): pl.pallas_call(functools.partial(attention_kernel, heads), grid=(tiles,),...  21.4 us
    ppermute x3, waiting for transfers between devices, plane_sum(): got_y = lax.ppermute(send_y, 'a', swap)  20 us
    ppermute x4, waiting for transfers between devices, spread(): lax.ppermute(piece, 'a', swap)  20 us
    unnamed x112, local copies, waits for them, and re-layouts  17.2 us
    ppermute x4, waiting for transfers between devices, spread(): lax.ppermute(piece, 'b', swap)  16.2 us
    ppermute x2, starting transfers between devices, depth_sum(): total = keep + lax.ppermute(send, 'c', swap).astype(F32)  13.1 us
  transfers between devices with their start and end apart: 56, of which 19 were waited for; matrix products, arithmetic and copies ran while one was open for 5% of the time, Pallas kernels for 27%

profile of v1, /device:TPU:0, one launch (start us, length us, event | category | flops | bytes accessed | tf_op | source)
XLA Modules:
  0.0 334.5 jit_solution(18026956269465991314)
XLA Ops:
  2.1 1.2 copy-done.1
  4.0 2.2 shard_map.255.normed.counts.normed_mine
  7.4 2.7 collective-permute-start
  10.8 9.9 %collective-permute-done.near0 = bf16[208,768]{1,0:T(8,128)(2,1)S(1)} collective-permute-done((bf16[208,768]{1,0:T(8,128)(2,1)S(1)}, bf16[208,768]{1,0:T(8,128)(2,1)S(1)}, u32[]{:S(2)}, u32[]{:S(2)}) %collective-permute-start) | collective-permute-done | bytes 319520 | tf_op jit(solution)/shard_map/ppermute | solution.py:872
  20.6 1.6 collective-permute-start.1
  22.3 1.5 collective-permute-start.2
  24.8 5.2 %collective-permute-done.1.near1 = bf16[208,768]{1,0:T(8,128)(2,1)S(1)} collective-permute-done((bf16[208,768]{1,0:T(8,128)(2,1)S(1)}, bf16[208,768]{1,0:T(8,128)(2,1)S(1)}, u32[]{:S(2)}, u32[]{:S(2)}) %collective-permute-start.1) | collective-permute-done | bytes 319520 | tf_op jit(solution)/shard_map/ppermute | solution.py:857
  30.7 7.2 %collective-permute-done.2.near2 = bf16[208,768]{1,0:T(8,128)(2,1)S(1)} collective-permute-done((bf16[208,768]{1,0:T(8,128)(2,1)S(1)}, bf16[208,768]{1,0:T(8,128)(2,1)S(1)}, u32[]{:S(2)}, u32[]{:S(2)}) %collective-permute-start.2) | collective-permute-done | bytes 319520 | tf_op jit(solution)/shard_map/ppermute | solution.py:858
  38.7 10.7 %shard_map.256 = (bf16[8,1280,192]{2,1,0:T(8,128)(2,1)S(1)}, bf16[1280,768]{1,0:T(8,128)(2,1)S(1)}, bf16[640,768]{1,0:T(8,128)(2,1)S(1)}) custom-call(s32[3]{0:T(128)S(1)} %pad_add_fusion.place, bf16[576,768]{1,0:T(8,128)(2,1)S(1)} %bitcast.91, bf16[192,768]{1,0:T(8,128)(2,1)S(1)} %copy-done.12, bf16[208,768]{1,0:T(8,128)(2,1)S(1)} %shard_map.254.piece, ...), custom_call_target="tpu_custom_call" | custom-call | flops 1765949440 | bytes 9915200 | tf_op jit(solution)/shard_map/pallas_call | solution.py:427
  50.4 9.3 %collective-permute-start.9 = (bf16[640,768]{1,0:T(8,128)(2,1)S(1)}, bf16[640,768]{1,0:T(8,128)(2,1)S(1)}, u32[]{:S(2)}, u32[]{:S(2)}) collective-permute-start(bf16[640,768]{1,0:T(8,128)(2,1)S(1)} %get-tuple-element.55), channel_id=1, source_target_pairs={{0,4},{4,0},{1,5},{5,1},{2,6},{6,2},{3,7},{7,3},{8,12},{12,8},{9,1... | collective-permute-start | bytes 2949128 | tf_op jit(solution)/shard_map/ppermute | solution.py:885
  60.4 3.0 collective-permute-start.16
  64.1 3.1 collective-permute-start.15
  67.4 10.7 %shard_map.257 = (bf16[8,1280,192]{2,1,0:T(8,128)(2,1)S(1)}, bf16[1280,768]{1,0:T(8,128)(2,1)S(1)}, f32[640,768]{1,0:T(8,128)S(1)}) custom-call(s32[3]{0:T(128)S(1)} %pad_add_fusion.place, bf16[576,768]{1,0:T(8,128)(2,1)S(1)} %bitcast.92, bf16[192,768]{1,0:T(8,128)(2,1)S(1)} %copy-done.12, ...), custom_call_target="tpu_custom_call", output_to_operand_aliasing={{0}: (14, {}), {1}: (15, {})} | custom-call | flops 1765949440 | bytes 9915200 | tf_op jit(solution)/shard_map/pallas_call | solution.py:427
  78.1 2.3 copy-done.5
  80.4 1.2 shard_map.258
  81.8 1.6 collective-permute-start.17
  83.4 1.2 collective-permute-start.18
  84.6 1.5 collective-permute-start.19
  86.8 11.0 %collective-permute-done.17.piece1 = bf16[400,768]{1,0:T(8,128)(2,1)S(1)} collective-permute-done((bf16[400,768]{1,0:T(8,128)(2,1)S(1)}, bf16[400,768]{1,0:T(8,128)(2,1)S(1)}, u32[]{:S(2)}, u32[]{:S(2)}) %collective-permute-start.17) | collective-permute-done | bytes 614432 | tf_op jit(solution)/shard_map/ppermute | solution.py:857
  97.8 1.5 collective-permute-start.12
  99.3 12.7 %collective-permute-done.18.piece2 = bf16[400,768]{1,0:T(8,128)(2,1)S(1)} collective-permute-done((bf16[400,768]{1,0:T(8,128)(2,1)S(1)}, bf16[400,768]{1,0:T(8,128)(2,1)S(1)}, u32[]{:S(2)}, u32[]{:S(2)}) %collective-permute-start.18) | collective-permute-done | bytes 614432 | tf_op jit(solution)/shard_map/ppermute | solution.py:858
  112.1 1.5 collective-permute-start.13
  115.7 18.8 %shard_map.260 = (bf16[2,2,96,768]{3,2,1,0:T(8,128)(2,1)S(1)}, bf16[2,2,96,768]{3,2,1,0:T(8,128)(2,1)S(1)}, bf16[2,2,96,768]{3,2,1,0:T(8,128)(2,1)S(1)}, bf16[2,...) custom-call(s32[3]{0:T(128)S(1)} %pad_add_fusion.place, ...), custom_call_target="tpu_custom_call" | custom-call | flops 9059696640 | bytes 19796480 | tf_op jit(solution)/shard_map/pallas_call | solution.py:770
  134.6 2.2 collective-permute-start.48
  136.9 2.0 collective-permute-start.46
  139.7 20.6 %shard_map.261 = (bf16[2,2,96,768]{3,2,1,0:T(8,128)(2,1)S(1)}, bf16[2,2,96,768]{3,2,1,0:T(8,128)(2,1)S(1)}, bf16[2,2,96,768]{3,2,1,0:T(8,128)(2,1)S(1)}, bf16[2,...) custom-call(s32[3]{0:T(128)S(1)} %pad_add_fusion.place, ...), custom_call_target="tpu_custom_call" | custom-call | flops 9059696640 | bytes 19796480 | tf_op jit(solution)/shard_map/pallas_call | solution.py:770
  163.3 1.5 collective-permute-start.47
  164.9 11.8 %collective-permute-done.43 = bf16[2,2,96,768]{3,2,0,1:T(8,128)(2,1)S(1)} collective-permute-done((bf16[2,2,96,768]{3,2,0,1:T(8,128)(2,1)S(1)}, bf16[2,2,96,768]{3,2,0,1:T(8,128)(2,1)S(1)}, u32[]{:S(2)}, u32[]{:S(2)}) %collective-permute-start.43) | collective-permute-done | bytes 589856 | tf_op jit(solution)/shard_map/ppermute | solution.py:925
  177.4 1.4 collective-permute-start.42
  178.8 4.8 %collective-permute-done.49 = bf16[2,96,768]{2,1,0:T(8,128)(2,1)S(1)} collective-permute-done((bf16[2,96,768]{2,1,0:T(8,128)(2,1)S(1)}, bf16[2,96,768]{2,1,0:T(8,128)(2,1)S(1)}, u32[]{:S(2)}, u32[]{:S(2)}) %collective-permute-start.49) | collective-permute-done | bytes 294944 | tf_op jit(solution)/shard_map/ppermute | solution.py:928
  185.5 3.5 %collective-permute-done.44 = bf16[2,96,768]{2,1,0:T(8,128)(2,1)S(1)} collective-permute-done((bf16[2,96,768]{2,1,0:T(8,128)(2,1)S(1)}, bf16[2,96,768]{2,1,0:T(8,128)(2,1)S(1)}, u32[]{:S(2)}, u32[]{:S(2)}) %collective-permute-start.44) | collective-permute-done | bytes 294944 | tf_op jit(solution)/shard_map/ppermute | solution.py:928
  190.1 1.5 collective-permute-start.45
  191.6 2.9 shard_map.262
  194.5 1.3 copy-done.7
  195.8 5.8 %collective-permute-start.22 = (bf16[640,768]{1,0:T(8,128)(2,1)}, bf16[640,768]{1,0:T(8,128)(2,1)}, u32[]{:S(2)}, u32[]{:S(2)}) collective-permute-start(bf16[640,768]{1,0:T(8,128)(2,1)} %get-tuple-element.64.grad_mine), channel_id=1, source_target_pairs={{0,4},{4,0},{1,5},{5,1},{2,6},{6,2},{3,7},{7,3},{8,12},{12,8},{9,1... | collective-permute-start | bytes 2949128 | tf_op jit(solution)/shard_map/ppermute | solution.py:914
  201.6 1.3 convert_add_fusion
  203.0 12.7 %collective-permute-start.51 = (bf16[2,96,768]{2,1,0:T(8,128)(2,1)S(1)}, bf16[2,96,768]{2,1,0:T(8,128)(2,1)S(1)}, u32[]{:S(2)}, u32[]{:S(2)}) collective-permute-start(bf16[2,96,768]{2,1,0:T(8,128)(2,1)S(1)} %fusion.13), channel_id=1, source_target_pairs={{0,4},{4,0},{1,5},{5,1},{2,6},{6,2},{3,7},{7,3},{8,12},{12,8},{9,1... | collective-permute-start | bytes 884744 | tf_op jit(solution)/shard_map/ppermute | solution.py:939
  220.6 29.0 %shard_map.263 = (bf16[2,2,96,768]{3,2,1,0:T(8,128)(2,1)S(1)}, bf16[2,2,96,768]{3,2,1,0:T(8,128)(2,1)S(1)}, bf16[2,2,96,768]{3,2,1,0:T(8,128)(2,1)S(1)}, bf16[2,...) custom-call(s32[3]{0:T(128)S(1)} %pad_add_fusion.place, ...), custom_call_target="tpu_custom_call" | custom-call | flops 6430310400 | bytes 17830400 | tf_op jit(solution)/shard_map/pallas_call | solution.py:607
  249.7 2.4 collective-permute-start.30
  252.4 1.6 collective-permute-start.54
  254.0 12.3 %collective-permute-done.30 = bf16[2,2,96,768]{3,2,0,1:T(8,128)(2,1)S(1)} collective-permute-done((bf16[2,2,96,768]{3,2,0,1:T(8,128)(2,1)S(1)}, bf16[2,2,96,768]{3,2,0,1:T(8,128)(2,1)S(1)}, u32[]{:S(2)}, u32[]{:S(2)}) %collective-permute-start.30) | collective-permute-done | bytes 589856 | tf_op jit(solution)/shard_map/ppermute | solution.py:924
  266.5 8.2 %collective-permute-done.32 = bf16[2,2,96,768]{3,2,0,1:T(8,128)(2,1)S(1)} collective-permute-done((bf16[2,2,96,768]{3,2,0,1:T(8,128)(2,1)S(1)}, bf16[2,2,96,768]{3,2,0,1:T(8,128)(2,1)S(1)}, u32[]{:S(2)}, u32[]{:S(2)}) %collective-permute-start.32) | collective-permute-done | bytes 589856 | tf_op jit(solution)/shard_map/ppermute | solution.py:925
  275.9 4.8 %collective-permute-done.31 = bf16[2,96,768]{2,1,0:T(8,128)(2,1)} collective-permute-done((bf16[2,96,768]{2,1,0:T(8,128)(2,1)S(1)}, bf16[2,96,768]{2,1,0:T(8,128)(2,1)}, u32[]{:S(2)}, u32[]{:S(2)}) %collective-permute-start.31) | collective-permute-done | bytes 294944 | tf_op jit(solution)/shard_map/ppermute | solution.py:927
  280.7 1.2 fusion.14
  281.9 2.2 collective-permute-done.33
  284.1 1.2 fusion.15
  286.8 1.5 copy-done.8
  288.3 1.5 copy-done.9
  289.8 2.9 shard_map.264
  293.7 4.7 %collective-permute-start.24 = (f32[14,768]{1,0:T(8,128)S(1)}, f32[14,768]{1,0:T(8,128)S(1)}, u32[]{:S(2)}, u32[]{:S(2)}) collective-permute-start(f32[14,768]{1,0:T(8,128)S(1)} %pad_maximum_fusion.5), channel_id=1, source_target_pairs={{0,4},{4,0},{1,5},{5,1},{2,6},{6,2},{3,7},{7,3},{8,12},{12,8},{9,1... | collective-permute-start | bytes 129032 | tf_op jit(solution)/shard_map/ppermute | solution.py:973
  299.7 1.8 collective-permute-start.25
  301.5 1.2 pad_maximum_fusion.mine
  302.8 3.1 collective-permute-start.55
  305.9 1.4 collective-permute-start.26
  307.4 1.3 collective-permute-start.38
  308.6 2.7 collective-permute-done.26
  311.4 3.8 %collective-permute-done.39 = bf16[1,96,768]{2,1,0:T(8,128)(2,1)} collective-permute-done((bf16[1,96,768]{2,1,0:T(8,128)(2,1)S(1)}, bf16[1,96,768]{2,1,0:T(8,128)(2,1)}, u32[]{:S(2)}, u32[]{:S(2)}) %collective-permute-start.39) | collective-permute-done | bytes 147488 | tf_op jit(solution)/shard_map/ppermute | solution.py:859
  315.1 1.7 collective-permute-start.29
  316.9 3.1 collective-permute-start.28
  320.3 1.9 pad_maximum_fusion.1.mine
  322.3 3.1 add_convert_fusion
  327.2 3.8 %shard_map.266 = (f32[768,768]{1,0:T(8,128)}, f32[768,768]{1,0:T(8,128)}) custom-call(s32[3]{0:T(128)S(1)} %pad_add_fusion.place, bf16[4,2,96,768]{3,2,1,0:T(8,128)(2,1)S(1)} %pad_maximum_fusion.mine, bf16[4,2,96,768]{3,2,1,0:T(8,128)(2,1)} %collective-permute-done.55.other), custom_call_target="tpu_custom_call" | custom-call | bytes 7077888 | tf_op jit(solution)/shard_map/pallas_call | solution.py:805
  330.9 1.4 shard_map.265
  332.4 1.3 slice.198
  (230 shorter events, 32.7 us)
Async XLA Ops:
  6.2 61.1 %copy-start = (bf16[656,768]{1,0:T(8,128)(2,1)}, bf16[656,768]{1,0:T(8,128)(2,1)S(1)}, u32[]{:S(2)}) copy-start(bf16[656,768]{1,0:T(8,128)(2,1)S(1)} %shard_map.255.normed.counts.normed_mine) | copy-start | bytes 3022852
  6.2 32.5 %collective-permute-start.8 = (bf16[656,768]{1,0:T(8,128)(2,1)S(1)}, bf16[656,768]{1,0:T(8,128)(2,1)S(1)}, u32[]{:S(2)}, u32[]{:S(2)}) collective-permute-start(bf16[656,768]{1,0:T(8,128)(2,1)S(1)} %shard_map.255.normed.counts.normed_mine), channel_id=1, source_target_pairs={{0,4},{4,0},{1,5},{5,1},{2,6},{6,2},{3,7},{7,3},{8,12},{12,8},{9,1... | collective-permute-start | bytes 3022856 | tf_op jit(solution)/shard_map/ppermute | solution.py:877
  7.4 52.3 %copy-start.47 = (bf16[768]{0:T(1024)(128)(2,1)S(1)}, bf16[768]{0:T(1024)(128)(2,1)}, u32[]{:S(2)}) copy-start(bf16[768]{0:T(1024)(128)(2,1)} %param.26) | copy-start | bytes 4612
  7.4 52.3 %copy-start.13 = (bf16[768,768]{1,0:T(8,128)(2,1)S(1)}, bf16[768,768]{1,0:T(8,128)(2,1)}, u32[]{:S(2)}) copy-start(bf16[768,768]{1,0:T(8,128)(2,1)} %up.5) | copy-start | bytes 3538948
  7.4 52.3 %copy-start.14 = (bf16[768,768]{1,0:T(8,128)(2,1)S(1)}, bf16[768,768]{1,0:T(8,128)(2,1)}, u32[]{:S(2)}) copy-start(bf16[768,768]{1,0:T(8,128)(2,1)} %down.5) | copy-start | bytes 3538948
  7.4 13.2 %collective-permute-start = (bf16[208,768]{1,0:T(8,128)(2,1)S(1)}, bf16[208,768]{1,0:T(8,128)(2,1)S(1)}, u32[]{:S(2)}, u32[]{:S(2)}) collective-permute-start(bf16[208,768]{1,0:T(8,128)(2,1)S(1)} %shard_map.254.piece), channel_id=1, source_target_pairs={{0,1},{1,2},{2,3},{3,0},{4,6},{5,7},{6,4},{7,5},{8,9},{9,10},{10,1... | collective-permute-start | bytes 958472 | tf_op jit(solution)/shard_map/ppermute | solution.py:872
  10.1 14.1 %collective-permute-start.4 = (bf16[208,768]{1,0:T(8,128)(2,1)S(1)}, bf16[208,768]{1,0:T(8,128)(2,1)S(1)}, u32[]{:S(2)}, u32[]{:S(2)}) collective-permute-start(bf16[208,768]{1,0:T(8,128)(2,1)S(1)} %shard_map.254.piece), channel_id=1, source_target_pairs={{4,7},{5,4},{6,5},{7,6},{12,15},{13,12},{14,13},{15,14},{20,23},{2... | collective-permute-start | bytes 958472 | tf_op jit(solution)/shard_map/ppermute | solution.py:873
  20.6 46.6 %copy-start.19 = (bf16[208,768]{1,0:T(8,128)(2,1)}, bf16[208,768]{1,0:T(8,128)(2,1)S(1)}, u32[]{:S(2)}) copy-start(bf16[208,768]{1,0:T(8,128)(2,1)S(1)} %collective-permute-done.near0) | copy-start | bytes 958468
  20.6 9.4 %collective-permute-start.1 = (bf16[208,768]{1,0:T(8,128)(2,1)S(1)}, bf16[208,768]{1,0:T(8,128)(2,1)S(1)}, u32[]{:S(2)}, u32[]{:S(2)}) collective-permute-start(bf16[208,768]{1,0:T(8,128)(2,1)S(1)} %collective-permute-done.near0), channel_id=1, source_target_pairs={{0,8},{8,0},{1,9},{9,1},{2,10},{10,2},{3,11},{11,3},{4,12},{12,4},... | collective-permute-start | bytes 958472 | tf_op jit(solution)/shard_map/ppermute | solution.py:857
  22.3 15.7 %collective-permute-start.2 = (bf16[208,768]{1,0:T(8,128)(2,1)S(1)}, bf16[208,768]{1,0:T(8,128)(2,1)S(1)}, u32[]{:S(2)}, u32[]{:S(2)}) collective-permute-start(bf16[208,768]{1,0:T(8,128)(2,1)S(1)} %collective-permute-done.near0), channel_id=1, source_target_pairs={{0,16},{16,0},{1,17},{17,1},{2,18},{18,2},{3,19},{19,3},{4,20},{20... | collective-permute-start | bytes 958472 | tf_op jit(solution)/shard_map/ppermute | solution.py:858
  23.8 14.9 %collective-permute-start.3 = (bf16[208,768]{1,0:T(8,128)(2,1)S(1)}, bf16[208,768]{1,0:T(8,128)(2,1)S(1)}, u32[]{:S(2)}, u32[]{:S(2)}) collective-permute-start(bf16[208,768]{1,0:T(8,128)(2,1)S(1)} %collective-permute-done.near0), channel_id=1, source_target_pairs={{0,24},{8,16},{16,8},{24,0},{1,25},{9,17},{17,9},{25,1},{2,26},{10... | collective-permute-start | bytes 958472 | tf_op jit(solution)/shard_map/ppermute | solution.py:859
  24.1 43.2 %copy-start.21 = (bf16[208,768]{1,0:T(8,128)(2,1)}, bf16[208,768]{1,0:T(8,128)(2,1)S(1)}, u32[]{:S(2)}) copy-start(bf16[208,768]{1,0:T(8,128)(2,1)S(1)} %collective-permute-done.4.far0) | copy-start | bytes 958468
  24.1 14.5 %collective-permute-start.5 = (bf16[208,768]{1,0:T(8,128)(2,1)S(1)}, bf16[208,768]{1,0:T(8,128)(2,1)S(1)}, u32[]{:S(2)}, u32[]{:S(2)}) collective-permute-start(bf16[208,768]{1,0:T(8,128)(2,1)S(1)} %collective-permute-done.4.far0), channel_id=1, source_target_pairs={{4,12},{12,4},{20,28},{28,20},{5,13},{13,5},{21,29},{29,21},{6,14}... | collective-permute-start | bytes 958472 | tf_op jit(solution)/shard_map/ppermute | solution.py:865
  30.0 8.6 %collective-permute-start.6 = (bf16[208,768]{1,0:T(8,128)(2,1)S(1)}, bf16[208,768]{1,0:T(8,128)(2,1)S(1)}, u32[]{:S(2)}, u32[]{:S(2)}) collective-permute-start(bf16[208,768]{1,0:T(8,128)(2,1)S(1)} %collective-permute-done.4.far0), channel_id=1, source_target_pairs={{4,20},{12,28},{20,4},{28,12},{5,21},{13,29},{21,5},{29,13},{6,22}... | collective-permute-start | bytes 958472 | tf_op jit(solution)/shard_map/ppermute | solution.py:866
  38.0 0.7 collective-permute-start.7
  50.4 30.1 %collective-permute-start.9 = (bf16[640,768]{1,0:T(8,128)(2,1)S(1)}, bf16[640,768]{1,0:T(8,128)(2,1)S(1)}, u32[]{:S(2)}, u32[]{:S(2)}) collective-permute-start(bf16[640,768]{1,0:T(8,128)(2,1)S(1)} %get-tuple-element.55), channel_id=1, source_target_pairs={{0,4},{4,0},{1,5},{5,1},{2,6},{6,2},{3,7},{7,3},{8,12},{12,8},{9,1... | collective-permute-start | bytes 2949128 | tf_op jit(solution)/shard_map/ppermute | solution.py:885
  60.4 21.3 %collective-permute-start.16 = (bf16[400,768]{1,0:T(8,128)(2,1)S(1)}, bf16[400,768]{1,0:T(8,128)(2,1)S(1)}, u32[]{:S(2)}, u32[]{:S(2)}) collective-permute-start(bf16[400,768]{1,0:T(8,128)(2,1)S(1)} %shard_map.259.piece), channel_id=1, source_target_pairs={{0,1},{1,2},{2,3},{3,0},{4,6},{5,7},{6,4},{7,5},{8,9},{9,10},{10,1... | collective-permute-start | bytes 1843208 | tf_op jit(solution)/shard_map/ppermute | solution.py:879
  63.4 21.2 %collective-permute-start.10 = (bf16[400,768]{1,0:T(8,128)(2,1)S(1)}, bf16[400,768]{1,0:T(8,128)(2,1)S(1)}, u32[]{:S(2)}, u32[]{:S(2)}) collective-permute-start(bf16[400,768]{1,0:T(8,128)(2,1)S(1)} %shard_map.259.piece), channel_id=1, source_target_pairs={{4,7},{5,4},{6,5},{7,6},{12,15},{13,12},{14,13},{15,14},{20,23},{2... | collective-permute-start | bytes 1843208 | tf_op jit(solution)/shard_map/ppermute | solution.py:880
  64.1 22.0 %collective-permute-start.15 = (bf16[640,768]{1,0:T(8,128)(2,1)S(1)}, bf16[640,768]{1,0:T(8,128)(2,1)S(1)}, u32[]{:S(2)}, u32[]{:S(2)}) collective-permute-start(bf16[640,768]{1,0:T(8,128)(2,1)S(1)} %copy-done.15), channel_id=1, source_target_pairs={{0,4},{4,0},{1,5},{5,1},{2,6},{6,2},{3,7},{7,3},{8,12},{12,8},{9,1... | collective-permute-start | bytes 2949128 | tf_op jit(solution)/shard_map/ppermute | solution.py:881
  81.7 109.9 %copy-start.3 = (f32[640,768]{1,0:T(8,128)}, f32[640,768]{1,0:T(8,128)S(1)}, u32[]{:S(2)}) copy-start(f32[640,768]{1,0:T(8,128)S(1)} %get-tuple-element.56.first_sum) | copy-start | bytes 5898244
  81.7 33.0 %collective-permute-start.14 = (bf16[640,768]{1,0:T(8,128)(2,1)S(1)}, bf16[640,768]{1,0:T(8,128)(2,1)S(1)}, u32[]{:S(2)}, u32[]{:S(2)}) collective-permute-start(bf16[640,768]{1,0:T(8,128)(2,1)S(1)} %get-tuple-element.57.normed_mine), channel_id=1, source_target_pairs={{0,4},{4,0},{1,5},{5,1},{2,6},{6,2},{3,7},{7,3},{8,12},{12,8},{9,1... | collective-permute-start | bytes 2949128 | tf_op jit(solution)/shard_map/ppermute | solution.py:897
  81.8 16.1 %collective-permute-start.17 = (bf16[400,768]{1,0:T(8,128)(2,1)S(1)}, bf16[400,768]{1,0:T(8,128)(2,1)S(1)}, u32[]{:S(2)}, u32[]{:S(2)}) collective-permute-start(bf16[400,768]{1,0:T(8,128)(2,1)S(1)} %collective-permute-done.16.piece0), channel_id=1, source_target_pairs={{0,8},{8,0},{1,9},{9,1},{2,10},{10,2},{3,11},{11,3},{4,12},{12,4},... | collective-permute-start | bytes 1843208 | tf_op jit(solution)/shard_map/ppermute | solution.py:857
  83.4 28.7 %collective-permute-start.18 = (bf16[400,768]{1,0:T(8,128)(2,1)S(1)}, bf16[400,768]{1,0:T(8,128)(2,1)S(1)}, u32[]{:S(2)}, u32[]{:S(2)}) collective-permute-start(bf16[400,768]{1,0:T(8,128)(2,1)S(1)} %collective-permute-done.16.piece0), channel_id=1, source_target_pairs={{0,16},{16,0},{1,17},{17,1},{2,18},{18,2},{3,19},{19,3},{4,20},{20... | collective-permute-start | bytes 1843208 | tf_op jit(solution)/shard_map/ppermute | solution.py:858
  84.6 49.9 %copy-start.50 = (bf16[400,768]{1,0:T(8,128)(2,1)}, bf16[400,768]{1,0:T(8,128)(2,1)S(1)}, u32[]{:S(2)}) copy-start(bf16[400,768]{1,0:T(8,128)(2,1)S(1)} %collective-permute-done.10.piece0) | copy-start | bytes 1843204
  84.6 29.2 %collective-permute-start.19 = (bf16[400,768]{1,0:T(8,128)(2,1)S(1)}, bf16[400,768]{1,0:T(8,128)(2,1)S(1)}, u32[]{:S(2)}, u32[]{:S(2)}) collective-permute-start(bf16[400,768]{1,0:T(8,128)(2,1)S(1)} %collective-permute-done.16.piece0), channel_id=1, source_target_pairs={{0,24},{8,16},{16,8},{24,0},{1,25},{9,17},{17,9},{25,1},{2,26},{10... | collective-permute-start | bytes 1843208 | tf_op jit(solution)/shard_map/ppermute | solution.py:859
  86.1 52.7 %collective-permute-start.11 = (bf16[400,768]{1,0:T(8,128)(2,1)S(1)}, bf16[400,768]{1,0:T(8,128)(2,1)S(1)}, u32[]{:S(2)}, u32[]{:S(2)}) collective-permute-start(bf16[400,768]{1,0:T(8,128)(2,1)S(1)} %collective-permute-done.10.piece0), channel_id=1, source_target_pairs={{4,12},{12,4},{20,28},{28,20},{5,13},{13,5},{21,29},{29,21},{6,14}... | collective-permute-start | bytes 1843208 | tf_op jit(solution)/shard_map/ppermute | solution.py:865
  97.8 41.0 %collective-permute-start.12 = (bf16[400,768]{1,0:T(8,128)(2,1)S(1)}, bf16[400,768]{1,0:T(8,128)(2,1)}, u32[]{:S(2)}, u32[]{:S(2)}) collective-permute-start(bf16[400,768]{1,0:T(8,128)(2,1)S(1)} %collective-permute-done.10.piece0), channel_id=1, source_target_pairs={{4,20},{12,28},{20,4},{28,12},{5,21},{13,29},{21,5},{29,13},{6,22}... | collective-permute-start | bytes 1843208 | tf_op jit(solution)/shard_map/ppermute | solution.py:866
  112.1 26.8 %collective-permute-start.13 = (bf16[400,768]{1,0:T(8,128)(2,1)S(1)}, bf16[400,768]{1,0:T(8,128)(2,1)}, u32[]{:S(2)}, u32[]{:S(2)}) collective-permute-start(bf16[400,768]{1,0:T(8,128)(2,1)S(1)} %collective-permute-done.10.piece0), channel_id=1, source_target_pairs={{4,28},{12,20},{20,12},{28,4},{5,29},{13,21},{21,13},{29,5},{6,30}... | collective-permute-start | bytes 1843208 | tf_op jit(solution)/shard_map/ppermute | solution.py:867
  134.6 27.6 %collective-permute-start.48 = (bf16[2,2,96,768]{3,2,0,1:T(8,128)(2,1)S(1)}, bf16[2,2,96,768]{3,2,0,1:T(8,128)(2,1)S(1)}, u32[]{:S(2)}, u32[]{:S(2)}) collective-permute-start(bf16[2,2,96,768]{3,2,0,1:T(8,128)(2,1)S(1)} %copy.47), channel_id=1, source_target_pairs={{0,16},{16,0},{1,17},{17,1},{2,18},{18,2},{3,19},{19,3},{4,20},{20... | collective-permute-start | bytes 1769480 | tf_op jit(solution)/shard_map/ppermute | solution.py:925
  136.9 26.4 %collective-permute-start.46 = (bf16[2,2,96,768]{3,2,0,1:T(8,128)(2,1)S(1)}, bf16[2,2,96,768]{3,2,0,1:T(8,128)(2,1)S(1)}, u32[]{:S(2)}, u32[]{:S(2)}) collective-permute-start(bf16[2,2,96,768]{3,2,0,1:T(8,128)(2,1)S(1)} %copy.44), channel_id=1, source_target_pairs={{0,8},{8,0},{1,9},{9,1},{2,10},{10,2},{3,11},{11,3},{4,12},{12,4},... | collective-permute-start | bytes 1769480 | tf_op jit(solution)/shard_map/ppermute | solution.py:924
  160.3 16.3 %collective-permute-start.43 = (bf16[2,2,96,768]{3,2,0,1:T(8,128)(2,1)S(1)}, bf16[2,2,96,768]{3,2,0,1:T(8,128)(2,1)S(1)}, u32[]{:S(2)}, u32[]{:S(2)}) collective-permute-start(bf16[2,2,96,768]{3,2,0,1:T(8,128)(2,1)S(1)} %copy.41), channel_id=1, source_target_pairs={{0,16},{16,0},{1,17},{17,1},{2,18},{18,2},{3,19},{19,3},{4,20},{20... | collective-permute-start | bytes 1769480 | tf_op jit(solution)/shard_map/ppermute | solution.py:925
  160.4 31.2 %collective-permute-start.21 = (bf16[640,768]{1,0:T(8,128)(2,1)}, bf16[640,768]{1,0:T(8,128)(2,1)S(1)}, u32[]{:S(2)}, u32[]{:S(2)}) collective-permute-start(bf16[640,768]{1,0:T(8,128)(2,1)} %get-tuple-element.63), channel_id=1, source_target_pairs={{0,4},{4,0},{1,5},{5,1},{2,6},{6,2},{3,7},{7,3},{8,12},{12,8},{9,1... | collective-permute-start | bytes 2949128 | tf_op jit(solution)/shard_map/ppermute | solution.py:907
  161.0 16.3 %collective-permute-start.41 = (bf16[2,2,96,768]{3,2,0,1:T(8,128)(2,1)S(1)}, bf16[2,2,96,768]{3,2,0,1:T(8,128)(2,1)S(1)}, u32[]{:S(2)}, u32[]{:S(2)}) collective-permute-start(bf16[2,2,96,768]{3,2,0,1:T(8,128)(2,1)S(1)} %copy.38), channel_id=1, source_target_pairs={{0,8},{8,0},{1,9},{9,1},{2,10},{10,2},{3,11},{11,3},{4,12},{12,4},... | collective-permute-start | bytes 1769480 | tf_op jit(solution)/shard_map/ppermute | solution.py:924
  162.2 21.4 %collective-permute-start.49 = (bf16[2,96,768]{2,1,0:T(8,128)(2,1)S(1)}, bf16[2,96,768]{2,1,0:T(8,128)(2,1)S(1)}, u32[]{:S(2)}, u32[]{:S(2)}) collective-permute-start(bf16[2,96,768]{2,1,0:T(8,128)(2,1)S(1)} %fusion.12), channel_id=1, source_target_pairs={{0,8},{8,0},{1,9},{9,1},{2,10},{10,2},{3,11},{11,3},{4,12},{12,4},... | collective-permute-start | bytes 884744 | tf_op jit(solution)/shard_map/ppermute | solution.py:928
  163.3 20.4 %collective-permute-start.47 = (bf16[2,96,768]{2,1,0:T(8,128)(2,1)S(1)}, bf16[2,96,768]{2,1,0:T(8,128)(2,1)S(1)}, u32[]{:S(2)}, u32[]{:S(2)}) collective-permute-start(bf16[2,96,768]{2,1,0:T(8,128)(2,1)S(1)} %fusion.11), channel_id=1, source_target_pairs={{0,16},{16,0},{1,17},{17,1},{2,18},{18,2},{3,19},{19,3},{4,20},{20... | collective-permute-start | bytes 884744 | tf_op jit(solution)/shard_map/ppermute | solution.py:927
  176.7 12.2 %collective-permute-start.44 = (bf16[2,96,768]{2,1,0:T(8,128)(2,1)S(1)}, bf16[2,96,768]{2,1,0:T(8,128)(2,1)S(1)}, u32[]{:S(2)}, u32[]{:S(2)}) collective-permute-start(bf16[2,96,768]{2,1,0:T(8,128)(2,1)S(1)} %fusion.10), channel_id=1, source_target_pairs={{0,8},{8,0},{1,9},{9,1},{2,10},{10,2},{3,11},{11,3},{4,12},{12,4},... | collective-permute-start | bytes 884744 | tf_op jit(solution)/shard_map/ppermute | solution.py:928
  177.4 11.7 %collective-permute-start.42 = (bf16[2,96,768]{2,1,0:T(8,128)(2,1)S(1)}, bf16[2,96,768]{2,1,0:T(8,128)(2,1)S(1)}, u32[]{:S(2)}, u32[]{:S(2)}) collective-permute-start(bf16[2,96,768]{2,1,0:T(8,128)(2,1)S(1)} %fusion.9), channel_id=1, source_target_pairs={{0,16},{16,0},{1,17},{17,1},{2,18},{18,2},{3,19},{19,3},{4,20},{20... | collective-permute-start | bytes 884744 | tf_op jit(solution)/shard_map/ppermute | solution.py:927
  184.7 16.9 %collective-permute-start.50 = (bf16[2,2,96,768]{3,2,1,0:T(8,128)(2,1)}, bf16[2,2,96,768]{3,2,1,0:T(8,128)(2,1)}, u32[]{:S(2)}, u32[]{:S(2)}) collective-permute-start(bf16[2,2,96,768]{3,2,1,0:T(8,128)(2,1)} %pad_maximum_fusion.3), channel_id=1, source_target_pairs={{1,0},{2,1},{3,2},{0,3},{6,4},{7,5},{4,6},{5,7},{9,8},{10,9},{11,1... | collective-permute-start | bytes 1769480 | tf_op jit(solution)/shard_map/ppermute | solution.py:950
  190.1 11.5 %collective-permute-start.45 = (bf16[2,2,96,768]{3,2,1,0:T(8,128)(2,1)}, bf16[2,2,96,768]{3,2,1,0:T(8,128)(2,1)}, u32[]{:S(2)}, u32[]{:S(2)}) collective-permute-start(bf16[2,2,96,768]{3,2,1,0:T(8,128)(2,1)} %pad_maximum_fusion.2), channel_id=1, source_target_pairs={{7,4},{4,5},{5,6},{6,7},{15,12},{12,13},{13,14},{14,15},{23,20},{2... | collective-permute-start | bytes 1769480 | tf_op jit(solution)/shard_map/ppermute | solution.py:951
  195.8 19.9 %collective-permute-start.22 = (bf16[640,768]{1,0:T(8,128)(2,1)}, bf16[640,768]{1,0:T(8,128)(2,1)}, u32[]{:S(2)}, u32[]{:S(2)}) collective-permute-start(bf16[640,768]{1,0:T(8,128)(2,1)} %get-tuple-element.64.grad_mine), channel_id=1, source_target_pairs={{0,4},{4,0},{1,5},{5,1},{2,6},{6,2},{3,7},{7,3},{8,12},{12,8},{9,1... | collective-permute-start | bytes 2949128 | tf_op jit(solution)/shard_map/ppermute | solution.py:914
  203.0 49.3 %collective-permute-start.51 = (bf16[2,96,768]{2,1,0:T(8,128)(2,1)S(1)}, bf16[2,96,768]{2,1,0:T(8,128)(2,1)S(1)}, u32[]{:S(2)}, u32[]{:S(2)}) collective-permute-start(bf16[2,96,768]{2,1,0:T(8,128)(2,1)S(1)} %fusion.13), channel_id=1, source_target_pairs={{0,4},{4,0},{1,5},{5,1},{2,6},{6,2},{3,7},{7,3},{8,12},{12,8},{9,1... | collective-permute-start | bytes 884744 | tf_op jit(solution)/shard_map/ppermute | solution.py:939
  249.7 16.6 %collective-permute-start.30 = (bf16[2,2,96,768]{3,2,0,1:T(8,128)(2,1)S(1)}, bf16[2,2,96,768]{3,2,0,1:T(8,128)(2,1)S(1)}, u32[]{:S(2)}, u32[]{:S(2)}) collective-permute-start(bf16[2,2,96,768]{3,2,0,1:T(8,128)(2,1)S(1)} %copy.32), channel_id=1, source_target_pairs={{0,8},{8,0},{1,9},{9,1},{2,10},{10,2},{3,11},{11,3},{4,12},{12,4},... | collective-permute-start | bytes 1769480 | tf_op jit(solution)/shard_map/ppermute | solution.py:924
  252.1 70.2 %collective-permute-start.20 = (bf16[640,768]{1,0:T(8,128)(2,1)}, bf16[640,768]{1,0:T(8,128)(2,1)}, u32[]{:S(2)}, u32[]{:S(2)}) collective-permute-start(bf16[640,768]{1,0:T(8,128)(2,1)} %get-tuple-element.61), channel_id=1, source_target_pairs={{0,4},{4,0},{1,5},{5,1},{2,6},{6,2},{3,7},{7,3},{8,12},{12,8},{9,1... | collective-permute-start | bytes 2949128 | tf_op jit(solution)/shard_map/ppermute | solution.py:911
  252.1 22.5 %collective-permute-start.32 = (bf16[2,2,96,768]{3,2,0,1:T(8,128)(2,1)S(1)}, bf16[2,2,96,768]{3,2,0,1:T(8,128)(2,1)S(1)}, u32[]{:S(2)}, u32[]{:S(2)}) collective-permute-start(bf16[2,2,96,768]{3,2,0,1:T(8,128)(2,1)S(1)} %copy.35), channel_id=1, source_target_pairs={{0,16},{16,0},{1,17},{17,1},{2,18},{18,2},{3,19},{19,3},{4,20},{20... | collective-permute-start | bytes 1769480 | tf_op jit(solution)/shard_map/ppermute | solution.py:925
  252.4 47.3 %collective-permute-start.54 = (bf16[2,96,768]{2,1,0:T(8,128)(2,1)S(1)}, bf16[2,96,768]{2,1,0:T(8,128)(2,1)}, u32[]{:S(2)}, u32[]{:S(2)}) collective-permute-start(bf16[2,96,768]{2,1,0:T(8,128)(2,1)S(1)} %fusion), channel_id=1, source_target_pairs={{0,24},{8,16},{16,8},{24,0},{1,25},{9,17},{17,9},{25,1},{2,26},{10... | collective-permute-start | bytes 884744 | tf_op jit(solution)/shard_map/ppermute | solution.py:859
  254.0 32.2 %collective-permute-start.23 = (bf16[640,768]{1,0:T(8,128)(2,1)}, bf16[640,768]{1,0:T(8,128)(2,1)S(1)}, u32[]{:S(2)}, u32[]{:S(2)}) collective-permute-start(bf16[640,768]{1,0:T(8,128)(2,1)} %get-tuple-element.68), channel_id=1, source_target_pairs={{0,4},{4,0},{1,5},{5,1},{2,6},{6,2},{3,7},{7,3},{8,12},{12,8},{9,1... | collective-permute-start | bytes 2949128 | tf_op jit(solution)/shard_map/ppermute | solution.py:918
  266.4 14.3 %collective-permute-start.31 = (bf16[2,96,768]{2,1,0:T(8,128)(2,1)S(1)}, bf16[2,96,768]{2,1,0:T(8,128)(2,1)}, u32[]{:S(2)}, u32[]{:S(2)}) collective-permute-start(bf16[2,96,768]{2,1,0:T(8,128)(2,1)S(1)} %fusion.7), channel_id=1, source_target_pairs={{0,16},{16,0},{1,17},{17,1},{2,18},{18,2},{3,19},{19,3},{4,20},{20... | collective-permute-start | bytes 884744 | tf_op jit(solution)/shard_map/ppermute | solution.py:927
  275.6 8.6 %collective-permute-start.33 = (bf16[2,96,768]{2,1,0:T(8,128)(2,1)}, bf16[2,96,768]{2,1,0:T(8,128)(2,1)}, u32[]{:S(2)}, u32[]{:S(2)}) collective-permute-start(bf16[2,96,768]{2,1,0:T(8,128)(2,1)} %fusion.8), channel_id=1, source_target_pairs={{0,8},{8,0},{1,9},{9,1},{2,10},{10,2},{3,11},{11,3},{4,12},{12,4},... | collective-permute-start | bytes 884744 | tf_op jit(solution)/shard_map/ppermute | solution.py:928
  285.4 8.0 %collective-permute-start.35 = (bf16[2,1,96,768]{3,2,1,0:T(8,128)(2,1)S(1)}, bf16[2,1,96,768]{3,2,1,0:T(8,128)(2,1)S(1)}, u32[]{:S(2)}, u32[]{:S(2)}) collective-permute-start(bf16[2,1,96,768]{3,2,1,0:T(8,128)(2,1)S(1)} %get-tuple-element.98), channel_id=1, source_target_pairs={{1,0},{2,1},{3,2},{0,3},{6,4},{7,5},{4,6},{5,7},{9,8},{10,9},{11,1... | collective-permute-start | bytes 884744 | tf_op jit(solution)/shard_map/ppermute | solution.py:956
  285.4 8.3 %collective-permute-start.34 = (bf16[2,1,96,768]{3,2,1,0:T(8,128)(2,1)S(1)}, bf16[2,1,96,768]{3,2,1,0:T(8,128)(2,1)S(1)}, u32[]{:S(2)}, u32[]{:S(2)}) collective-permute-start(bf16[2,1,96,768]{3,2,1,0:T(8,128)(2,1)S(1)} %get-tuple-element.97), channel_id=1, source_target_pairs={{7,4},{4,5},{5,6},{6,7},{15,12},{12,13},{13,14},{14,15},{23,20},{2... | collective-permute-start | bytes 884744 | tf_op jit(solution)/shard_map/ppermute | solution.py:957
  286.2 15.3 %collective-permute-start.53 = (bf16[2,96,768]{2,1,0:T(8,128)(2,1)S(1)}, bf16[2,96,768]{2,1,0:T(8,128)(2,1)S(1)}, u32[]{:S(2)}, u32[]{:S(2)}) collective-permute-start(bf16[2,96,768]{2,1,0:T(8,128)(2,1)S(1)} %fusion), channel_id=1, source_target_pairs={{0,16},{16,0},{1,17},{17,1},{2,18},{18,2},{3,19},{19,3},{4,20},{20... | collective-permute-start | bytes 884744 | tf_op jit(solution)/shard_map/ppermute | solution.py:858
  293.3 8.2 %collective-permute-start.52 = (bf16[2,96,768]{2,1,0:T(8,128)(2,1)S(1)}, bf16[2,96,768]{2,1,0:T(8,128)(2,1)S(1)}, u32[]{:S(2)}, u32[]{:S(2)}) collective-permute-start(bf16[2,96,768]{2,1,0:T(8,128)(2,1)S(1)} %fusion), channel_id=1, source_target_pairs={{0,8},{8,0},{1,9},{9,1},{2,10},{10,2},{3,11},{11,3},{4,12},{12,4},... | collective-permute-start | bytes 884744 | tf_op jit(solution)/shard_map/ppermute | solution.py:857
  293.7 5.6 %collective-permute-start.24 = (f32[14,768]{1,0:T(8,128)S(1)}, f32[14,768]{1,0:T(8,128)S(1)}, u32[]{:S(2)}, u32[]{:S(2)}) collective-permute-start(f32[14,768]{1,0:T(8,128)S(1)} %pad_maximum_fusion.5), channel_id=1, source_target_pairs={{0,4},{4,0},{1,5},{5,1},{2,6},{6,2},{3,7},{7,3},{8,12},{12,8},{9,1... | collective-permute-start | bytes 129032 | tf_op jit(solution)/shard_map/ppermute | solution.py:973
  299.3 8.0 %collective-permute-start.36 = (bf16[1,96,768]{2,1,0:T(8,128)(2,1)S(1)}, bf16[1,96,768]{2,1,0:T(8,128)(2,1)S(1)}, u32[]{:S(2)}, u32[]{:S(2)}) collective-permute-start(bf16[1,96,768]{2,1,0:T(8,128)(2,1)S(1)} %fusion.22), channel_id=1, source_target_pairs={{0,4},{4,0},{1,5},{5,1},{2,6},{6,2},{3,7},{7,3},{8,12},{12,8},{9,1... | collective-permute-start | bytes 442376 | tf_op jit(solution)/shard_map/ppermute | solution.py:939
  299.7 6.2 %collective-permute-start.25 = (f32[14,768]{1,0:T(8,128)S(1)}, f32[14,768]{1,0:T(8,128)S(1)}, u32[]{:S(2)}, u32[]{:S(2)}) collective-permute-start(f32[14,768]{1,0:T(8,128)S(1)} %fusion.23), channel_id=1, source_target_pairs={{0,8},{8,0},{1,9},{9,1},{2,10},{10,2},{3,11},{11,3},{4,12},{12,4},... | collective-permute-start | bytes 129032 | tf_op jit(solution)/shard_map/ppermute | solution.py:973
  302.8 24.4 %collective-permute-start.55 = (bf16[4,2,96,768]{3,2,1,0:T(8,128)(2,1)S(1)}, bf16[4,2,96,768]{3,2,1,0:T(8,128)(2,1)}, u32[]{:S(2)}, u32[]{:S(2)}) collective-permute-start(bf16[4,2,96,768]{3,2,1,0:T(8,128)(2,1)S(1)} %pad_maximum_fusion.mine), channel_id=1, source_target_pairs={{0,4},{4,0},{1,5},{5,1},{2,6},{6,2},{3,7},{7,3},{8,12},{12,8},{9,1... | collective-permute-start | bytes 3538952 | tf_op jit(solution)/shard_map/ppermute | solution.py:946
  305.9 5.5 %collective-permute-start.26 = (f32[14,768]{1,0:T(8,128)S(1)}, f32[14,768]{1,0:T(8,128)S(1)}, u32[]{:S(2)}, u32[]{:S(2)}) collective-permute-start(f32[14,768]{1,0:T(8,128)S(1)} %add.165), channel_id=1, source_target_pairs={{0,16},{16,0},{1,17},{17,1},{2,18},{18,2},{3,19},{19,3},{4,20},{20... | collective-permute-start | bytes 129032 | tf_op jit(solution)/shard_map/ppermute | solution.py:973
  307.3 7.8 %collective-permute-start.39 = (bf16[1,96,768]{2,1,0:T(8,128)(2,1)S(1)}, bf16[1,96,768]{2,1,0:T(8,128)(2,1)}, u32[]{:S(2)}, u32[]{:S(2)}) collective-permute-start(bf16[1,96,768]{2,1,0:T(8,128)(2,1)S(1)} %fusion.21), channel_id=1, source_target_pairs={{0,24},{8,16},{16,8},{24,0},{1,25},{9,17},{17,9},{25,1},{2,26},{10... | collective-permute-start | bytes 442376 | tf_op jit(solution)/shard_map/ppermute | solution.py:859
  307.4 9.5 %collective-permute-start.38 = (bf16[1,96,768]{2,1,0:T(8,128)(2,1)S(1)}, bf16[1,96,768]{2,1,0:T(8,128)(2,1)}, u32[]{:S(2)}, u32[]{:S(2)}) collective-permute-start(bf16[1,96,768]{2,1,0:T(8,128)(2,1)S(1)} %fusion.21), channel_id=1, source_target_pairs={{0,16},{16,0},{1,17},{17,1},{2,18},{18,2},{3,19},{19,3},{4,20},{20... | collective-permute-start | bytes 442376 | tf_op jit(solution)/shard_map/ppermute | solution.py:858
  311.3 8.6 %collective-permute-start.37 = (bf16[1,96,768]{2,1,0:T(8,128)(2,1)S(1)}, bf16[1,96,768]{2,1,0:T(8,128)(2,1)}, u32[]{:S(2)}, u32[]{:S(2)}) collective-permute-start(bf16[1,96,768]{2,1,0:T(8,128)(2,1)S(1)} %fusion.21), channel_id=1, source_target_pairs={{0,8},{8,0},{1,9},{9,1},{2,10},{10,2},{3,11},{11,3},{4,12},{12,4},... | collective-permute-start | bytes 442376 | tf_op jit(solution)/shard_map/ppermute | solution.py:857
  315.1 10.2 %collective-permute-start.29 = (f32[14,768]{1,0:T(8,128)S(1)}, f32[14,768]{1,0:T(8,128)S(1)}, u32[]{:S(2)}, u32[]{:S(2)}) collective-permute-start(f32[14,768]{1,0:T(8,128)S(1)} %add.166), channel_id=1, source_target_pairs={{0,3},{1,0},{2,1},{3,2},{4,7},{5,4},{6,5},{7,6},{8,11},{9,8},{10,9... | collective-permute-start | bytes 129032 | tf_op jit(solution)/shard_map/ppermute | solution.py:975
  316.9 8.5 %collective-permute-start.28 = (f32[14,768]{1,0:T(8,128)S(1)}, f32[14,768]{1,0:T(8,128)S(1)}, u32[]{:S(2)}, u32[]{:S(2)}) collective-permute-start(f32[14,768]{1,0:T(8,128)S(1)} %add.166), channel_id=1, source_target_pairs={{0,2},{1,3},{2,0},{3,1},{4,6},{5,7},{6,4},{7,5},{8,10},{9,11},{10,... | collective-permute-start | bytes 129032 | tf_op jit(solution)/shard_map/ppermute | solution.py:975
  319.9 5.9 %collective-permute-start.27 = (f32[14,768]{1,0:T(8,128)S(1)}, f32[14,768]{1,0:T(8,128)S(1)}, u32[]{:S(2)}, u32[]{:S(2)}) collective-permute-start(f32[14,768]{1,0:T(8,128)S(1)} %add.166), channel_id=1, source_target_pairs={{0,1},{1,2},{2,3},{3,0},{4,5},{5,6},{6,7},{7,4},{8,9},{9,10},{10,1... | collective-permute-start | bytes 129032 | tf_op jit(solution)/shard_map/ppermute | solution.py:975
  322.3 8.7 %collective-permute-start.40 = (bf16[4,1,96,768]{3,2,1,0:T(8,128)(2,1)}, bf16[4,1,96,768]{3,2,1,0:T(8,128)(2,1)}, u32[]{:S(2)}, u32[]{:S(2)}) collective-permute-start(bf16[4,1,96,768]{3,2,1,0:T(8,128)(2,1)} %pad_maximum_fusion.1.mine), channel_id=1, source_target_pairs={{0,4},{4,0},{1,5},{5,1},{2,6},{6,2},{3,7},{7,3},{8,12},{12,8},{9,1... | collective-permute-start | bytes 1769480 | tf_op jit(solution)/shard_map/ppermute | solution.py:946
  (48 other events, 580.0 us)

commit v2 on v1

v2 whole, which is shorter than its diff:
```python
import functools

import jax
import jax.numpy as jnp
import numpy as np
from jax import lax
from jax.experimental import pallas as pl
from jax.experimental.pallas import tpu as pltpu
from jax.sharding import PartitionSpec as P

HD = 64
SLOTS = 80
LANES = 128
TILE_IMAGES = 4
MASKED = -1000000000.0
EPS = 1e-06
F32 = jnp.float32
BF16 = jnp.bfloat16

ANY = pl.BlockSpec(memory_space=pl.ANY)
SMEM = pl.BlockSpec(memory_space=pltpu.SMEM)
VMEM = pl.BlockSpec(memory_space=pltpu.VMEM)


def shape(dims, kind):
    return jax.ShapeDtypeStruct(tuple(dims), kind)


def kept(dims, kind):
    return pltpu.HBM(tuple(dims), kind)


def from_hbm(*arrays):
    return tuple(pltpu.with_memory_space_constraint(a, pltpu.HBM) for a in arrays)


def params(megabytes, grid_dims=0):
    semantics = ("arbitrary",) * grid_dims if grid_dims else None
    return pltpu.CompilerParams(
        vmem_limit_bytes=megabytes * 1024 * 1024, dimension_semantics=semantics
    )


def cost(flops, moved):
    return pl.CostEstimate(flops=int(flops), bytes_accessed=int(moved), transcendentals=0)


def dot(left, right):
    return lax.dot_general(left, right, (((1,), (0,)), ((), ())), preferred_element_type=F32)


def dot_rows(left, right):
    return lax.dot_general(left, right, (((1,), (1,)), ((), ())), preferred_element_type=F32)


def dot_columns(left, right):
    return lax.dot_general(left, right, (((0,), (0,)), ((), ())), preferred_element_type=F32)


def centred(rows):
    center = rows - jnp.mean(rows, axis=-1, keepdims=True)
    spread = jnp.mean(center * center, axis=-1, keepdims=True)
    return center, lax.rsqrt(spread + EPS)


def norm_back(rows, gain, grad):
    center, rstd = centred(rows)
    xhat = center * rstd
    e = grad * gain
    back = rstd * (
        e - jnp.mean(e, axis=-1, keepdims=True) - xhat * jnp.mean(e * xhat, axis=-1, keepdims=True)
    )
    return (
        back,
        jnp.sum(grad * xhat, axis=0, keepdims=True),
        jnp.sum(grad, axis=0, keepdims=True),
    )


def norm_one_kernel(images, chunk, place, counts, tokens, gain, shift, out):
    rows = tokens.shape[0]

    @pl.loop(0, rows // chunk)
    def _(step):
        at = pl.ds(pl.multiple_of(step * chunk, chunk), chunk)
        center, rstd = centred(tokens[at, :].astype(F32))
        out[at, :] = (center * rstd * gain[...] + shift[...]).astype(BF16)

    extra = out.shape[0] - rows
    row = lax.broadcasted_iota(jnp.int32, (extra, out.shape[1]), 0)
    table = jnp.zeros((extra, out.shape[1]), F32)
    first = place[2] * images
    for image in range(images):
        table = jnp.where(row == image, counts[first + image].astype(F32), table)
    out[rows:, :] = table.astype(BF16)


def norm_one(place, counts, tokens, gain, shift):
    rows, width = tokens.shape
    images = rows // SLOTS
    return pl.pallas_call(
        functools.partial(norm_one_kernel, images, SLOTS),
        out_shape=shape((rows + 16, width), BF16),
        in_specs=[SMEM, SMEM, VMEM, VMEM, VMEM],
        out_specs=VMEM,
        compiler_params=params(16),
        cost_estimate=cost(rows * width * 10, rows * width * 4),
    )(place, counts, tokens, gain, shift)


def norm_two_kernel(tokens, mine, received, bias, gain, shift, first_sum, normed):
    total = tokens[...].astype(F32) + (mine[...] + received[...].astype(F32)) + bias[...]
    first_sum[...] = total
    center, rstd = centred(total)
    normed[...] = (center * rstd * gain[...] + shift[...]).astype(BF16)


def rows_spec(tile, width):
    return pl.BlockSpec((tile, width), lambda i: (i, 0))


def fixed_spec(*dims):
    return pl.BlockSpec(dims, lambda i: (0,) * len(dims))


def norm_two(tokens, mine, received, bias, gain, shift):
    rows, width = tokens.shape
    tile = 2 * SLOTS
    row = rows_spec(tile, width)
    vector = fixed_spec(1, width)
    return pl.pallas_call(
        norm_two_kernel,
        grid=(rows // tile,),
        out_shape=(kept((rows, width), F32), shape((rows, width), BF16)),
        in_specs=[row, row, row, vector, vector, vector],
        out_specs=(row, row),
        compiler_params=params(16, 1),
        cost_estimate=cost(rows * width * 12, rows * width * 14),
    )(*from_hbm(tokens), mine, received, bias, gain, shift)


def norm_two_back_kernel(mine, received, first_sum, gain, output_grad, grad_first, low, sums):
    grad = mine[...] + received[...].astype(F32)
    back, grad_gain, grad_shift = norm_back(first_sum[...], gain[...], grad)
    out_grad = output_grad[...].astype(F32)
    total = out_grad + back
    grad_first[...] = total
    low[...] = total.astype(BF16)

    @pl.when(pl.program_id(0) == 0)
    def _():
        sums[...] = jnp.zeros_like(sums)

    sums[0:1, :] += grad_gain
    sums[1:2, :] += grad_shift
    sums[2:3, :] += jnp.sum(total, axis=0, keepdims=True)
    sums[3:4, :] += jnp.sum(out_grad, axis=0, keepdims=True)


def norm_two_back(mine, received, first_sum, gain, output_grad):
    rows, width = mine.shape
    tile = 2 * SLOTS
    row = rows_spec(tile, width)
    return pl.pallas_call(
        norm_two_back_kernel,
        grid=(rows // tile,),
        out_shape=(kept((rows, width), F32), shape((rows, width), BF16), shape((8, width), F32)),
        in_specs=[row, row, row, fixed_spec(1, width), row],
        out_specs=(row, row, fixed_spec(8, width)),
        compiler_params=params(16, 1),
        cost_estimate=cost(rows * width * 25, rows * width * 18),
    )(mine, received, *from_hbm(first_sum), gain, *from_hbm(output_grad))


def norm_one_back_kernel(
    groups,
    place,
    mine,
    received,
    tokens,
    gain,
    grad_first,
    sums_two,
    bias_near,
    bias_far,
    input_near,
    input_far,
    grad_tokens,
    vectors,
):
    grad = mine[...] + received[...].astype(F32)
    back, grad_gain, grad_shift = norm_back(tokens[...].astype(F32), gain[...], grad)
    grad_tokens[...] = grad_first[...] + back

    @pl.when(pl.program_id(0) == 0)
    def _():
        near = lax.rem(place[2] - 1 - place[1] + groups, groups)
        far = lax.rem(place[2] - 3 * place[1] + groups, groups)
        row = lax.broadcasted_iota(jnp.int32, vectors.shape, 0)
        table = jnp.zeros(vectors.shape, F32)
        for index in range(4):
            table = jnp.where(row == 2 + index, sums_two[index : index + 1, :], table)
        table = jnp.where(row == 6 + near, bias_near[0:1, :], table)
        vectors[...] = jnp.where(row == 6 + far, bias_far[0:1, :], table)
        columns = input_near.shape[1]
        few = lax.broadcasted_iota(jnp.int32, (vectors.shape[0], columns), 0)
        for index in range(2):
            table = jnp.where(
                few == 6 + groups + near, input_near[index : index + 1, :], 0.0
            ) + jnp.where(few == 6 + groups + far, input_far[index : index + 1, :], 0.0)
            vectors[:, 2 * index * LANES : 2 * index * LANES + columns] += table

    vectors[0:1, :] += grad_gain
    vectors[1:2, :] += grad_shift


def norm_one_back(groups, place, mine, received, tokens, gain, grad_first, *small):
    rows, width = mine.shape
    tile = 2 * SLOTS
    row = rows_spec(tile, width)
    return pl.pallas_call(
        functools.partial(norm_one_back_kernel, groups),
        grid=(rows // tile,),
        out_shape=(kept((rows, width), F32), shape((16, width), F32)),
        in_specs=[SMEM, row, row, row, fixed_spec(1, width), row]
        + [fixed_spec(*array.shape) for array in small],
        out_specs=(row, fixed_spec(16, width)),
        compiler_params=params(16, 1),
        cost_estimate=cost(rows * width * 25, rows * width * 16),
    )(place, mine, received, *from_hbm(tokens), gain, *from_hbm(grad_first), *small)


def pack_attention_kernel(place, projection, mixer, bias, up_bias, out, tail, sem, tail_sem):
    quarter = place[0]
    tail_copy = pltpu.make_async_copy(mixer, tail.at[pl.ds(0, mixer.shape[0])], tail_sem)
    tail_copy.start()
    size = out.shape[0] - 16
    feature_rows = projection.shape[0]
    first = pl.multiple_of(quarter * size, 16)
    from_projection = quarter * size < feature_rows

    @pl.when(from_projection)
    def _():
        copy = pltpu.make_async_copy(
            projection.at[pl.ds(first, size)], out.at[pl.ds(0, size)], sem
        )
        copy.start()
        copy.wait()

    @pl.when(jnp.logical_not(from_projection))
    def _():
        copy = pltpu.make_async_copy(mixer, out.at[pl.ds(0, size)], sem)
        copy.start()
        copy.wait()

    columns = bias.shape[1]
    row = lax.broadcasted_iota(jnp.int32, (16, columns), 0)
    both = bias[...].astype(F32)
    rows = jnp.where(row == 0, both[0:1, :], jnp.where(row == 1, both[1:2, :], 0.0))
    row_all = lax.broadcasted_iota(jnp.int32, (16, out.shape[1]), 0)
    out[size:, :] = jnp.where(row_all == 2, up_bias[...].astype(F32), 0.0).astype(BF16)
    row_two = jnp.where(row == 2, up_bias[:, 0:columns].astype(F32), rows)
    out[size:, 0:columns] = row_two.astype(BF16)
    tail[size:, :] = out[size:, :]
    tail_copy.wait()


def pack_attention(place, projection, mixer, bias, up_bias):
    size, width = mixer.shape
    return pl.pallas_call(
        pack_attention_kernel,
        out_shape=(shape((size + 16, width), BF16),) * 2,
        in_specs=[SMEM, ANY, ANY, VMEM, VMEM],
        out_specs=(VMEM, VMEM),
        scratch_shapes=[pltpu.SemaphoreType.DMA(()), pltpu.SemaphoreType.DMA(())],
        compiler_params=params(16),
        cost_estimate=cost(0, 2 * size * width),
    )(place, *from_hbm(projection, mixer), bias, up_bias)


def pack_hidden_kernel(place, up, down, out, sems):
    size = out.shape[0] // 2
    first = pl.multiple_of(place[0] * size, 16)
    copies = [
        pltpu.make_async_copy(
            source.at[pl.ds(first, size)], out.at[pl.ds(index * size, size)], sems.at[index]
        )
        for index, source in enumerate((up, down))
    ]
    run_copies(copies)


def pack_hidden(place, up, down):
    size, width = up.shape[0] // 4, up.shape[1]
    return pl.pallas_call(
        pack_hidden_kernel,
        out_shape=shape((2 * size, width), BF16),
        in_specs=[SMEM, ANY, ANY],
        out_specs=VMEM,
        scratch_shapes=[pltpu.SemaphoreType.DMA((2,))],
        compiler_params=params(16),
        cost_estimate=cost(0, 4 * size * width),
    )(place, *from_hbm(up, down))


def run_copies(copies):
    for copy in copies:
        copy.start()
    for copy in copies:
        copy.wait()


def make_copies(copies, sems):
    return [
        pltpu.make_async_copy(source, to, sems.at[index])
        for index, (source, to) in enumerate(copies)
    ]


def piece_copies(place, pieces, target, sems):
    size = pieces[0].shape[0] - 16
    copies = []
    for flip, piece in enumerate(pieces):
        to = pl.multiple_of(lax.bitwise_xor(place[0], flip) * size, 16)
        copies.append((piece.at[pl.ds(0, size)], target.at[pl.ds(to, size)]))
    copies.append((pieces[0].at[pl.ds(size, 16)], target.at[pl.ds(4 * size, 16)]))
    return make_copies(copies, sems)


def hidden_copies(place, pieces, bias_piece, target, sems):
    size = pieces[0].shape[0] // 2
    copies = []
    for flip in range(4):
        quarter = lax.bitwise_xor(place[0], flip)
        for matrix in range(2):
            to = pl.multiple_of((4 * matrix + quarter) * size, 16)
            source = pieces[3 + matrix] if flip == 3 else pieces[flip].at[pl.ds(matrix * size, size)]
            copies.append((source, target.at[pl.ds(to, size)]))
    first = bias_piece.shape[0] - 16
    copies.append((bias_piece.at[pl.ds(first, 16)], target.at[pl.ds(8 * size, 16)]))
    return make_copies(copies, sems)


def head_lanes(rows, width):
    return lax.broadcasted_iota(jnp.int32, (rows, width), 1) // HD


def spread_heads(block, lanes, heads):
    gap = jnp.zeros((LANES - SLOTS, block.shape[1]), block.dtype)
    parts = []
    for head in range(heads):
        parts.append(jnp.where(lanes == head, block, jnp.zeros_like(block)))
        parts.append(gap)
    return jnp.concatenate(parts, axis=0)


def gather_heads(product, lanes, heads):
    total = product[0:SLOTS]
    for head in range(1, heads):
        total = jnp.where(lanes == head, product[head * LANES : head * LANES + SLOTS], total)
    return total


def load_far(place, own, far, target, sems, bias_only):
    def copies(parts):
        at, out = 0, []
        for index, part in enumerate(parts):
            skip = part.shape[0] - 16 if bias_only and index == 2 else 0
            size = part.shape[0] - skip
            out.append((part.at[pl.ds(skip, size)], target.at[pl.ds(at, size)]))
            at += size
        return make_copies(out, sems)

    @pl.when(place[1] == 0)
    def _():
        run_copies(copies(own))

    @pl.when(place[1] != 0)
    def _():
        run_copies(copies(far))


def attention_kernel(
    heads,
    place,
    projection,
    tail,
    near0,
    near1,
    near2,
    near3,
    far0,
    far1,
    normed,
    counts,
    *rest,
):
    saved, soft, part, weights, table, sems = rest[-6:]

    @pl.when(pl.program_id(0) == 0)
    def _():
        copies = piece_copies(place, (near0, near1, near2, near3), weights.at[1], sems)
        for copy in copies:
            copy.start()
        far_sems = sems.at[pl.ds(8, 8)]
        load_far(place, (projection, tail), (far0, far1), weights.at[0], far_sems, False)
        for copy in copies:
            copy.wait()

    cols = heads * HD
    visible_rows = counts[:, 0:LANES].astype(F32)
    for image in range(visible_rows.shape[0]):
        table[image, :, :] = visible_rows[image : image + 1, :]
    rows = normed[...]
    for slot in range(2):
        for index in range(3):
            value = dot_rows(rows, weights[slot, index * cols : (index + 1) * cols, :])
            if index != 1:
                bias_row = 0 if index == 0 else 1
                bias = weights[slot, 4 * cols : 4 * cols + 16, 0:cols].astype(F32)
                value = value + bias[bias_row : bias_row + 1, :]
            saved[4 * slot + index, :, :] = value.astype(BF16)

    lanes = head_lanes(SLOTS, cols)
    key_index = lax.broadcasted_iota(jnp.int32, (SLOTS, LANES), 1).astype(F32)
    first = pl.program_id(0) * TILE_IMAGES

    def one_image(image, carry):
        at = pl.ds(pl.multiple_of(image * SLOTS, 16), SLOTS)
        visible = key_index < table[first + image]
        for slot in range(2):
            queries = saved[4 * slot, at, :]
            keys = spread_heads(saved[4 * slot + 1, at, :], lanes, heads)
            values = spread_heads(saved[4 * slot + 2, at, :], lanes, heads)
            scores = dot_rows(queries, keys) * (HD**-0.5)
            lows = []
            for head in range(heads):
                one = jnp.where(visible, scores[:, head * LANES : (head + 1) * LANES], MASKED)
                exponent = jnp.exp(one - jnp.max(one, axis=-1, keepdims=True))
                total = jnp.sum(exponent, axis=-1, keepdims=True)
                lows.append((exponent / total).astype(BF16))
            low = jnp.concatenate(lows, axis=1)
            soft[at, slot * heads * LANES : (slot + 1) * heads * LANES] = low
            saved[4 * slot + 3, at, :] = dot(low, values).astype(BF16)
        return carry

    lax.fori_loop(0, TILE_IMAGES, one_image, 0, unroll=2)
    total = dot(saved[3, :, :], weights[0, 3 * cols : 4 * cols, :])
    total = total + dot(saved[7, :, :], weights[1, 3 * cols : 4 * cols, :])
    part[...] = total.astype(part.dtype)


def attention(place, own, near, far, normed, before, kind):
    projection, tail = own
    cols, width = projection.shape[0] // 3, projection.shape[1]
    heads = cols // HD
    rows = normed.shape[0] - 16
    tile = TILE_IMAGES * SLOTS
    tiles = rows // tile
    base = tiles if before is None else 0
    extra = () if before is None else from_hbm(*before)
    args = (place, projection, tail, *near, *far, normed, normed, *extra)
    return pl.pallas_call(
        functools.partial(attention_kernel, heads),
        grid=(tiles,),
        out_shape=(
            kept((8, 2 * rows, cols), BF16),
            kept((2 * rows, 2 * heads * LANES), BF16),
            shape((rows, width), kind),
        ),
        in_specs=[SMEM]
        + [ANY] * 8
        + [
            pl.BlockSpec((tile, width), lambda i: (i, 0)),
            pl.BlockSpec((16, width), lambda i: (rows // 16, 0)),
        ]
        + [ANY] * len(extra),
        out_specs=(
            pl.BlockSpec((8, tile, cols), lambda i: (0, base + i, 0)),
            pl.BlockSpec((tile, 2 * heads * LANES), lambda i: (base + i, 0)),
            pl.BlockSpec((tile, width), lambda i: (i, 0)),
        ),
        scratch_shapes=[
            pltpu.VMEM((2, 4 * cols + 16, width), BF16),
            pltpu.VMEM((16, 1, LANES), F32),
            pltpu.SemaphoreType.DMA((16,)),
        ],
        input_output_aliases={11: 0, 12: 1} if extra else {},
        compiler_params=params(20, 1),
        cost_estimate=cost(rows * width * cols * 16 + rows * 400000, rows * width * 10 + 5e6),
    )(*args)


def split_gradient(place, source, matrices, send_x, send_y, keep_x, keep_y):
    half = send_x.shape[2]
    for flip in range(4):
        quarter = lax.bitwise_xor(place[0], flip)
        for part in range(2):
            at = pl.ds(pl.multiple_of((2 * quarter + part) * half, 16), half)
            if part == 0:
                ref, index = (keep_x, flip // 2) if flip % 2 == 0 else (send_x, flip // 2)
            else:
                ref, index = (keep_y, flip % 2) if flip < 2 else (send_y, flip % 2)
            for matrix in range(matrices):
                ref[index, matrix, :, :] = source(matrix, at).astype(BF16)


def gradient_outputs(matrices, size, width):
    spec = pl.BlockSpec((2, matrices, size // 8, width), lambda i: (0, 0, 0, 0))
    return (shape((2, matrices, size // 8, width), BF16),) * 4, (spec,) * 4


def attention_back_kernel(heads, far, last, place, *rest):
    count = 4
    pieces, rest = rest[:count], rest[count:]
    normed_mine, normed_other, grad_mine, grad_other, saved, soft = rest[:6]
    rest = rest[6:]
    if last:
        back_in, rest = rest[0], rest[1:]
    keep, send_x, send_y, send_xy, bias_sums = rest[:5]
    rest = rest[5:]
    if last:
        back_mine, back_other = rest[:2]
        rest = rest[2:]
    else:
        back_sum, rest = rest[0], rest[1:]
    weights, sums, grads, sems = rest
    step = pl.program_id(0)
    steps = pl.num_programs(0)
    cols = heads * HD
    mine = step < steps // 2

    @pl.when(step == 0)
    def _():
        if far:
            load_far(place, pieces[:2], pieces[2:], weights, sems, False)
        else:
            run_copies(piece_copies(place, pieces, weights, sems))
        sums[...] = jnp.zeros_like(sums)
        bias_sums[...] = jnp.zeros_like(bias_sums)

    normed = jnp.where(mine, normed_mine[...], normed_other[...])
    grad = jnp.where(mine, grad_mine[...], grad_other[...])
    grads[3, :, :] = dot_rows(grad, weights[3 * cols : 4 * cols, :]).astype(BF16)
    lanes = head_lanes(SLOTS, cols)

    def one_image(image, carry):
        at = pl.ds(pl.multiple_of(image * SLOTS, 16), SLOTS)
        queries = saved[0, at, :]
        keys = spread_heads(saved[1, at, :], lanes, heads)
        values = spread_heads(saved[2, at, :], lanes, heads)
        grad_mixed = grads[3, at, :]
        low = soft[at, :]
        grad_soft = dot_rows(grad_mixed, values)
        lows = []
        for head in range(heads):
            one = low[:, head * LANES : (head + 1) * LANES].astype(F32)
            grad_one = grad_soft[:, head * LANES : (head + 1) * LANES]
            inner = jnp.sum(grad_one * one, axis=-1, keepdims=True)
            lows.append((one * (grad_one - inner) * (HD**-0.5)).astype(BF16))
        grad_scores = jnp.concatenate(lows, axis=1)
        grad_queries = dot(grad_scores, keys)
        grad_values = gather_heads(dot_columns(low, grad_mixed), lanes, heads)
        grad_keys = gather_heads(dot_columns(grad_scores, queries), lanes, heads)
        bias_sums[0:1, :] += jnp.sum(grad_queries, axis=0, keepdims=True)
        bias_sums[1:2, :] += jnp.sum(grad_values, axis=0, keepdims=True)
        grads[0, at, :] = grad_queries.astype(BF16)
        grads[1, at, :] = grad_keys.astype(BF16)
        grads[2, at, :] = grad_values.astype(BF16)
        return carry

    lax.fori_loop(0, TILE_IMAGES, one_image, 0, unroll=True)
    back = back_in[...] if last else None
    for index in range(3):
        at = slice(index * cols, (index + 1) * cols)
        value = grads[index, :, :]
        term = dot(value, weights[at, :])
        back = term if back is None else back + term
        sums[at, :] += dot_columns(value, normed)
    sums[3 * cols : 4 * cols, :] += dot_columns(saved[3, :, :], grad)
    if last:

        @pl.when(mine)
        def _():
            back_mine[...] = back

        @pl.when(jnp.logical_not(mine))
        def _():
            back_other[...] = back.astype(BF16)

    else:
        back_sum[...] = back

    @pl.when(step == steps - 1)
    def _():
        size = keep.shape[2]
        for flip, ref in enumerate((keep, send_x, send_y, send_xy)):
            quarter = lax.bitwise_xor(place[0], flip)
            for half in range(2):
                at = pl.ds(pl.multiple_of((2 * quarter + half) * size, 16), size)
                ref[half, 0, :, :] = sums[at, :].astype(BF16)


def half_spec(tile, width, tiles, second):
    if second:
        return pl.BlockSpec((tile, width), lambda i: (jnp.maximum(i - tiles, 0), 0))
    return pl.BlockSpec((tile, width), lambda i: (jnp.minimum(i, tiles - 1), 0))


def attention_back(place, slot, own, pieces, normed, grads, saved, soft, before):
    rows, width = grads[0].shape
    cols = saved.shape[2]
    heads = cols // HD
    tile = TILE_IMAGES * SLOTS
    tiles = rows // tile
    far, last = own is not None, before is not None
    mine, other = half_spec(tile, width, tiles, False), half_spec(tile, width, tiles, True)
    both = rows_spec(tile, width)
    grad_shapes, grad_specs = gradient_outputs(1, 4 * cols, width)
    if last:
        more_shapes = (shape((rows, width), F32), shape((rows, width), BF16))
        more_specs = (mine, other)
    else:
        more_shapes = (kept((2 * rows, width), F32),)
        more_specs = (both,)
    weights = (*own, *pieces) if far else pieces
    return pl.pallas_call(
        functools.partial(attention_back_kernel, heads, far, last),
        grid=(2 * tiles,),
        out_shape=(*grad_shapes, shape((8, cols), F32), *more_shapes),
        in_specs=[SMEM]
        + [ANY] * len(weights)
        + [
            mine,
            other,
            mine,
            other,
            pl.BlockSpec((4, tile, cols), lambda i: (slot, i, 0)),
            pl.BlockSpec((tile, heads * LANES), lambda i: (i, slot)),
        ]
        + ([both] if last else []),
        out_specs=(*grad_specs, fixed_spec(8, cols), *more_specs),
        scratch_shapes=[
            pltpu.VMEM((4 * cols + 16, width), BF16),
            pltpu.VMEM((4 * cols, width), F32),
            pltpu.VMEM((4, tile, cols), BF16),
            pltpu.SemaphoreType.DMA((16,)),
        ],
        compiler_params=params(24, 1),
        cost_estimate=cost(rows * width * cols * 30 + rows * 6e5, rows * width * 20 + 4e6),
    )(place, *weights, *normed, *grads, *from_hbm(saved, soft, *(before or ())))


def hidden_kernel(whole, last, place, *rest):
    count = 6
    pieces, rest = rest[:count], rest[count:]
    normed_mine, normed_other, grad_mine, grad_other = rest[:4]
    rest = rest[4:]
    if last:
        out_in, back_in = rest[:2]
        rest = rest[2:]
        whole_grads, bias_sums = rest[:2]
        out_mine, out_other, back_mine, back_other = rest[2:6]
        rest = rest[6:]
    else:
        send_x, send_y, keep_x, keep_y, bias_sums = rest[:5]
        out_sum, back_sum = rest[5:7]
        rest = rest[7:]
    weights, sums_up, sums_down, out_part, back_part, sems = rest
    step = pl.program_id(0)
    steps = pl.num_programs(0)
    width = normed_mine.shape[1]

    @pl.when(step == 0)
    def _():
        if whole:
            load_far(place, pieces[:3], pieces[3:], weights, sems, True)
        else:
            run_copies(hidden_copies(place, pieces[:5], pieces[5], weights, sems))
        sums_up[...] = jnp.zeros_like(sums_up)
        sums_down[...] = jnp.zeros_like(sums_down)
        bias_sums[...] = jnp.zeros_like(bias_sums)

    mine = step < steps // 2
    normed = jnp.where(mine, normed_mine[...], normed_other[...])
    grad = jnp.where(mine, grad_mine[...], grad_other[...])
    bias_rows = weights[2 * width : 2 * width + 16, :].astype(F32)
    chunk = 256
    for first in range(0, width, chunk):
        columns = slice(first, first + chunk)
        up_part = weights[0:width, columns]
        down_part = weights[width + first : width + first + chunk, :]
        hidden = dot(normed, up_part) + bias_rows[2:3, columns]
        phi = 0.5 + 0.5 * lax.erf(hidden * (0.5**0.5))
        slope = phi + hidden * (jnp.exp(-0.5 * hidden * hidden) * ((2.0 * np.pi) ** -0.5))
        active = (hidden * phi).astype(BF16)
        grad_pre = dot_rows(grad, down_part) * slope
        bias_sums[0:1, columns] += jnp.sum(grad_pre, axis=0, keepdims=True)
        grad_low = grad_pre.astype(BF16)
        out_term = dot(active, down_part)
        back_term = dot_rows(grad_low, up_part)
        if first == 0:
            if last:
                out_part[...] = out_in[...] + out_term
                back_part[...] = back_in[...] + back_term
            else:
                out_part[...] = out_term
                back_part[...] = back_term
        else:
            out_part[...] += out_term
            back_part[...] += back_term
        sums_up[:, columns] += dot_columns(normed, grad_low)
        sums_down[columns, :] += dot_columns(active, grad)

    if last:

        @pl.when(mine)
        def _():
            out_mine[...] = out_part[...]
            back_mine[...] = back_part[...]

        @pl.when(jnp.logical_not(mine))
        def _():
            out_other[...] = out_part[...].astype(BF16)
            back_other[...] = back_part[...].astype(BF16)

    else:
        out_sum[...] = out_part[...]
        back_sum[...] = back_part[...]

    @pl.when(step == steps - 1)
    def _():
        if last:
            size = whole_grads.shape[3]
            for flip in range(4):
                quarter = lax.bitwise_xor(place[0], flip)
                for half in range(2):
                    at = pl.ds(pl.multiple_of((2 * quarter + half) * size, 16), size)
                    whole_grads[half, flip, 0, :, :] = sums_up[at, :].astype(BF16)
                    whole_grads[half, flip, 1, :, :] = sums_down[at, :].astype(BF16)
        else:
            split_gradient(
                place,
                lambda m, at: (sums_up if m == 0 else sums_down)[at, :],
                2,
                send_x,
                send_y,
                keep_x,
                keep_y,
            )


def hidden_block(place, pieces, normed, grads, sums_before, whole):
    rows, width = normed[0].shape
    tile = TILE_IMAGES * SLOTS
    tiles = rows // tile
    last = sums_before is not None
    mine, other = half_spec(tile, width, tiles, False), half_spec(tile, width, tiles, True)
    both = rows_spec(tile, width)
    if last:
        dims = (2, 4, 2, width // 8, width)
        grad_shapes, grad_specs = (shape(dims, BF16),), (fixed_spec(*dims),)
    else:
        grad_shapes, grad_specs = gradient_outputs(2, width, width)
    if last:
        more_shapes = (
            kept((rows, width), F32),
            shape((rows, width), BF16),
            shape((rows, width), F32),
            shape((rows, width), BF16),
        )
        more_specs = (mine, other, mine, other)
    else:
        more_shapes = (kept((2 * rows, width), F32),) * 2
        more_specs = (both, both)
    return pl.pallas_call(
        functools.partial(hidden_kernel, whole, last),
        grid=(2 * tiles,),
        out_shape=(*grad_shapes, shape((8, width), F32), *more_shapes),
        in_specs=[SMEM]
        + [ANY] * 6
        + [mine, other, mine, other]
        + ([both, both] if last else []),
        out_specs=(*grad_specs, fixed_spec(8, width), *more_specs),
        scratch_shapes=[
            pltpu.VMEM((2 * width + 16, width), BF16),
            pltpu.VMEM((width, width), F32),
            pltpu.VMEM((width, width), F32),
            pltpu.VMEM((tile, width), F32),
            pltpu.VMEM((tile, width), F32),
            pltpu.SemaphoreType.DMA((16,)),
        ],
        compiler_params=params(40, 1),
        cost_estimate=cost(rows * width * width * 24, rows * width * 24 + 8e6),
    )(place, *pieces, *normed, *grads, *from_hbm(*(sums_before or ())))


def first_sums_kernel(keep_x, keep_y, got_x, got_y, send_y, send_x, base):
    add = lambda u, v: u.astype(F32) + v.astype(F32)
    base[0] = add(keep_x[0], got_x[0])
    base[1] = add(keep_y[0], got_y[0])
    send_y[...] = add(keep_x[1], got_x[1]).astype(BF16)
    send_x[...] = add(keep_y[1], got_y[1]).astype(BF16)


def plane_sums_kernel(base, next_y, next_x, plane):
    plane[0] = (base[0] + next_y[...].astype(F32)).astype(BF16)
    plane[1] = (base[1] + next_x[...].astype(F32)).astype(BF16)


def depth_sums_kernel(core, local_far, far, near, keep, send):
    halves = []
    for half in range(2):
        first = jnp.where(core == 0, local_far[half], far[half])
        halves.append(first.astype(F32) + near[half].astype(F32))
    keep[...] = jnp.where(core == 0, halves[0], halves[1])
    send[...] = jnp.where(core == 0, halves[1], halves[0]).astype(BF16)


def pair_send_kernel(core, own, got, send):
    send[...] = jnp.where(core == 0, own[1], got[0])


def pair_sums_kernel(core, own, got, received, keep, send_x, send_y, send_xy):
    for flip, ref in enumerate((keep, send_x, send_y, send_xy)):
        half = jnp.where(core == 0, own[0, flip], got[1, flip])
        ref[...] = (half.astype(F32) + received[flip].astype(F32)).astype(BF16)


def half_split_kernel(core, both, keep, send):
    keep[...] = jnp.where(core == 0, both[0], both[1])
    send[...] = jnp.where(core == 0, both[1], both[0])


def last_sums_kernel(keep, received, total):
    total[...] = (keep[...] + received[...].astype(F32)).astype(BF16)


def total_kernel(*refs):
    total = refs[0][...].astype(F32)
    for ref in refs[1:-1]:
        total = total + ref[...].astype(F32)
    refs[-1][...] = total.astype(refs[-1].dtype)


def sums_kernel(parts, place, *refs):
    ins = sum(count for _, count, _ in parts)
    in_refs, out_refs = refs[:ins], refs[ins:]
    for body, count, outs in parts:
        mine, in_refs = in_refs[:count], in_refs[count:]
        results, out_refs = out_refs[:outs], out_refs[outs:]
        if body in (depth_sums_kernel, pair_send_kernel, pair_sums_kernel, half_split_kernel):
            body(place[1], *mine, *results)
        else:
            body(*mine, *results)


def sums(place, *work):
    parts, args, out_shapes = [], [], []
    for body, arrays in work:
        like = arrays[0].shape
        if body is first_sums_kernel:
            outs = [shape(like[1:], BF16), shape(like[1:], BF16), shape(like, F32)]
        elif body is plane_sums_kernel:
            outs = [shape(like, BF16)]
        elif body is pair_send_kernel:
            outs = [shape(like[1:], BF16)]
        elif body is pair_sums_kernel:
            outs = [shape(like[2:], BF16)] * 4
        elif body is half_split_kernel:
            outs = [shape(like[1:], BF16)] * 2
        elif body is depth_sums_kernel:
            outs = [shape(like[1:], F32), shape(like[1:], BF16)]
        else:
            outs = [shape(like, arrays[0].dtype if body is total_kernel else BF16)]
        parts.append((body, len(arrays), len(outs)))
        args += arrays
        out_shapes += outs
    moved = sum(4 * np.prod(o.shape) for o in out_shapes)
    results = pl.pallas_call(
        functools.partial(sums_kernel, tuple(parts)),
        out_shape=tuple(out_shapes),
        in_specs=[SMEM] + [VMEM] * len(args),
        out_specs=(VMEM,) * len(out_shapes),
        compiler_params=params(16),
        cost_estimate=cost(0, moved),
    )(place, *args)
    grouped = []
    for _, _, count in parts:
        grouped.append(tuple(results[:count]))
        results = results[count:]
    return grouped


def finish_kernel(place, *refs):
    mine, other, outs = refs[:4], refs[4:8], refs[8:]
    half = mine[0].shape[1]
    for flip in range(4):
        quarter = lax.bitwise_xor(place[0], flip)
        for side, parts in enumerate((mine, other)):
            part = place[1] if side == 0 else 1 - place[1]
            for matrix, out in enumerate(outs):
                at = pl.ds(pl.multiple_of((2 * quarter + part) * half, 8), half)
                out[at, :] = parts[flip][matrix, :, :].astype(F32)


def finish_attention_kernel(place, *refs):
    mine, other, (grad_input, grad_mixer) = refs[:4], refs[4:8], refs[8:]
    half = mine[0].shape[1]
    for flip in range(4):
        quarter = lax.bitwise_xor(place[0], flip)
        for side, parts in enumerate((mine, other)):
            part = place[1] if side == 0 else 1 - place[1]

            @pl.when(quarter < 3)
            def _():
                at = pl.ds(pl.multiple_of((2 * quarter + part) * half, 8), half)
                grad_input[at, :] = parts[flip][0, :, :].astype(F32)

            @pl.when(quarter == 3)
            def _():
                at = pl.ds(pl.multiple_of(part * half, 8), half)
                grad_mixer[at, :] = parts[flip][0, :, :].astype(F32)


def finish(place, mine, other):
    matrices, half, width = mine[0].shape
    if matrices == 1:
        kernel = finish_attention_kernel
        out_shapes = (shape((6 * half, width), F32), shape((2 * half, width), F32))
    else:
        kernel = finish_kernel
        out_shapes = (shape((8 * half, width), F32),) * matrices
    return pl.pallas_call(
        kernel,
        out_shape=out_shapes,
        in_specs=[SMEM] + [VMEM] * 8,
        out_specs=(VMEM,) * len(out_shapes),
        compiler_params=params(16),
        cost_estimate=cost(0, matrices * half * width * 48),
    )(place, *mine, *other)


def local(
    tokens,
    visible_counts,
    norm_one_gain,
    norm_one_shift,
    input_weight,
    input_bias,
    mixer_weight,
    mixer_bias,
    norm_two_gain,
    norm_two_shift,
    up_weight,
    up_bias,
    down_weight,
    down_bias,
    output_grad,
    groups,
    outer,
):
    width = tokens.shape[1]
    rows = tokens.shape[0]
    cols = mixer_weight.shape[0]
    t = lax.axis_index("t")
    core = lax.axis_index("c")
    place = jnp.stack([2 * lax.axis_index("a") + lax.axis_index("b"), core, t]).astype(jnp.int32)
    one_row = lambda v: v.reshape(1, -1)

    swap = [(0, 1), (1, 0)]
    cross = [(0, 3), (1, 2), (2, 1), (3, 0)]
    to_near = [(z, (z + 1) % groups) for z in range(groups)] + [
        (groups + z, groups + (z + 2) % groups) for z in range(groups)
    ]
    to_far = [(groups + z, groups + (z + 3) % groups) for z in range(groups)]
    back_near = [(j, i) for i, j in to_near]
    back_far = [(j, i) for i, j in to_far]

    def spread(piece):
        return (
            piece,
            lax.ppermute(piece, "b", swap),
            lax.ppermute(piece, "a", swap),
            lax.ppermute(piece, ("a", "b"), cross),
        )

    def together(*groups):
        return lax.optimization_barrier(groups)

    def after(value, *others):
        return lax.optimization_barrier((value, *others))[0]

    def first_exchange(send_x, send_y, keep_x, keep_y):
        got_x = lax.ppermute(send_x, "b", swap)
        got_y = lax.ppermute(send_y, "a", swap)
        return keep_x, keep_y, got_x, got_y

    def second_exchange(send_y, send_x, base):
        return base, lax.ppermute(send_y, "a", swap), lax.ppermute(send_x, "b", swap)

    def direct(keep, send_x, send_y, send_xy):
        return (
            keep,
            lax.ppermute(send_x, "b", swap),
            lax.ppermute(send_y, "a", swap),
            lax.ppermute(send_xy, ("a", "b"), cross),
        )

    def over_outer(value):
        return lax.psum(value.astype(F32), "o").astype(BF16) if outer > 1 else value

    projection = input_weight.transpose(1, 2, 0).reshape(3 * cols, width)
    normed_one = norm_one(
        place,
        visible_counts,
        tokens,
        one_row(norm_one_gain),
        one_row(norm_one_shift),
    )
    piece_one, tail_one = pack_attention(
        place, projection, mixer_weight, after(input_bias, normed_one), one_row(up_bias)
    )
    depth_near_one = lax.ppermute(piece_one, ("c", "t"), to_near)
    normed_other = lax.ppermute(normed_one, "c", swap)
    piece_two = pack_hidden(place, up_weight, down_weight)
    depth_near_one, normed_other, piece_two = together(depth_near_one, normed_other, piece_two)
    near_one = spread(depth_near_one)
    far_projection = lax.ppermute(after(projection, depth_near_one), ("c", "t"), to_far)
    far_mixer = lax.ppermute(after(tail_one, depth_near_one), ("c", "t"), to_far)
    near_two = lax.ppermute(after(piece_two, far_mixer, *near_one), ("c", "t"), to_near)

    own_one = (projection, tail_one)
    far_one = (far_projection, far_mixer)
    saved, soft, part = attention(place, own_one, near_one, far_one, normed_other, None, BF16)
    saved, soft, part, near_two = together(saved, soft, part, near_two)
    grad_other = lax.ppermute(after(output_grad, part), "c", swap)
    part_received = lax.ppermute(part, "c", swap)
    near_x = lax.ppermute(near_two, "b", swap)
    near_y = lax.ppermute(near_two, "a", swap)
    far_up = lax.ppermute(after(up_weight, near_two), ("c", "t"), to_far)
    saved, soft, part = attention(
        place, own_one, near_one, far_one, normed_one, (saved, soft), F32
    )
    part, part_received, near_x, near_y, far_up, grad_other = together(
        part, part_received, near_x, near_y, far_up, grad_other
    )
    quarter = near_two.shape[0] // 2
    near_up = lax.ppermute(near_y[:quarter], "b", swap)
    near_down = lax.ppermute(near_x[quarter:], "a", swap)
    first_sum, normed_two = norm_two(
        tokens,
        part,
        part_received,
        one_row(mixer_bias),
        one_row(norm_two_gain),
        one_row(norm_two_shift),
    )
    far_down = lax.ppermute(after(down_weight, far_up), ("c", "t"), to_far)
    normed_two_both = (normed_two, lax.ppermute(normed_two, "c", swap))

    grad_both = (output_grad, grad_other)
    pieces = (near_two, near_x, near_y, near_up, near_down, depth_near_one)
    near_outs = hidden_block(place, pieces, normed_two_both, grad_both, None, False)
    near_outs, far_down = together(near_outs, far_down)
    *grads_near, bias_near, out_sum, back_sum = near_outs
    stage_near = first_exchange(*grads_near)
    shards = (up_weight, down_weight, tail_one, far_up, far_down, far_mixer)
    far_outs = hidden_block(
        place, shards, normed_two_both, grad_both, (out_sum, back_sum), True
    )
    far_outs, stage_near = together(far_outs, stage_near)
    grads_far, bias_far, out_mine, out_send, back_mine, back_send = far_outs

    got_far = lax.ppermute(grads_far, ("c", "t"), back_far)
    back_received = lax.ppermute(back_send, "c", swap)
    (stage_near,) = sums(place, (first_sums_kernel, stage_near))
    back_received = after(back_received, *stage_near)
    stage_near = second_exchange(*stage_near)
    grad_first, grad_first_low, sums_two = norm_two_back(
        back_mine, back_received, first_sum, one_row(norm_two_gain), output_grad
    )
    first_other = lax.ppermute(grad_first_low, "c", swap)
    out_received = lax.ppermute(after(out_send, first_other), "c", swap)

    normed_both = (normed_one, normed_other)
    first_both = (grad_first_low, first_other)
    *grads_one_near, bias_one_near, back_sum = attention_back(
        place, 1, None, near_one, normed_both, first_both, saved, soft, None
    )
    grads_one_near, back_sum, stage_near, got_far, out_received = together(
        grads_one_near, back_sum, stage_near, got_far, out_received
    )
    one_near = direct(*grads_one_near)
    (plane_near,), (send_far,) = sums(
        place, (plane_sums_kernel, stage_near), (pair_send_kernel, (grads_far, got_far))
    )
    depth_near = lax.ppermute(plane_near, ("c", "t"), back_near)
    received_far = lax.ppermute(send_far, "c", swap)
    back_sum = after(back_sum, plane_near)
    *grads_one_far, bias_one_far, back_mine, back_send = attention_back(
        place, 0, own_one, far_one, normed_both, first_both, saved, soft, (back_sum,)
    )
    grads_one_far, back_mine, back_send, one_near, received_far, depth_near = together(
        grads_one_far, back_mine, back_send, one_near, received_far, depth_near
    )

    one_far = direct(*grads_one_far)
    back_received = lax.ppermute(back_send, "c", swap)
    (one_near,), sums_far, (keep_two, send_two) = sums(
        place,
        (total_kernel, one_near),
        (pair_sums_kernel, (grads_far, got_far, received_far)),
        (half_split_kernel, (depth_near,)),
    )
    one_depth_near = lax.ppermute(one_near, ("c", "t"), back_near)
    received_two = lax.ppermute(send_two, "c", swap)
    grad_tokens, vectors = norm_one_back(
        groups,
        place,
        back_mine,
        back_received,
        tokens,
        one_row(norm_one_gain),
        grad_first,
        sums_two,
        bias_near,
        bias_far,
        bias_one_near,
        bias_one_far,
    )
    vectors_core = lax.ppermute(vectors, "c", swap)
    vectors_core, one_far, received_two = together(vectors_core, one_far, received_two)
    (one_far,), (vectors,) = sums(
        place, (total_kernel, one_far), (total_kernel, (vectors, vectors_core))
    )
    one_depth_far = lax.ppermute(one_far, ("c", "t"), back_far)
    sums_far = direct(*sums_far)
    result = (first_sum + (out_mine + out_received.astype(F32)) + down_bias).astype(BF16)
    one_depth_far, one_depth_near, result = together(one_depth_far, one_depth_near, result)
    ((keep_one, send_one),) = sums(
        place, (depth_sums_kernel, (one_far, one_depth_far, one_depth_near))
    )
    received_one = lax.ppermute(send_one, "c", swap)
    vectors_plane = spread(vectors)
    received_one, vectors_plane, sums_far = together(received_one, vectors_plane, sums_far)
    (part_one,), (part_two,), (vectors,) = sums(
        place,
        (last_sums_kernel, (keep_one, received_one)),
        (total_kernel, (*sums_far, keep_two, received_two)),
        (total_kernel, vectors_plane),
    )
    mine_one = spread(over_outer(part_one))
    mine_two = spread(over_outer(part_two))
    turns = [
        lax.ppermute(vectors, "t", [(z, (z + k) % groups) for z in range(groups)])
        for k in range(1, groups)
    ]
    other_two = tuple(lax.ppermute(part, "c", swap) for part in mine_two)
    grad_up, grad_down = finish(place, mine_two, other_two)
    other_one = tuple(lax.ppermute(part, "c", swap) for part in mine_one)
    grad_input, grad_mixer = finish(place, mine_one, other_one)
    grad_input = grad_input.reshape(3, cols, width).transpose(2, 0, 1)
    vectors = sum(turns, vectors)
    if outer > 1:
        vectors = lax.psum(vectors, "o")
    grad_up_bias = lax.dynamic_slice_in_dim(vectors, 6 + t, 1)[0]
    grad_input_bias = lax.dynamic_slice_in_dim(vectors, 6 + groups + t, 1).reshape(-1, 2 * LANES)[
        :2, :cols
    ]
    return (
        result,
        grad_tokens,
        vectors[0],
        vectors[1],
        grad_input,
        grad_input_bias,
        grad_mixer,
        vectors[4],
        vectors[2],
        vectors[3],
        grad_up,
        grad_up_bias,
        grad_down,
        vectors[5],
    )


def solution(mesh):
    dp, groups = mesh.shape["dp"], mesh.shape["tensor"]
    outer = dp // 8
    split = jax.sharding.Mesh(
        mesh.devices.reshape(outer, 2, 2, 2, groups), ("o", "a", "b", "c", "t")
    )
    dp_axes = ("o", "a", "b", "c")
    all_axes = dp_axes + ("t",)
    in_specs = (
        P(all_axes, None),
        P(dp_axes),
        P(),
        P(),
        P(None, None, "t"),
        P(None, "t"),
        P("t", None),
        P(),
        P(),
        P(),
        P(None, "t"),
        P("t"),
        P("t", None),
        P(),
        P(all_axes, None),
    )
    out_specs = (
        P(all_axes, None),
        P(all_axes, None),
        P(),
        P(),
        P(None, None, "t"),
        P(None, "t"),
        P("t", None),
        P(),
        P(),
        P(),
        P(None, "t"),
        P("t"),
        P("t", None),
        P(),
    )
    return jax.shard_map(
        functools.partial(local, groups=groups, outer=outer),
        mesh=split,
        in_specs=in_specs,
        out_specs=out_specs,
        check_vma=False,
    )
```

time: 336 us -> 267 us (0.79)
  waiting for transfers between devices: 103 us -> 54.8 us
  local copies, waits for them, and re-layouts: 22.6 us -> 8.1 us
  other arithmetic: 14.1 us -> 2.37 us
  Pallas kernels: 105 us -> 113 us
    ppermute x35 -> x41, waiting for transfers between devices: 61.9 us -> 27.9 us  [the longest x1 8.73 us: local(): depth_near_one = lax.ppermute(piece_one, ('c', 't'), to_near)]
    ppermute x4, waiting for transfers between devices: 20 us -> 6.92 us  [spread(): lax.ppermute(piece, 'a', swap)]
    ppermute x4, waiting for transfers between devices: 16.2 us -> 4.09 us  [spread(): lax.ppermute(piece, 'b', swap)]
    unnamed x112 -> x38, local copies, waits for them, and re-layouts: 17.2 us -> 5.41 us
    pallas_call x8 -> x15, Pallas kernels: 42.4 us -> 52.4 us  [the longest x2 25.3 us: attention_back(): pl.pallas_call(functools.partial(attention_back_kernel, heads, far, last)...]
    ppermute x1, starting transfers between devices: 9.29 us -> 0.08 us  [local(): part_received = lax.ppermute(part, 'c', swap)]
    ppermute x4, waiting for transfers between devices: 4.08 us -> 12.8 us  [spread(): lax.ppermute(piece, ('a', 'b'), cross)]
    another operation x11 -> x0, other arithmetic: 7.88 us -> none  [the longest x9 4.69 us: plane_sum(): return jnp.stack([first, second])]
  transfers between devices with their start and end apart: 56 -> 62, of which waited for: 19 -> 19; matrix products, arithmetic and copies ran while one was open for 5% -> 1% of each run, Pallas kernels for 27% -> 38%
where the time goes in v2:
time: 267 us; the launch traced here: 266 us
  Pallas kernels  113 us (42%)
  starting transfers between devices  86.1 us (32%)
  waiting for transfers between devices  54.8 us (21%)
  local copies, waits for them, and re-layouts  8.1 us (3%)
    pallas_call x2, Pallas kernels, hidden_block(): pl.pallas_call(functools.partial(hidden_kernel, whole, last), grid=(2 * t...  35.3 us
    pallas_call x2, Pallas kernels, attention_back(): pl.pallas_call(functools.partial(attention_back_kernel, heads, far, last)...  25.3 us
    pallas_call x2, Pallas kernels, attention(): pl.pallas_call(functools.partial(attention_kernel, heads), grid=(tiles,),...  23.5 us
    ppermute x1, starting transfers between devices, local(): grad_other = lax.ppermute(after(output_grad, part), 'c', swap)  18 us
    ppermute x4, waiting for transfers between devices, spread(): lax.ppermute(piece, ('a', 'b'), cross)  12.8 us
    ppermute x1, waiting for transfers between devices, local(): depth_near_one = lax.ppermute(piece_one, ('c', 't'), to_near)  8.73 us
    ppermute x4, waiting for transfers between devices, spread(): lax.ppermute(piece, 'a', swap)  6.92 us
    ppermute x1, waiting for transfers between devices, local(): near_up = lax.ppermute(near_y[:quarter], 'b', swap)  6.82 us
  transfers between devices with their start and end apart: 62, of which 19 were waited for; matrix products, arithmetic and copies ran while one was open for 1% of the time, Pallas kernels for 38%

profile of v2, /device:TPU:0, one launch (start us, length us, event | category | flops | bytes accessed | tf_op | source)
XLA Modules:
  0.0 265.9 jit_solution(2261022028842574013)
XLA Ops:
  2.1 1.2 copy-done.1
  4.0 2.2 shard_map.254.normed.counts.rest_4_
  6.8 1.6 shard_map.255
  8.4 2.7 collective-permute-start
  11.1 1.6 shard_map.256
  12.7 8.7 %collective-permute-done.near0.rest_5_.rest_0_ = bf16[208,768]{1,0:T(8,128)(2,1)S(1)} collective-permute-done((bf16[208,768]{1,0:T(8,128)(2,1)S(1)}, bf16[208,768]{1,0:T(8,128)(2,1)S(1)}, u32[]{:S(2)}, u32[]{:S(2)}) %collective-permute-start) | collective-permute-done | bytes 319520 | tf_op jit(solution)/shard_map/ppermute | solution.py:1024
  23.0 1.6 collective-permute-start.4
  24.6 1.5 collective-permute-start.5
  26.6 3.5 %collective-permute-done.4.near1.rest_1_ = bf16[208,768]{1,0:T(8,128)(2,1)S(1)} collective-permute-done((bf16[208,768]{1,0:T(8,128)(2,1)S(1)}, bf16[208,768]{1,0:T(8,128)(2,1)S(1)}, u32[]{:S(2)}, u32[]{:S(2)}) %collective-permute-start.4) | collective-permute-done | bytes 319520 | tf_op jit(solution)/shard_map/ppermute | solution.py:983
  30.1 5.2 %collective-permute-done.5.near2.rest_2_ = bf16[208,768]{1,0:T(8,128)(2,1)S(1)} collective-permute-done((bf16[208,768]{1,0:T(8,128)(2,1)S(1)}, bf16[208,768]{1,0:T(8,128)(2,1)S(1)}, u32[]{:S(2)}, u32[]{:S(2)}) %collective-permute-start.5) | collective-permute-done | bytes 319520 | tf_op jit(solution)/shard_map/ppermute | solution.py:984
  35.3 2.2 collective-permute-start.7
  37.5 11.7 %shard_map.257 = (bf16[8,1280,192]{2,1,0:T(8,128)(2,1)}, bf16[1280,768]{1,0:T(8,128)(2,1)}, bf16[640,768]{1,0:T(8,128)(2,1)S(1)}) custom-call(s32[3]{0:T(128)S(1)} %pad_add_fusion.place, bf16[576,768]{1,0:T(8,128)(2,1)S(1)} %bitcast.11, bf16[208,768]{1,0:T(8,128)(2,1)S(1)} %get-tuple-element.164.tail.rest_2_.rest_1_, ...), custom_call_target="tpu_custom_call" | custom-call | flops 1765949440 | bytes 9915200 | tf_op jit(solution)/shard_map/pallas_call | solution.py:463
  50.6 18.0 %collective-permute-start.12 = (bf16[640,768]{1,0:T(8,128)(2,1)S(1)}, bf16[640,768]{1,0:T(8,128)(2,1)S(1)}, u32[]{:S(2)}, u32[]{:S(2)}) collective-permute-start(bf16[640,768]{1,0:T(8,128)(2,1)S(1)} %copy-done.5), channel_id=1, source_target_pairs={{0,4},{4,0},{1,5},{5,1},{2,6},{6,2},{3,7},{7,3},{8,12},{12,8},{9,1... | collective-permute-start | bytes 2949128 | tf_op jit(solution)/shard_map/ppermute | solution.py:1037
  69.4 2.2 collective-permute-start.9
  71.6 11.8 %shard_map.258 = (bf16[8,1280,192]{2,1,0:T(8,128)(2,1)}, bf16[1280,768]{1,0:T(8,128)(2,1)}, f32[640,768]{1,0:T(8,128)S(1)}) custom-call(s32[3]{0:T(128)S(1)} %pad_add_fusion.place, bf16[576,768]{1,0:T(8,128)(2,1)S(1)} %bitcast.12, bf16[208,768]{1,0:T(8,128)(2,1)S(1)} %get-tuple-element.164.tail.rest_2_.rest_1_, ...), custom_call_target="tpu_custom_call", output_to_operand_aliasing={{0}: (11, {}), {1}: (12, {})} | custom-call | flops 1765949440 | bytes 9915200 | tf_op jit(solution)/shard_map/pallas_call | solution.py:463
  83.4 0.9 collective-permute-done.10.rest_2_
  84.3 1.0 collective-permute-done.9.rest_1_
  85.3 3.8 %shard_map.259 = (f32[640,768]{1,0:T(8,128)}, bf16[640,768]{1,0:T(8,128)(2,1)S(1)}) custom-call(bf16[640,768]{1,0:T(8,128)(2,1)} %tokens.5, f32[640,768]{1,0:T(8,128)S(1)} %get-tuple-element.181.mine, bf16[640,768]{1,0:T(8,128)(2,1)S(1)} %collective-permute-done.8.received, f32[1,768]{1,0:T(1,128)S(1)} %reshape.62.bias, f32[1,768]{1,0:T(1,128)S(1)} %reshape.63.gain, ...), custom_call_target="tpu_custom_call" | custom-call | flops 5898240 | bytes 6881280 | tf_op jit(solution)/shard_map/pallas_call | solution.py:131
  89.1 0.9 collective-permute-start.16
  90.0 1.8 collective-permute-start.13
  92.4 6.8 %collective-permute-done.13.rest_3_ = bf16[192,768]{1,0:T(8,128)(2,1)S(1)} collective-permute-done((bf16[192,768]{1,0:T(8,128)(2,1)S(1)}, bf16[192,768]{1,0:T(8,128)(2,1)S(1)}, u32[]{:S(2)}, u32[]{:S(2)}) %collective-permute-start.13) | collective-permute-done | bytes 294944 | tf_op jit(solution)/shard_map/ppermute | solution.py:1049
  99.3 2.2 collective-permute-done.14.rest_4_
  101.4 16.7 %shard_map.260 = (bf16[2,2,96,768]{3,2,1,0:T(8,128)(2,1)S(1)}, bf16[2,2,96,768]{3,2,1,0:T(8,128)(2,1)S(1)}, bf16[2,2,96,768]{3,2,1,0:T(8,128)(2,1)S(1)}, bf16[2,...) custom-call(s32[3]{0:T(128)S(1)} %pad_add_fusion.place, ...), custom_call_target="tpu_custom_call" | custom-call | flops 9059696640 | bytes 19796480 | tf_op jit(solution)/shard_map/pallas_call | solution.py:776
  118.1 1.0 copy-done.8
  120.2 1.3 copy-done.9
  121.5 1.2 copy-done.11
  122.7 18.6 %shard_map.261 = (bf16[2,4,2,96,768]{4,3,2,1,0:T(8,128)(2,1)}, f32[8,768]{1,0:T(8,128)S(1)}, f32[640,768]{1,0:T(8,128)}, bf16[640,768]{1,0:T(8,128)(2,1)S(1)}, f...) custom-call(s32[3]{0:T(128)S(1)} %pad_add_fusion.place, bf16[768,768]{1,0:T(8,128)(2,1)S(1)} %copy-done.3, ...), custom_call_target="tpu_custom_call" | custom-call | flops 9059696640 | bytes 19796480 | tf_op jit(solution)/shard_map/pallas_call | solution.py:776
  141.4 1.0 collective-permute-start.23
  144.0 4.8 %shard_map.263 = (f32[640,768]{1,0:T(8,128)}, bf16[640,768]{1,0:T(8,128)(2,1)S(1)}, f32[8,768]{1,0:T(8,128)S(1)}) custom-call(f32[640,768]{1,0:T(8,128)S(1)} %get-tuple-element.206.mine, bf16[640,768]{1,0:T(8,128)(2,1)S(1)} %collective-permute-done.19.received, f32[640,768]{1,0:T(8,128)} %get-tuple-element.216.first_sum, f32[1,768]{1,0:T(1,128)S(1)} %reshape.63.gain, ...), custom_call_target="tpu_custom_call" | custom-call | flops 12288000 | bytes 8847360 | tf_op jit(solution)/shard_map/pallas_call | solution.py:164
  148.7 0.9 collective-permute-start.20
  149.6 2.2 collective-permute-done.20.rest_7_
  152.2 1.2 collective-permute-start.21
  153.4 1.8 collective-permute-start.22
  155.2 13.1 %shard_map.264 = (bf16[2,1,96,768]{3,2,1,0:T(8,128)(2,1)S(1)}, bf16[2,1,96,768]{3,2,1,0:T(8,128)(2,1)S(1)}, bf16[2,1,96,768]{3,2,1,0:T(8,128)(2,1)S(1)}, bf16[2,...) custom-call(s32[3]{0:T(128)S(1)} %pad_add_fusion.place, ...), custom_call_target="tpu_custom_call" | custom-call | flops 3215155200 | bytes 13830400 | tf_op jit(solution)/shard_map/pallas_call | solution.py:627
  169.1 5.2 %collective-permute-start.28 = (bf16[4,2,96,768]{3,2,1,0:T(8,128)(2,1)S(1)}, bf16[4,2,96,768]{3,2,1,0:T(8,128)(2,1)S(1)}, u32[]{:S(2)}, u32[]{:S(2)}) collective-permute-start(bf16[4,2,96,768]{3,2,1,0:T(8,128)(2,1)S(1)} %get-tuple-element.245), channel_id=1, source_target_pairs={{0,4},{4,0},{1,5},{5,1},{2,6},{6,2},{3,7},{7,3},{8,12},{12,8},{9,1... | collective-permute-start | bytes 3538952 | tf_op jit(solution)/shard_map/ppermute | solution.py:1099
  174.4 1.3 collective-permute-start.25
  175.6 1.7 collective-permute-start.26
  177.9 12.2 %shard_map.266 = (bf16[2,1,96,768]{3,2,1,0:T(8,128)(2,1)S(1)}, bf16[2,1,96,768]{3,2,1,0:T(8,128)(2,1)S(1)}, bf16[2,1,96,768]{3,2,1,0:T(8,128)(2,1)S(1)}, bf16[2,...) custom-call(s32[3]{0:T(128)S(1)} %pad_add_fusion.place, ...), custom_call_target="tpu_custom_call" | custom-call | flops 3215155200 | bytes 13830400 | tf_op jit(solution)/shard_map/pallas_call | solution.py:627
  190.7 3.9 %collective-permute-start.30 = (bf16[640,768]{1,0:T(8,128)(2,1)S(1)}, bf16[640,768]{1,0:T(8,128)(2,1)S(1)}, u32[]{:S(2)}, u32[]{:S(2)}) collective-permute-start(bf16[640,768]{1,0:T(8,128)(2,1)S(1)} %get-tuple-element.247), channel_id=1, source_target_pairs={{0,4},{4,0},{1,5},{5,1},{2,6},{6,2},{3,7},{7,3},{8,12},{12,8},{9,1... | collective-permute-start | bytes 2949128 | tf_op jit(solution)/shard_map/ppermute | solution.py:1109
  194.6 1.0 shard_map.268
  195.8 1.3 collective-permute-start.32
  197.1 1.7 collective-permute-start.33
  199.3 4.9 %shard_map.267 = (f32[640,768]{1,0:T(8,128)}, f32[16,768]{1,0:T(8,128)S(1)}) custom-call(s32[3]{0:T(128)S(1)} %pad_add_fusion.place, f32[640,768]{1,0:T(8,128)S(1)} %get-tuple-element.246.mine, bf16[640,768]{1,0:T(8,128)(2,1)S(1)} %collective-permute-done.30.received, bf16[640,768]{1,0:T(8,128)(2,1)} %tokens.5, f32[1,768]{1,0:T(1,128)S(1)} %reshape.59.gain, ...), custom_call_target="tpu_custom_call" | custom-call | flops 12288000 | bytes 7864320 | tf_op jit(solution)/shard_map/pallas_call | solution.py:221
  204.3 2.1 collective-permute-start.37
  206.4 1.3 collective-permute-start.42
  207.6 4.7 %collective-permute-done.33.refs_2_ = bf16[2,1,96,768]{3,2,1,0:T(8,128)(2,1)S(1)} collective-permute-done((bf16[2,1,96,768]{3,2,1,0:T(8,128)(2,1)S(1)}, bf16[2,1,96,768]{3,2,1,0:T(8,128)(2,1)S(1)}, u32[]{:S(2)}, u32[]{:S(2)}) %collective-permute-start.33) | collective-permute-done | bytes 294944 | tf_op jit(solution)/shard_map/ppermute | solution.py:1006
  212.3 1.9 collective-permute-start.43
  215.6 1.4 add_convert_fusion
  217.7 6.2 %collective-permute-start.38 = (bf16[1,96,768]{2,1,0:T(8,128)(2,1)S(1)}, bf16[1,96,768]{2,1,0:T(8,128)(2,1)S(1)}, u32[]{:S(2)}, u32[]{:S(2)}) collective-permute-start(bf16[1,96,768]{2,1,0:T(8,128)(2,1)S(1)} %get-tuple-element.280), channel_id=1, source_target_pairs={{0,4},{4,0},{1,5},{5,1},{2,6},{6,2},{3,7},{7,3},{8,12},{12,8},{9,1... | collective-permute-start | bytes 442376 | tf_op jit(solution)/shard_map/ppermute | solution.py:1144
  223.9 1.5 collective-permute-start.39
  225.4 1.7 collective-permute-start.40
  228.0 1.5 collective-permute-done.40.refs_10_
  229.5 2.6 collective-permute-done.41.refs_11_
  232.1 1.2 shard_map.271
  233.7 1.2 collective-permute-start.49
  235.0 3.1 %collective-permute-start.46 = (f32[16,768]{1,0:T(8,128)}, f32[16,768]{1,0:T(8,128)}, u32[]{:S(2)}, u32[]{:S(2)}) collective-permute-start(f32[16,768]{1,0:T(8,128)} %get-tuple-element.297), channel_id=1, source_target_pairs={{0,2},{1,3},{2,0},{3,1},{4,6},{5,7},{6,4},{7,5},{8,10},{9,11},{10,... | collective-permute-start | bytes 147464 | tf_op jit(solution)/shard_map/ppermute | solution.py:1156
  238.8 2.4 collective-permute-done.45
  241.2 2.0 collective-permute-start.55
  243.6 1.1 collective-permute-start.57
  244.7 1.9 collective-permute-start.50
  246.5 10.1 %collective-permute-done.50.refs_3_ = bf16[1,96,768]{2,1,0:T(8,128)(2,1)S(1)} collective-permute-done((bf16[1,96,768]{2,1,0:T(8,128)(2,1)S(1)}, bf16[1,96,768]{2,1,0:T(8,128)(2,1)S(1)}, u32[]{:S(2)}, u32[]{:S(2)}) %collective-permute-start.50) | collective-permute-done | bytes 147488 | tf_op jit(solution)/shard_map/ppermute | solution.py:985
  258.6 0.9 add_add_fusion
  260.7 2.2 shard_map.272
  262.9 3.0 %shard_map.273 = (f32[768,768]{1,0:T(8,128)}, f32[768,768]{1,0:T(8,128)}) custom-call(s32[3]{0:T(128)S(1)} %pad_add_fusion.place, bf16[2,96,768]{2,1,0:T(8,128)(2,1)S(1)} %get-tuple-element.301.refs_0_, bf16[2,96,768]{2,1,0:T(8,128)(2,1)S(1)} %collective-permute-done.55.refs_1_, bf16[2,96,768]{2,1,0:T(8,128)(2,1)S(1)} %collective-permute-done.56.refs_2_, ...), custom_call_target="tpu_custom_call" | custom-call | bytes 7077888 | tf_op jit(solution)/shard_map/pallas_call | solution.py:934
  (132 shorter events, 20.8 us)
Async XLA Ops:
  6.2 15.2 %collective-permute-start.1 = (bf16[656,768]{1,0:T(8,128)(2,1)S(1)}, bf16[656,768]{1,0:T(8,128)(2,1)S(1)}, u32[]{:S(2)}, u32[]{:S(2)}) collective-permute-start(bf16[656,768]{1,0:T(8,128)(2,1)S(1)} %shard_map.254.normed.counts.rest_4_), channel_id=1, source_target_pairs={{0,4},{4,0},{1,5},{5,1},{2,6},{6,2},{3,7},{7,3},{8,12},{12,8},{9,1... | collective-permute-start | bytes 3022856 | tf_op jit(solution)/shard_map/ppermute | solution.py:1025
  8.4 13.0 %collective-permute-start = (bf16[208,768]{1,0:T(8,128)(2,1)S(1)}, bf16[208,768]{1,0:T(8,128)(2,1)S(1)}, u32[]{:S(2)}, u32[]{:S(2)}) collective-permute-start(bf16[208,768]{1,0:T(8,128)(2,1)S(1)} %get-tuple-element.161), channel_id=1, source_target_pairs={{0,1},{1,2},{2,3},{3,0},{4,6},{5,7},{6,4},{7,5},{8,9},{9,10},{10,1... | collective-permute-start | bytes 958472 | tf_op jit(solution)/shard_map/ppermute | solution.py:1024
  21.4 16.0 %collective-permute-start.2 = (bf16[576,768]{1,0:T(8,128)(2,1)S(1)}, bf16[576,768]{1,0:T(8,128)(2,1)S(1)}, u32[]{:S(2)}, u32[]{:S(2)}) collective-permute-start(bf16[576,768]{1,0:T(8,128)(2,1)S(1)} %bitcast.10), channel_id=1, source_target_pairs={{4,7},{5,4},{6,5},{7,6},{12,15},{13,12},{14,13},{15,14},{20,23},{2... | collective-permute-start | bytes 2654216 | tf_op jit(solution)/shard_map/ppermute | solution.py:1029
  22.2 49.4 %copy-start.15 = (f32[768]{0:T(1024)S(1)}, f32[768]{0:T(1024)}, u32[]{:S(2)}) copy-start(f32[768]{0:T(1024)} %param.23) | copy-start | bytes 9220
  22.2 49.4 %copy-start.17 = (f32[768]{0:T(1024)S(1)}, f32[768]{0:T(1024)}, u32[]{:S(2)}) copy-start(f32[768]{0:T(1024)} %param.24) | copy-start | bytes 9220
  22.2 4.4 %collective-permute-start.3 = (bf16[208,768]{1,0:T(8,128)(2,1)S(1)}, bf16[208,768]{1,0:T(8,128)(2,1)S(1)}, u32[]{:S(2)}, u32[]{:S(2)}) collective-permute-start(bf16[208,768]{1,0:T(8,128)(2,1)S(1)} %get-tuple-element.164.tail.rest_2_.rest_1_), channel_id=1, source_target_pairs={{4,7},{5,4},{6,5},{7,6},{12,15},{13,12},{14,13},{15,14},{20,23},{2... | collective-permute-start | bytes 958472 | tf_op jit(solution)/shard_map/ppermute | solution.py:1030
  23.0 7.1 %collective-permute-start.4 = (bf16[208,768]{1,0:T(8,128)(2,1)S(1)}, bf16[208,768]{1,0:T(8,128)(2,1)S(1)}, u32[]{:S(2)}, u32[]{:S(2)}) collective-permute-start(bf16[208,768]{1,0:T(8,128)(2,1)S(1)} %collective-permute-done.near0.rest_5_.rest_0_), channel_id=1, source_target_pairs={{0,8},{8,0},{1,9},{9,1},{2,10},{10,2},{3,11},{11,3},{4,12},{12,4},... | collective-permute-start | bytes 958472 | tf_op jit(solution)/shard_map/ppermute | solution.py:983
  24.6 10.7 %collective-permute-start.5 = (bf16[208,768]{1,0:T(8,128)(2,1)S(1)}, bf16[208,768]{1,0:T(8,128)(2,1)S(1)}, u32[]{:S(2)}, u32[]{:S(2)}) collective-permute-start(bf16[208,768]{1,0:T(8,128)(2,1)S(1)} %collective-permute-done.near0.rest_5_.rest_0_), channel_id=1, source_target_pairs={{0,16},{16,0},{1,17},{17,1},{2,18},{18,2},{3,19},{19,3},{4,20},{20... | collective-permute-start | bytes 958472 | tf_op jit(solution)/shard_map/ppermute | solution.py:984
  26.1 9.2 %collective-permute-start.6 = (bf16[208,768]{1,0:T(8,128)(2,1)S(1)}, bf16[208,768]{1,0:T(8,128)(2,1)S(1)}, u32[]{:S(2)}, u32[]{:S(2)}) collective-permute-start(bf16[208,768]{1,0:T(8,128)(2,1)S(1)} %collective-permute-done.near0.rest_5_.rest_0_), channel_id=1, source_target_pairs={{0,24},{8,16},{16,8},{24,0},{1,25},{9,17},{17,9},{25,1},{2,26},{10... | collective-permute-start | bytes 958472 | tf_op jit(solution)/shard_map/ppermute | solution.py:985
  35.3 14.5 %collective-permute-start.7 = (bf16[384,768]{1,0:T(8,128)(2,1)S(1)}, bf16[384,768]{1,0:T(8,128)(2,1)S(1)}, u32[]{:S(2)}, u32[]{:S(2)}) collective-permute-start(bf16[384,768]{1,0:T(8,128)(2,1)S(1)} %shard_map.256), channel_id=1, source_target_pairs={{0,1},{1,2},{2,3},{3,0},{4,6},{5,7},{6,4},{7,5},{8,9},{9,10},{10,1... | collective-permute-start | bytes 1769480 | tf_op jit(solution)/shard_map/ppermute | solution.py:1031
  49.8 35.4 %collective-permute-start.11 = (bf16[768,768]{1,0:T(8,128)(2,1)S(1)}, bf16[768,768]{1,0:T(8,128)(2,1)S(1)}, u32[]{:S(2)}, u32[]{:S(2)}) collective-permute-start(bf16[768,768]{1,0:T(8,128)(2,1)S(1)} %copy-done.3), channel_id=1, source_target_pairs={{4,7},{5,4},{6,5},{7,6},{12,15},{13,12},{14,13},{15,14},{20,23},{2... | collective-permute-start | bytes 3538952 | tf_op jit(solution)/shard_map/ppermute | solution.py:1041
  50.6 34.7 %collective-permute-start.12 = (bf16[640,768]{1,0:T(8,128)(2,1)S(1)}, bf16[640,768]{1,0:T(8,128)(2,1)S(1)}, u32[]{:S(2)}, u32[]{:S(2)}) collective-permute-start(bf16[640,768]{1,0:T(8,128)(2,1)S(1)} %copy-done.5), channel_id=1, source_target_pairs={{0,4},{4,0},{1,5},{5,1},{2,6},{6,2},{3,7},{7,3},{8,12},{12,8},{9,1... | collective-permute-start | bytes 2949128 | tf_op jit(solution)/shard_map/ppermute | solution.py:1037
  68.5 16.7 %collective-permute-start.8 = (bf16[640,768]{1,0:T(8,128)(2,1)S(1)}, bf16[640,768]{1,0:T(8,128)(2,1)S(1)}, u32[]{:S(2)}, u32[]{:S(2)}) collective-permute-start(bf16[640,768]{1,0:T(8,128)(2,1)S(1)} %get-tuple-element.174), channel_id=1, source_target_pairs={{0,4},{4,0},{1,5},{5,1},{2,6},{6,2},{3,7},{7,3},{8,12},{12,8},{9,1... | collective-permute-start | bytes 2949128 | tf_op jit(solution)/shard_map/ppermute | solution.py:1038
  68.6 15.7 %collective-permute-start.10 = (bf16[384,768]{1,0:T(8,128)(2,1)S(1)}, bf16[384,768]{1,0:T(8,128)(2,1)S(1)}, u32[]{:S(2)}, u32[]{:S(2)}) collective-permute-start(bf16[384,768]{1,0:T(8,128)(2,1)S(1)} %collective-permute-done.7.rest_0_), channel_id=1, source_target_pairs={{0,16},{16,0},{1,17},{17,1},{2,18},{18,2},{3,19},{19,3},{4,20},{20... | collective-permute-start | bytes 1769480 | tf_op jit(solution)/shard_map/ppermute | solution.py:1040
  69.4 15.8 %collective-permute-start.9 = (bf16[384,768]{1,0:T(8,128)(2,1)S(1)}, bf16[384,768]{1,0:T(8,128)(2,1)S(1)}, u32[]{:S(2)}, u32[]{:S(2)}) collective-permute-start(bf16[384,768]{1,0:T(8,128)(2,1)S(1)} %collective-permute-done.7.rest_0_), channel_id=1, source_target_pairs={{0,8},{8,0},{1,9},{9,1},{2,10},{10,2},{3,11},{11,3},{4,12},{12,4},... | collective-permute-start | bytes 1769480 | tf_op jit(solution)/shard_map/ppermute | solution.py:1039
  89.1 12.4 %collective-permute-start.15 = (bf16[640,768]{1,0:T(8,128)(2,1)S(1)}, bf16[640,768]{1,0:T(8,128)(2,1)S(1)}, u32[]{:S(2)}, u32[]{:S(2)}) collective-permute-start(bf16[640,768]{1,0:T(8,128)(2,1)S(1)} %get-tuple-element.183.rest_6_), channel_id=1, source_target_pairs={{0,4},{4,0},{1,5},{5,1},{2,6},{6,2},{3,7},{7,3},{8,12},{12,8},{9,1... | collective-permute-start | bytes 2949128 | tf_op jit(solution)/shard_map/ppermute | solution.py:1060
  89.1 29.0 %collective-permute-start.16 = (bf16[768,768]{1,0:T(8,128)(2,1)S(1)}, bf16[768,768]{1,0:T(8,128)(2,1)S(1)}, u32[]{:S(2)}, u32[]{:S(2)}) collective-permute-start(bf16[768,768]{1,0:T(8,128)(2,1)S(1)} %copy-done.4), channel_id=1, source_target_pairs={{4,7},{5,4},{6,5},{7,6},{12,15},{13,12},{14,13},{15,14},{20,23},{2... | collective-permute-start | bytes 3538952 | tf_op jit(solution)/shard_map/ppermute | solution.py:1059
  90.0 9.3 %collective-permute-start.13 = (bf16[192,768]{1,0:T(8,128)(2,1)S(1)}, bf16[192,768]{1,0:T(8,128)(2,1)S(1)}, u32[]{:S(2)}, u32[]{:S(2)}) collective-permute-start(bf16[192,768]{1,0:T(8,128)(2,1)S(1)} %slice.27), channel_id=1, source_target_pairs={{0,8},{8,0},{1,9},{9,1},{2,10},{10,2},{3,11},{11,3},{4,12},{12,4},... | collective-permute-start | bytes 884744 | tf_op jit(solution)/shard_map/ppermute | solution.py:1049
  91.8 9.6 %collective-permute-start.14 = (bf16[192,768]{1,0:T(8,128)(2,1)S(1)}, bf16[192,768]{1,0:T(8,128)(2,1)S(1)}, u32[]{:S(2)}, u32[]{:S(2)}) collective-permute-start(bf16[192,768]{1,0:T(8,128)(2,1)S(1)} %slice.28), channel_id=1, source_target_pairs={{0,16},{16,0},{1,17},{17,1},{2,18},{18,2},{3,19},{19,3},{4,20},{20... | collective-permute-start | bytes 884744 | tf_op jit(solution)/shard_map/ppermute | solution.py:1050
  119.1 22.2 %collective-permute-start.17 = (bf16[2,2,96,768]{3,2,1,0:T(8,128)(2,1)S(1)}, bf16[2,2,96,768]{3,2,1,0:T(8,128)(2,1)S(1)}, u32[]{:S(2)}, u32[]{:S(2)}) collective-permute-start(bf16[2,2,96,768]{3,2,1,0:T(8,128)(2,1)S(1)} %get-tuple-element.204), channel_id=1, source_target_pairs={{0,8},{8,0},{1,9},{9,1},{2,10},{10,2},{3,11},{11,3},{4,12},{12,4},... | collective-permute-start | bytes 1769480 | tf_op jit(solution)/shard_map/ppermute | solution.py:995
  119.4 21.9 %collective-permute-start.18 = (bf16[2,2,96,768]{3,2,1,0:T(8,128)(2,1)S(1)}, bf16[2,2,96,768]{3,2,1,0:T(8,128)(2,1)S(1)}, u32[]{:S(2)}, u32[]{:S(2)}) collective-permute-start(bf16[2,2,96,768]{3,2,1,0:T(8,128)(2,1)S(1)} %get-tuple-element.205), channel_id=1, source_target_pairs={{0,16},{16,0},{1,17},{17,1},{2,18},{18,2},{3,19},{19,3},{4,20},{20... | collective-permute-start | bytes 1769480 | tf_op jit(solution)/shard_map/ppermute | solution.py:996
  141.3 2.6 collective-permute-start.19
  141.4 26.9 %collective-permute-start.23 = (bf16[2,4,2,96,768]{4,3,2,1,0:T(8,128)(2,1)}, bf16[2,4,2,96,768]{4,3,2,1,0:T(8,128)(2,1)S(1)}, u32[]{:S(2)}, u32[]{:S(2)}) collective-permute-start(bf16[2,4,2,96,768]{4,3,2,1,0:T(8,128)(2,1)} %get-tuple-element.225.refs_3_.refs_4_), channel_id=1, source_target_pairs={{7,4},{4,5},{5,6},{6,7},{15,12},{12,13},{13,14},{14,15},{23,20},{2... | collective-permute-start | bytes 7077896 | tf_op jit(solution)/shard_map/ppermute | solution.py:1075
  148.7 3.1 %collective-permute-start.20 = (bf16[640,768]{1,0:T(8,128)(2,1)S(1)}, bf16[640,768]{1,0:T(8,128)(2,1)S(1)}, u32[]{:S(2)}, u32[]{:S(2)}) collective-permute-start(bf16[640,768]{1,0:T(8,128)(2,1)S(1)} %get-tuple-element.217.rest_6_), channel_id=1, source_target_pairs={{0,4},{4,0},{1,5},{5,1},{2,6},{6,2},{3,7},{7,3},{8,12},{12,8},{9,1... | collective-permute-start | bytes 2949128 | tf_op jit(solution)/shard_map/ppermute | solution.py:1083
  151.8 16.5 %collective-permute-start.24 = (bf16[640,768]{1,0:T(8,128)(2,1)S(1)}, bf16[640,768]{1,0:T(8,128)(2,1)S(1)}, u32[]{:S(2)}, u32[]{:S(2)}) collective-permute-start(bf16[640,768]{1,0:T(8,128)(2,1)S(1)} %get-tuple-element.227), channel_id=1, source_target_pairs={{0,4},{4,0},{1,5},{5,1},{2,6},{6,2},{3,7},{7,3},{8,12},{12,8},{9,1... | collective-permute-start | bytes 2949128 | tf_op jit(solution)/shard_map/ppermute | solution.py:1084
  152.2 16.1 %collective-permute-start.21 = (bf16[2,96,768]{2,1,0:T(8,128)(2,1)S(1)}, bf16[2,96,768]{2,1,0:T(8,128)(2,1)S(1)}, u32[]{:S(2)}, u32[]{:S(2)}) collective-permute-start(bf16[2,96,768]{2,1,0:T(8,128)(2,1)S(1)} %get-tuple-element.212), channel_id=1, source_target_pairs={{0,16},{16,0},{1,17},{17,1},{2,18},{18,2},{3,19},{19,3},{4,20},{20... | collective-permute-start | bytes 884744 | tf_op jit(solution)/shard_map/ppermute | solution.py:1000
  153.4 14.9 %collective-permute-start.22 = (bf16[2,96,768]{2,1,0:T(8,128)(2,1)S(1)}, bf16[2,96,768]{2,1,0:T(8,128)(2,1)S(1)}, u32[]{:S(2)}, u32[]{:S(2)}) collective-permute-start(bf16[2,96,768]{2,1,0:T(8,128)(2,1)S(1)} %get-tuple-element.213), channel_id=1, source_target_pairs={{0,8},{8,0},{1,9},{9,1},{2,10},{10,2},{3,11},{11,3},{4,12},{12,4},... | collective-permute-start | bytes 884744 | tf_op jit(solution)/shard_map/ppermute | solution.py:1000
  169.1 21.6 %collective-permute-start.28 = (bf16[4,2,96,768]{3,2,1,0:T(8,128)(2,1)S(1)}, bf16[4,2,96,768]{3,2,1,0:T(8,128)(2,1)S(1)}, u32[]{:S(2)}, u32[]{:S(2)}) collective-permute-start(bf16[4,2,96,768]{3,2,1,0:T(8,128)(2,1)S(1)} %get-tuple-element.245), channel_id=1, source_target_pairs={{0,4},{4,0},{1,5},{5,1},{2,6},{6,2},{3,7},{7,3},{8,12},{12,8},{9,1... | collective-permute-start | bytes 3538952 | tf_op jit(solution)/shard_map/ppermute | solution.py:1099
  174.4 16.4 %collective-permute-start.29 = (bf16[2,2,96,768]{3,2,1,0:T(8,128)(2,1)S(1)}, bf16[2,2,96,768]{3,2,1,0:T(8,128)(2,1)S(1)}, u32[]{:S(2)}, u32[]{:S(2)}) collective-permute-start(bf16[2,2,96,768]{3,2,1,0:T(8,128)(2,1)S(1)} %get-tuple-element.233), channel_id=1, source_target_pairs={{1,0},{2,1},{3,2},{0,3},{6,4},{7,5},{4,6},{5,7},{9,8},{10,9},{11,1... | collective-permute-start | bytes 1769480 | tf_op jit(solution)/shard_map/ppermute | solution.py:1098
  174.4 15.7 %collective-permute-start.25 = (bf16[2,1,96,768]{3,2,1,0:T(8,128)(2,1)S(1)}, bf16[2,1,96,768]{3,2,1,0:T(8,128)(2,1)S(1)}, u32[]{:S(2)}, u32[]{:S(2)}) collective-permute-start(bf16[2,1,96,768]{3,2,1,0:T(8,128)(2,1)S(1)} %get-tuple-element.242), channel_id=1, source_target_pairs={{0,8},{8,0},{1,9},{9,1},{2,10},{10,2},{3,11},{11,3},{4,12},{12,4},... | collective-permute-start | bytes 884744 | tf_op jit(solution)/shard_map/ppermute | solution.py:1005
  175.6 15.1 %collective-permute-start.26 = (bf16[2,1,96,768]{3,2,1,0:T(8,128)(2,1)S(1)}, bf16[2,1,96,768]{3,2,1,0:T(8,128)(2,1)S(1)}, u32[]{:S(2)}, u32[]{:S(2)}) collective-permute-start(bf16[2,1,96,768]{3,2,1,0:T(8,128)(2,1)S(1)} %get-tuple-element.243), channel_id=1, source_target_pairs={{0,16},{16,0},{1,17},{17,1},{2,18},{18,2},{3,19},{19,3},{4,20},{20... | collective-permute-start | bytes 884744 | tf_op jit(solution)/shard_map/ppermute | solution.py:1006
  177.3 13.4 %collective-permute-start.27 = (bf16[2,1,96,768]{3,2,1,0:T(8,128)(2,1)S(1)}, bf16[2,1,96,768]{3,2,1,0:T(8,128)(2,1)S(1)}, u32[]{:S(2)}, u32[]{:S(2)}) collective-permute-start(bf16[2,1,96,768]{3,2,1,0:T(8,128)(2,1)S(1)} %get-tuple-element.244), channel_id=1, source_target_pairs={{0,24},{8,16},{16,8},{24,0},{1,25},{9,17},{17,9},{25,1},{2,26},{10... | collective-permute-start | bytes 884744 | tf_op jit(solution)/shard_map/ppermute | solution.py:1007
  190.7 8.6 %collective-permute-start.30 = (bf16[640,768]{1,0:T(8,128)(2,1)S(1)}, bf16[640,768]{1,0:T(8,128)(2,1)S(1)}, u32[]{:S(2)}, u32[]{:S(2)}) collective-permute-start(bf16[640,768]{1,0:T(8,128)(2,1)S(1)} %get-tuple-element.247), channel_id=1, source_target_pairs={{0,4},{4,0},{1,5},{5,1},{2,6},{6,2},{3,7},{7,3},{8,12},{12,8},{9,1... | collective-permute-start | bytes 2949128 | tf_op jit(solution)/shard_map/ppermute | solution.py:1109
  195.7 8.6 %collective-permute-start.35 = (bf16[2,96,768]{2,1,0:T(8,128)(2,1)S(1)}, bf16[2,96,768]{2,1,0:T(8,128)(2,1)S(1)}, u32[]{:S(2)}, u32[]{:S(2)}) collective-permute-start(bf16[2,96,768]{2,1,0:T(8,128)(2,1)S(1)} %get-tuple-element.265), channel_id=1, source_target_pairs={{0,4},{4,0},{1,5},{5,1},{2,6},{6,2},{3,7},{7,3},{8,12},{12,8},{9,1... | collective-permute-start | bytes 884744 | tf_op jit(solution)/shard_map/ppermute | solution.py:1117
  195.8 10.6 %collective-permute-start.32 = (bf16[2,1,96,768]{3,2,1,0:T(8,128)(2,1)S(1)}, bf16[2,1,96,768]{3,2,1,0:T(8,128)(2,1)S(1)}, u32[]{:S(2)}, u32[]{:S(2)}) collective-permute-start(bf16[2,1,96,768]{3,2,1,0:T(8,128)(2,1)S(1)} %get-tuple-element.256), channel_id=1, source_target_pairs={{0,8},{8,0},{1,9},{9,1},{2,10},{10,2},{3,11},{11,3},{4,12},{12,4},... | collective-permute-start | bytes 884744 | tf_op jit(solution)/shard_map/ppermute | solution.py:1005
  197.1 15.2 %collective-permute-start.33 = (bf16[2,1,96,768]{3,2,1,0:T(8,128)(2,1)S(1)}, bf16[2,1,96,768]{3,2,1,0:T(8,128)(2,1)S(1)}, u32[]{:S(2)}, u32[]{:S(2)}) collective-permute-start(bf16[2,1,96,768]{3,2,1,0:T(8,128)(2,1)S(1)} %get-tuple-element.257), channel_id=1, source_target_pairs={{0,16},{16,0},{1,17},{17,1},{2,18},{18,2},{3,19},{19,3},{4,20},{20... | collective-permute-start | bytes 884744 | tf_op jit(solution)/shard_map/ppermute | solution.py:1006
  198.8 15.4 %collective-permute-start.34 = (bf16[2,1,96,768]{3,2,1,0:T(8,128)(2,1)S(1)}, bf16[2,1,96,768]{3,2,1,0:T(8,128)(2,1)S(1)}, u32[]{:S(2)}, u32[]{:S(2)}) collective-permute-start(bf16[2,1,96,768]{3,2,1,0:T(8,128)(2,1)S(1)} %get-tuple-element.258), channel_id=1, source_target_pairs={{0,24},{8,16},{16,8},{24,0},{1,25},{9,17},{17,9},{25,1},{2,26},{10... | collective-permute-start | bytes 884744 | tf_op jit(solution)/shard_map/ppermute | solution.py:1007
  204.3 10.0 %collective-permute-start.31 = (f32[16,768]{1,0:T(8,128)S(1)}, f32[16,768]{1,0:T(8,128)S(1)}, u32[]{:S(2)}, u32[]{:S(2)}) collective-permute-start(f32[16,768]{1,0:T(8,128)S(1)} %get-tuple-element.254.refs_4_), channel_id=1, source_target_pairs={{0,4},{4,0},{1,5},{5,1},{2,6},{6,2},{3,7},{7,3},{8,12},{12,8},{9,1... | collective-permute-start | bytes 147464 | tf_op jit(solution)/shard_map/ppermute | solution.py:1132
  204.3 12.8 %collective-permute-start.37 = (bf16[2,1,96,768]{3,2,1,0:T(8,128)(2,1)S(1)}, bf16[2,1,96,768]{3,2,1,0:T(8,128)(2,1)S(1)}, u32[]{:S(2)}, u32[]{:S(2)}) collective-permute-start(bf16[2,1,96,768]{3,2,1,0:T(8,128)(2,1)S(1)} %get-tuple-element.272), channel_id=1, source_target_pairs={{1,0},{2,1},{3,2},{0,3},{6,4},{7,5},{4,6},{5,7},{9,8},{10,9},{11,1... | collective-permute-start | bytes 884744 | tf_op jit(solution)/shard_map/ppermute | solution.py:1116
  206.4 19.0 %collective-permute-start.42 = (bf16[2,96,768]{2,1,0:T(8,128)(2,1)S(1)}, bf16[2,96,768]{2,1,0:T(8,128)(2,1)S(1)}, u32[]{:S(2)}, u32[]{:S(2)}) collective-permute-start(bf16[2,96,768]{2,1,0:T(8,128)(2,1)S(1)} %get-tuple-element.283), channel_id=1, source_target_pairs={{0,8},{8,0},{1,9},{9,1},{2,10},{10,2},{3,11},{11,3},{4,12},{12,4},... | collective-permute-start | bytes 884744 | tf_op jit(solution)/shard_map/ppermute | solution.py:1005
  212.3 14.8 %collective-permute-start.43 = (bf16[2,96,768]{2,1,0:T(8,128)(2,1)S(1)}, bf16[2,96,768]{2,1,0:T(8,128)(2,1)S(1)}, u32[]{:S(2)}, u32[]{:S(2)}) collective-permute-start(bf16[2,96,768]{2,1,0:T(8,128)(2,1)S(1)} %get-tuple-element.284), channel_id=1, source_target_pairs={{0,16},{16,0},{1,17},{17,1},{2,18},{18,2},{3,19},{19,3},{4,20},{20... | collective-permute-start | bytes 884744 | tf_op jit(solution)/shard_map/ppermute | solution.py:1006
  214.2 13.2 %collective-permute-start.44 = (bf16[2,96,768]{2,1,0:T(8,128)(2,1)S(1)}, bf16[2,96,768]{2,1,0:T(8,128)(2,1)S(1)}, u32[]{:S(2)}, u32[]{:S(2)}) collective-permute-start(bf16[2,96,768]{2,1,0:T(8,128)(2,1)S(1)} %get-tuple-element.285), channel_id=1, source_target_pairs={{0,24},{8,16},{16,8},{24,0},{1,25},{9,17},{17,9},{25,1},{2,26},{10... | collective-permute-start | bytes 884744 | tf_op jit(solution)/shard_map/ppermute | solution.py:1007
  214.9 2.1 collective-permute-start.36
  217.7 14.4 %collective-permute-start.38 = (bf16[1,96,768]{2,1,0:T(8,128)(2,1)S(1)}, bf16[1,96,768]{2,1,0:T(8,128)(2,1)S(1)}, u32[]{:S(2)}, u32[]{:S(2)}) collective-permute-start(bf16[1,96,768]{2,1,0:T(8,128)(2,1)S(1)} %get-tuple-element.280), channel_id=1, source_target_pairs={{0,4},{4,0},{1,5},{5,1},{2,6},{6,2},{3,7},{7,3},{8,12},{12,8},{9,1... | collective-permute-start | bytes 442376 | tf_op jit(solution)/shard_map/ppermute | solution.py:1144
  223.9 4.1 %collective-permute-start.39 = (f32[16,768]{1,0:T(8,128)S(1)}, f32[16,768]{1,0:T(8,128)S(1)}, u32[]{:S(2)}, u32[]{:S(2)}) collective-permute-start(f32[16,768]{1,0:T(8,128)S(1)} %get-tuple-element.293.refs_8_), channel_id=1, source_target_pairs={{0,8},{8,0},{1,9},{9,1},{2,10},{10,2},{3,11},{11,3},{4,12},{12,4},... | collective-permute-start | bytes 147464 | tf_op jit(solution)/shard_map/ppermute | solution.py:983
  225.4 4.1 %collective-permute-start.40 = (f32[16,768]{1,0:T(8,128)S(1)}, f32[16,768]{1,0:T(8,128)S(1)}, u32[]{:S(2)}, u32[]{:S(2)}) collective-permute-start(f32[16,768]{1,0:T(8,128)S(1)} %get-tuple-element.293.refs_8_), channel_id=1, source_target_pairs={{0,16},{16,0},{1,17},{17,1},{2,18},{18,2},{3,19},{19,3},{4,20},{20... | collective-permute-start | bytes 147464 | tf_op jit(solution)/shard_map/ppermute | solution.py:984
  227.1 5.0 %collective-permute-start.41 = (f32[16,768]{1,0:T(8,128)S(1)}, f32[16,768]{1,0:T(8,128)S(1)}, u32[]{:S(2)}, u32[]{:S(2)}) collective-permute-start(f32[16,768]{1,0:T(8,128)S(1)} %get-tuple-element.293.refs_8_), channel_id=1, source_target_pairs={{0,24},{8,16},{16,8},{24,0},{1,25},{9,17},{17,9},{25,1},{2,26},{10... | collective-permute-start | bytes 147464 | tf_op jit(solution)/shard_map/ppermute | solution.py:985
  233.3 11.3 %collective-permute-start.48 = (bf16[1,96,768]{2,1,0:T(8,128)(2,1)S(1)}, bf16[1,96,768]{2,1,0:T(8,128)(2,1)S(1)}, u32[]{:S(2)}, u32[]{:S(2)}) collective-permute-start(bf16[1,96,768]{2,1,0:T(8,128)(2,1)S(1)} %get-tuple-element.298.refs_0_), channel_id=1, source_target_pairs={{0,8},{8,0},{1,9},{9,1},{2,10},{10,2},{3,11},{11,3},{4,12},{12,4},... | collective-permute-start | bytes 442376 | tf_op jit(solution)/shard_map/ppermute | solution.py:983
  233.7 12.8 %collective-permute-start.49 = (bf16[1,96,768]{2,1,0:T(8,128)(2,1)S(1)}, bf16[1,96,768]{2,1,0:T(8,128)(2,1)S(1)}, u32[]{:S(2)}, u32[]{:S(2)}) collective-permute-start(bf16[1,96,768]{2,1,0:T(8,128)(2,1)S(1)} %get-tuple-element.298.refs_0_), channel_id=1, source_target_pairs={{0,16},{16,0},{1,17},{17,1},{2,18},{18,2},{3,19},{19,3},{4,20},{20... | collective-permute-start | bytes 442376 | tf_op jit(solution)/shard_map/ppermute | solution.py:984
  235.0 6.2 %collective-permute-start.45 = (f32[16,768]{1,0:T(8,128)}, f32[16,768]{1,0:T(8,128)}, u32[]{:S(2)}, u32[]{:S(2)}) collective-permute-start(f32[16,768]{1,0:T(8,128)} %get-tuple-element.297), channel_id=1, source_target_pairs={{0,1},{1,2},{2,3},{3,0},{4,5},{5,6},{6,7},{7,4},{8,9},{9,10},{10,1... | collective-permute-start | bytes 147464 | tf_op jit(solution)/shard_map/ppermute | solution.py:1156
  235.0 8.2 %collective-permute-start.46 = (f32[16,768]{1,0:T(8,128)}, f32[16,768]{1,0:T(8,128)}, u32[]{:S(2)}, u32[]{:S(2)}) collective-permute-start(f32[16,768]{1,0:T(8,128)} %get-tuple-element.297), channel_id=1, source_target_pairs={{0,2},{1,3},{2,0},{3,1},{4,6},{5,7},{6,4},{7,5},{8,10},{9,11},{10,... | collective-permute-start | bytes 147464 | tf_op jit(solution)/shard_map/ppermute | solution.py:1156
  238.1 5.5 %collective-permute-start.47 = (f32[16,768]{1,0:T(8,128)}, f32[16,768]{1,0:T(8,128)}, u32[]{:S(2)}, u32[]{:S(2)}) collective-permute-start(f32[16,768]{1,0:T(8,128)} %get-tuple-element.297), channel_id=1, source_target_pairs={{0,3},{1,0},{2,1},{3,2},{4,7},{5,4},{6,5},{7,6},{8,11},{9,8},{10,9... | collective-permute-start | bytes 147464 | tf_op jit(solution)/shard_map/ppermute | solution.py:1156
  241.2 16.0 %collective-permute-start.55 = (bf16[2,96,768]{2,1,0:T(8,128)(2,1)S(1)}, bf16[2,96,768]{2,1,0:T(8,128)(2,1)S(1)}, u32[]{:S(2)}, u32[]{:S(2)}) collective-permute-start(bf16[2,96,768]{2,1,0:T(8,128)(2,1)S(1)} %get-tuple-element.301.refs_0_), channel_id=1, source_target_pairs={{0,8},{8,0},{1,9},{9,1},{2,10},{10,2},{3,11},{11,3},{4,12},{12,4},... | collective-permute-start | bytes 884744 | tf_op jit(solution)/shard_map/ppermute | solution.py:983
  243.2 14.3 %collective-permute-start.56 = (bf16[2,96,768]{2,1,0:T(8,128)(2,1)S(1)}, bf16[2,96,768]{2,1,0:T(8,128)(2,1)S(1)}, u32[]{:S(2)}, u32[]{:S(2)}) collective-permute-start(bf16[2,96,768]{2,1,0:T(8,128)(2,1)S(1)} %get-tuple-element.301.refs_0_), channel_id=1, source_target_pairs={{0,16},{16,0},{1,17},{17,1},{2,18},{18,2},{3,19},{19,3},{4,20},{20... | collective-permute-start | bytes 884744 | tf_op jit(solution)/shard_map/ppermute | solution.py:984
  243.6 14.1 %collective-permute-start.57 = (bf16[2,96,768]{2,1,0:T(8,128)(2,1)S(1)}, bf16[2,96,768]{2,1,0:T(8,128)(2,1)S(1)}, u32[]{:S(2)}, u32[]{:S(2)}) collective-permute-start(bf16[2,96,768]{2,1,0:T(8,128)(2,1)S(1)} %get-tuple-element.301.refs_0_), channel_id=1, source_target_pairs={{0,24},{8,16},{16,8},{24,0},{1,25},{9,17},{17,9},{25,1},{2,26},{10... | collective-permute-start | bytes 884744 | tf_op jit(solution)/shard_map/ppermute | solution.py:985
  244.7 12.0 %collective-permute-start.50 = (bf16[1,96,768]{2,1,0:T(8,128)(2,1)S(1)}, bf16[1,96,768]{2,1,0:T(8,128)(2,1)S(1)}, u32[]{:S(2)}, u32[]{:S(2)}) collective-permute-start(bf16[1,96,768]{2,1,0:T(8,128)(2,1)S(1)} %get-tuple-element.298.refs_0_), channel_id=1, source_target_pairs={{0,24},{8,16},{16,8},{24,0},{1,25},{9,17},{17,9},{25,1},{2,26},{10... | collective-permute-start | bytes 442376 | tf_op jit(solution)/shard_map/ppermute | solution.py:985
  246.5 10.2 %collective-permute-start.51 = (bf16[1,96,768]{2,1,0:T(8,128)(2,1)S(1)}, bf16[1,96,768]{2,1,0:T(8,128)(2,1)S(1)}, u32[]{:S(2)}, u32[]{:S(2)}) collective-permute-start(bf16[1,96,768]{2,1,0:T(8,128)(2,1)S(1)} %get-tuple-element.298.refs_0_), channel_id=1, source_target_pairs={{0,4},{4,0},{1,5},{5,1},{2,6},{6,2},{3,7},{7,3},{8,12},{12,8},{9,1... | collective-permute-start | bytes 442376 | tf_op jit(solution)/shard_map/ppermute | solution.py:1161
  256.7 1.4 collective-permute-start.52
  256.7 1.6 collective-permute-start.53
  257.2 5.7 %collective-permute-start.58 = (bf16[2,96,768]{2,1,0:T(8,128)(2,1)S(1)}, bf16[2,96,768]{2,1,0:T(8,128)(2,1)S(1)}, u32[]{:S(2)}, u32[]{:S(2)}) collective-permute-start(bf16[2,96,768]{2,1,0:T(8,128)(2,1)S(1)} %get-tuple-element.301.refs_0_), channel_id=1, source_target_pairs={{0,4},{4,0},{1,5},{5,1},{2,6},{6,2},{3,7},{7,3},{8,12},{12,8},{9,1... | collective-permute-start | bytes 884744 | tf_op jit(solution)/shard_map/ppermute | solution.py:1159
  257.5 3.2 %collective-permute-start.54 = (bf16[1,96,768]{2,1,0:T(8,128)(2,1)S(1)}, bf16[1,96,768]{2,1,0:T(8,128)(2,1)S(1)}, u32[]{:S(2)}, u32[]{:S(2)}) collective-permute-start(bf16[1,96,768]{2,1,0:T(8,128)(2,1)S(1)} %collective-permute-done.50.refs_3_), channel_id=1, source_target_pairs={{0,4},{4,0},{1,5},{5,1},{2,6},{6,2},{3,7},{7,3},{8,12},{12,8},{9,1... | collective-permute-start | bytes 442376 | tf_op jit(solution)/shard_map/ppermute | solution.py:1161
  257.7 5.2 %collective-permute-start.59 = (bf16[2,96,768]{2,1,0:T(8,128)(2,1)S(1)}, bf16[2,96,768]{2,1,0:T(8,128)(2,1)S(1)}, u32[]{:S(2)}, u32[]{:S(2)}) collective-permute-start(bf16[2,96,768]{2,1,0:T(8,128)(2,1)S(1)} %collective-permute-done.55.refs_1_), channel_id=1, source_target_pairs={{0,4},{4,0},{1,5},{5,1},{2,6},{6,2},{3,7},{7,3},{8,12},{12,8},{9,1... | collective-permute-start | bytes 884744 | tf_op jit(solution)/shard_map/ppermute | solution.py:1159
  258.1 4.9 %collective-permute-start.60 = (bf16[2,96,768]{2,1,0:T(8,128)(2,1)S(1)}, bf16[2,96,768]{2,1,0:T(8,128)(2,1)S(1)}, u32[]{:S(2)}, u32[]{:S(2)}) collective-permute-start(bf16[2,96,768]{2,1,0:T(8,128)(2,1)S(1)} %collective-permute-done.56.refs_2_), channel_id=1, source_target_pairs={{0,4},{4,0},{1,5},{5,1},{2,6},{6,2},{3,7},{7,3},{8,12},{12,8},{9,1... | collective-permute-start | bytes 884744 | tf_op jit(solution)/shard_map/ppermute | solution.py:1159
  258.3 4.7 %collective-permute-start.61 = (bf16[2,96,768]{2,1,0:T(8,128)(2,1)S(1)}, bf16[2,96,768]{2,1,0:T(8,128)(2,1)S(1)}, u32[]{:S(2)}, u32[]{:S(2)}) collective-permute-start(bf16[2,96,768]{2,1,0:T(8,128)(2,1)S(1)} %collective-permute-done.57.refs_3_), channel_id=1, source_target_pairs={{0,4},{4,0},{1,5},{5,1},{2,6},{6,2},{3,7},{7,3},{8,12},{12,8},{9,1... | collective-permute-start | bytes 884744 | tf_op jit(solution)/shard_map/ppermute | solution.py:1159
  (17 other events, 220.2 us)
